TPU v7x, 32 devices: a whole 2x2x4 slice. The times are simulated.
32 devices in a mesh: mem: 8 (over z, y), band: 4 (over x, core).
Axes of the slice: x: 2, y: 2, z: 4, core: 2. Of those that a mesh axis runs over, the one named last changes fastest.
Arguments:
- alpha: bfloat16 [16, 4, 320, 720], P('mem', None, 'band'), may hold values from -6 to 6
- static_ctl: bfloat16 [4, 320, 720], P(None, 'band'), may hold values from -6 to 6
- perturbations: bfloat16 [16, 4, 320, 720], P('mem', None, None, 'band'), may hold values from -6 to 6
- static_std: float32 [4, 320, 720], P(None, None, 'band'), may hold values from 0.5 to 2
- lon_root: bfloat16 [720, 720], replicated, may hold values from -0.11 to 1.11
- lat_root: bfloat16 [320, 320], replicated, may hold values from -0.11 to 1.11
- jacobian: bfloat16 [32, 4, 320, 720], P(None, None, 'mem', 'band'), may hold values from -3 to 3
- obs_count: int32 [320, 720], P('mem', 'band'), may hold values from 1 to 6
- channel_mask: int32 [32, 320, 720], P(None, 'mem', 'band'), may hold values 0 or 1
- channel_error: float32 [32], replicated, may hold values from 1 to 2
- member_weight: int32 [16], replicated, may hold values from 1 to 4
Outputs:
- grad_alpha: float32 [16, 4, 320, 720], P('mem', None, 'band')
- grad_static: float32 [4, 320, 720], P(None, 'band')
All inputs are finite; a program needn't handle non-finite values. No bound on the sum of `channel_mask` on one device may be relied on, other than what follows from the above.
Results may differ from a plain program's by a relative error of at most 0.0055.
Values may be sent and summed in bfloat16 or wider, within the bound.
No kernel may reach another device: no remote copies, remote signals or barrier semaphores. Data moves between devices by JAX's collectives and lax.ppermute only.
A program may use at most 64 MiB of HBM per device.

v0:
```python
import jax
import jax.numpy as jnp
from jax import lax
from jax.sharding import PartitionSpec as P


def shards(
    alpha,
    static_ctl,
    perturbations,
    static_std,
    lon_root,
    lat_root,
    jacobian,
    obs_count,
    channel_mask,
    channel_error,
    member_weight,
):
    members = alpha.shape[0]
    rows = jacobian.shape[2]
    rank = lax.axis_index("mem")
    weights = member_weight.astype(jnp.float32)
    coef = weights / jnp.sqrt(jnp.sum(weights * weights))
    own_coef = lax.dynamic_slice_in_dim(coef, rank * members, members, 0)
    fields = jnp.concatenate([alpha, static_ctl[None]], axis=0)
    along_lon = jnp.dot(fields, lon_root, preferred_element_type=jnp.float32).astype(jnp.bfloat16)
    regrouped = lax.all_to_all(along_lon, "band", split_axis=3, concat_axis=2, tiled=True)
    member_lat = jnp.einsum(
        "ij,msjk->msik", lat_root, regrouped[:members], preferred_element_type=jnp.float32
    )
    own_root = lax.dynamic_slice_in_dim(lat_root, rank * rows, rows, 0)
    own_static = jnp.einsum(
        "ij,sjk->sik", own_root, regrouped[members], preferred_element_type=jnp.float32
    )
    scaled = 0.8 * own_coef
    ensemble_term = jnp.sum(
        scaled[:, None, None, None] * perturbations.astype(jnp.float32) * member_lat, axis=0
    )
    summed = lax.psum(ensemble_term, "mem")
    own_sum = lax.dynamic_slice_in_dim(summed, rank * rows, rows, 1)
    own_std = lax.dynamic_slice_in_dim(static_std, rank * rows, rows, 1)
    increment = own_sum + 0.6 * own_std * own_static
    obs_weight = (
        channel_mask.astype(jnp.float32)
        * obs_count.astype(jnp.float32)[None]
        / (channel_error * channel_error)[:, None, None]
    )
    jac_full = jacobian.astype(jnp.float32)
    radiance = jnp.sum(jac_full * increment[None], axis=1)
    obs_gradient = jnp.sum(jac_full * (obs_weight * radiance)[:, None], axis=0).astype(jnp.bfloat16)
    band_gradient = lax.all_gather(obs_gradient, "mem", axis=1, tiled=True).astype(jnp.float32)
    member_adjoint = (
        scaled[:, None, None, None] * perturbations.astype(jnp.float32) * band_gradient[None]
    ).astype(jnp.bfloat16)
    static_adjoint = (0.6 * static_std * band_gradient).astype(jnp.bfloat16)
    adjoints = jnp.concatenate([member_adjoint, static_adjoint[None]], axis=0)
    back_lat = jnp.einsum(
        "ji,msjk->msik", lat_root, adjoints, preferred_element_type=jnp.float32
    ).astype(jnp.bfloat16)
    returned = lax.all_to_all(back_lat, "band", split_axis=2, concat_axis=3, tiled=True)
    back_lon = jnp.einsum("msil,jl->msij", returned, lon_root, preferred_element_type=jnp.float32)
    grad_alpha = alpha.astype(jnp.float32) + back_lon[:members]
    grad_static = static_ctl.astype(jnp.float32) + back_lon[members]
    return (grad_alpha, grad_static)


def solution(mesh):
    in_specs = (
        P("mem", None, "band", None),
        P(None, "band", None),
        P("mem", None, None, "band"),
        P(None, None, "band"),
        P(),
        P(),
        P(None, None, "mem", "band"),
        P("mem", "band"),
        P(None, "mem", "band"),
        P(),
        P(),
    )
    out_specs = (P("mem", None, "band", None), P(None, "band", None))
    return jax.shard_map(shards, mesh=mesh, in_specs=in_specs, out_specs=out_specs, check_vma=False)
```

profile of v0, /device:TPU:0, one launch (start us, length us, event | category | flops | bytes accessed | tf_op | source)
XLA Modules:
  0.0 232.6 jit_solution(4130602733582369304)
XLA Ops:
  7.2 1.2 copy-done
  8.4 2.7 %convolution_convert_fusion.1 = bf16[3,4,80,720]{3,2,1,0:T(8,128)(2,1)S(1)} fusion(bf16[1,4,80,720]{3,2,1,0:T(8,128)(2,1)} %bitcast.52, bf16[2,4,80,720]{3,2,1,0:T(8,128)(2,1)} %param.11, bf16[720,720]{1,0:T(8,128)(2,1)S(1)} %copy-done), kind=kOutput, calls=%fused_computation.13 | convolution fusion | flops 996710400 | bytes 3801600 | tf_op jit(solution)/shard_map/dot_general | solution.py:27
  11.1 3.3 %copy.28 = bf16[3,4,80,720]{2,1,0,3:T(4,128)(2,1)} copy(bf16[3,4,80,720]{3,2,1,0:T(8,128)(2,1)S(1)} %convolution_convert_fusion.1) | data formatting | bytes 2764800 | tf_op jit(solution)/shard_map/convert_element_type | solution.py:27
  14.4 4.4 %all-to-all-start = ((bf16[3,4,80,720]{2,1,0,3:T(4,128)(2,1)}), bf16[3,4,80,720]{2,1,0,3:T(4,128)(2,1)S(1)}, u32[]{:S(2)}, u32[]{:S(2)}) async-start(bf16[3,4,80,720]{2,1,0,3:T(4,128)(2,1)} %copy.28), calls=%async_computation | async-start | bytes 4423680 | tf_op jit(solution)/shard_map/all_to_all | solution.py:28
  18.7 0.6 multiply_reduce_fusion
  20.1 25.5 %all-to-all-done = bf16[3,4,80,720]{2,1,0,3:T(4,128)(2,1)S(1)} async-done(((bf16[3,4,80,720]{2,1,0,3:T(4,128)(2,1)}), bf16[3,4,80,720]{2,1,0,3:T(4,128)(2,1)S(1)}, u32[]{:S(2)}, u32[]{:S(2)}) %all-to-all-start) | async-done | bytes 1382432 | tf_op jit(solution)/shard_map/all_to_all | solution.py:28
  45.6 3.8 %copy.29 = bf16[3,4,80,4,180]{4,2,3,1,0:T(8,128)(2,1)} copy(bf16[3,4,80,4,180]{2,1,0,4,3:T(4,128)(2,1)S(1)} %bitcast.46) | data formatting | bytes 2764800 | tf_op jit(solution)/shard_map/all_to_all | solution.py:28
  49.4 1.5 slice.21
  51.1 1.4 fusion.2
  52.5 1.5 copy.31
  54.1 0.3 constant_dynamic-slice_fusion
  54.6 1.1 slice.22
  55.7 83.2 %all-reduce.2.cloned.1.call-done = f32[4,320,180]{2,1,0:T(8,128)} async-done(((f32[4,320,180]{2,1,0:T(8,128)}), f32[4,320,180]{2,1,0:T(8,128)}) %all-reduce.2.cloned.1.call-update) | async-done | bytes 921616 | tf_op jit(solution)/shard_map/psum | solution.py:40
  138.9 1.2 fusion.13
  140.1 2.6 %fusion = f32[32,40,180]{2,1,0:T(8,128)S(1)} fusion(bf16[32,4,40,180]{3,2,1,0:T(8,128)(2,1)} %param.17, f32[4,40,180]{2,1,0:T(8,128)S(1)} %fusion.13), kind=kLoop, calls=%fused_computation.2 | loop fusion | flops 2534400 | bytes 2880000 | tf_op jit(solution)/shard_map/reduce_sum | solution.py:50
  143.0 1.5 copy-done.1
  144.5 0.7 fusion.1
  145.2 31.8 %all_gather.3 = bf16[4,320,180]{2,0,1:T(4,128)(2,1)S(1)} all-gather(bf16[4,40,180]{2,0,1:T(4,128)(2,1)S(1)} %copy.34), channel_id=1, replica_groups=mesh['mem'=8,'band'=4] {'mem'}, dimensions={1}, use_global_device_ids=true | all-gather | bytes 518400 | tf_op jit(solution)/shard_map/all_gather | solution.py:52
  177.0 0.9 copy.35
  178.1 1.0 copy-done.5
  179.1 0.4 multiply_convert_fusion
  179.5 0.6 copy-done.10
  180.0 2.5 %fusion.6 = bf16[3,4,320,180]{2,3,1,0:T(8,128)(2,1)} fusion(bf16[1,4,320,180]{2,3,1,0:T(8,128)(2,1)S(1)} %fusion.20, bf16[2,4,320,180]{2,3,1,0:T(8,128)(2,1)S(1)} %multiply_convert_fusion, bf16[320,320]{1,0:T(8,128)(2,1)S(1)} %copy-done.10), kind=kOutput, calls=%fused_computation.14 | convolution fusion | flops 443750400 | bytes 2969600 | tf_op jit(solution)/shard_map/ji,msjk->msik/dot_general | solution.py:58
  182.6 6.7 %copy.37 = bf16[3,4,320,180]{3,1,0,2:T(4,128)(2,1)S(1)} copy(bf16[3,4,320,180]{2,3,1,0:T(8,128)(2,1)} %fusion.6) | data formatting | bytes 2764800 | tf_op jit(solution)/shard_map/convert_element_type | solution.py:60
  189.2 26.8 %all_to_all.33 = bf16[3,4,320,180]{3,1,0,2:T(4,128)(2,1)S(1)} all-to-all(bf16[3,4,320,180]{3,1,0,2:T(4,128)(2,1)S(1)} %copy.37), channel_id=1, replica_groups=mesh['mem'=8,'band'=4] {'band'}, dimensions={2} | all-to-all | bytes 2764800 | tf_op jit(solution)/shard_map/all_to_all | solution.py:61
  216.0 0.3 copy.38
  216.3 1.0 copy.39
  217.4 2.5 %all_to_all.30 = bf16[3,4,80,720]{3,2,1,0:T(8,128)(2,1)} reshape(bf16[3,4,80,4,180]{4,3,2,1,0:T(4,128)(2,1)S(1)} %copy.39) | data formatting | bytes 2764800 | tf_op jit(solution)/shard_map/all_to_all | solution.py:61
  219.9 2.8 %fusion.16 = f32[3,4,80,720]{3,2,1,0:T(8,128)S(1)} fusion(bf16[3,4,80,720]{3,2,1,0:T(8,128)(2,1)} %all_to_all.30, bf16[720,720]{1,0:T(8,128)(2,1)S(1)} %copy-done), kind=kOutput, calls=%fused_computation.25 | convolution fusion | flops 995328000 | bytes 5184000 | tf_op jit(solution)/shard_map/msil,jl->msij/dot_general | solution.py:62
  222.7 1.0 fusion.19
  223.7 0.5 copy-done.6
  224.2 1.5 slice_add_fusion
  (32 shorter events, 1.1 us)
Async XLA Ops:
  7.2 1.3 copy-start
  14.4 4.4 %copy-start.11 = (s32[16]{0:T(128)S(1)}, s32[16]{0:T(128)}, u32[]{:S(2)}) copy-start(s32[16]{0:T(128)} %param.21) | copy-start | bytes 196
  14.4 31.3 %all-to-all-start = ((bf16[3,4,80,720]{2,1,0,3:T(4,128)(2,1)}), bf16[3,4,80,720]{2,1,0,3:T(4,128)(2,1)S(1)}, u32[]{:S(2)}, u32[]{:S(2)}) async-start(bf16[3,4,80,720]{2,1,0,3:T(4,128)(2,1)} %copy.28), calls=%async_computation | async-start | bytes 4423680 | tf_op jit(solution)/shard_map/all_to_all | solution.py:28
  18.7 120.2 %all-reduce.2.cloned.1.call-start = ((), (), s32[]{:S(2)}) async-start(), calls=%async_computation.2 | async-start | bytes 2621440 | tf_op jit(solution)/shard_map/psum | solution.py:40
  49.4 1.6 copy-start.4
  49.4 1.7 copy-start.9
  52.4 1.6 copy-start.12
  52.4 1.6 copy-start.8
  52.5 1.6 copy-start.2
  140.1 2.7 %copy-start.3 = (s32[32,40,180]{2,1,0:T(8,128)S(1)}, s32[32,40,180]{2,1,0:T(8,128)}, u32[]{:S(2)}) copy-start(s32[32,40,180]{2,1,0:T(8,128)} %param.19) | copy-start | bytes 2764804
  142.8 1.7 copy-start.1
  177.8 1.2 copy-start.5
  179.1 0.9 copy-start.10
  219.9 2.8 %copy-start.7 = (bf16[4,80,720]{2,1,0:T(8,128)(2,1)S(1)}, bf16[4,80,720]{2,1,0:T(8,128)(2,1)}, u32[]{:S(2)}) copy-start(bf16[4,80,720]{2,1,0:T(8,128)(2,1)} %param.12) | copy-start | bytes 1382404
  222.7 1.6 copy-start.6
Sparse Core Ops, SparseCore 0:
  54.1 84.7 all-reduce.1
where the time goes:
time: 233 us
  waiting for transfers between devices  109 us (47%)
  blocking collectives  58.6 us (25%)
  local copies, waits for them, and re-layouts  28 us (12%)
  between operations  15 us (6%)
  matrix products  10.5 us (5%)
  other arithmetic  7.4 us (3%)
  starting transfers between devices  4.37 us (2%)
    psum x1, waiting for transfers between devices, shards(): summed = lax.psum(ensemble_term, 'mem')  83.2 us
    all_gather x1, blocking collectives, shards(): lax.all_gather(obs_gradient, 'mem', axis=1, tiled=True).astype(jnp.float32)  31.8 us
    all_to_all x1, blocking collectives, shards(): lax.all_to_all(back_lat, 'band', split_axis=2, concat_axis=3, tiled=True)  26.8 us
    all_to_all x1, waiting for transfers between devices, shards(): lax.all_to_all(along_lon, 'band', split_axis=3, concat_axis=2, tiled=True)  25.5 us
    convert_element_type x1, local copies, waits for them, and re-layouts, shards(): back_lat = jnp.einsum('ji,msjk->msik', lat_root, adjoints, preferred_elem...  6.66 us
    unnamed x27, local copies, waits for them, and re-layouts  5.19 us
  transfers between devices with their start and end apart: 2, of which 2 were waited for; matrix products, arithmetic and copies ran while one was open for 1% of the time, Pallas kernels for 0%

commit v1 on v0

v1 whole, which is shorter than its diff:
```python
import functools
import math

import jax
import jax.numpy as jnp
from jax import lax
from jax.experimental import pallas as pl
from jax.experimental.pallas import tpu as pltpu
from jax.sharding import PartitionSpec as P


F32 = jnp.float32
BF16 = jnp.bfloat16
VMEM = pl.BlockSpec(memory_space=pltpu.VMEM)
SMEM = pl.BlockSpec(memory_space=pltpu.SMEM)
NT = (((1,), (1,)), ((), ()))


def up(n, m):
    return -(-n // m) * m


def struct(shape, dtype):
    return jax.ShapeDtypeStruct(tuple(shape), dtype)


def call(kernel, outs, *args, smem=0, scratch=(), flops=10**8, vmem=24 << 20, spaces=None):
    size = sum(math.prod(a.shape) * a.dtype.itemsize for a in (*args, *outs))
    return pl.pallas_call(
        kernel,
        out_shape=outs,
        in_specs=[SMEM] * smem + [VMEM] * (len(args) - smem)
        if spaces is None
        else [pl.BlockSpec(memory_space=space) for space in spaces],
        out_specs=[VMEM] * len(outs),
        scratch_shapes=list(scratch),
        compiler_params=pltpu.CompilerParams(vmem_limit_bytes=vmem),
        cost_estimate=pl.CostEstimate(flops=flops, bytes_accessed=size, transcendentals=0),
    )(*args)


def dot(a, b):
    return jnp.dot(a, b, preferred_element_type=F32)


def dot_nt(a, b):
    return lax.dot_general(a, b, NT, preferred_element_type=F32)


def iota(shape, axis):
    return lax.broadcasted_iota(jnp.int32, shape, axis)


def one_hot(mask):
    return mask.astype(F32).astype(BF16)


def pack(pieces, start, width, slot):
    out = []
    for p in pieces:
        out.append(p[:, start : start + width])
        if slot > width:
            out.append(jnp.zeros((p.shape[0], slot - width), p.dtype))
    return jnp.concatenate(out, 1)


class Plan:
    def __init__(self, bands, ranks, alpha, lat_root):
        self.bands, self.ranks = bands, ranks
        self.members, self.species, self.rows, self.lon = alpha.shape
        self.lat = lat_root.shape[0]
        self.width = self.lon // bands // 2
        self.slot = up(self.width, 32)
        self.lanes = self.species * self.slot
        self.pixel = self.lat // ranks
        self.blocks = ranks // 2
        self.height = up(2 * self.pixel, 16)
        self.padded = self.blocks * self.height
        groups = math.gcd(ranks, self.rows)
        self.count, self.copies = self.rows // groups, ranks // groups
        self.extra = up(self.count, 16)
        self.late = self.members // 2


def factors(plan, weights, rank):
    total = weights[0] * weights[0]
    for i in range(1, weights.shape[0]):
        total = total + weights[i] * weights[i]
    norm = jnp.sqrt(jnp.full((1, plan.lanes), total.astype(F32)))
    return [
        0.8 * (jnp.full((1, plan.lanes), weights[rank * plan.members + m].astype(F32)) / norm)
        for m in range(plan.members)
    ]


def lon_kernel(plan, alpha, static, root, *refs):
    n = 2 * plan.bands
    x_refs, (a_buf, s_buf, r_buf, packed, sems) = refs[:n], refs[n:]
    species, rows, extra, members = plan.species, plan.rows, plan.extra, plan.members
    copies = [
        pltpu.make_async_copy(src, dst, sems.at[i])
        for i, (src, dst) in enumerate(((root, r_buf), (alpha, a_buf), (static, s_buf)))
    ]
    for copy in copies:
        copy.start()
    rank, me = lax.axis_index("mem"), lax.axis_index("band")
    t = iota((extra, rows), 0)
    mine = iota((extra, rows), 1) == (rank // plan.copies) * plan.count + t
    select = one_hot(mine & (t < plan.count) & (rank % plan.copies == 0))
    for copy in copies:
        copy.wait()
    fields = []
    for s in range(species):
        short = dot(select, s_buf[s]).astype(BF16)
        left = jnp.concatenate([a_buf[m, s] for m in range(members)] + [short], 0)
        fields.append(dot(left, r_buf[...]))
    for half in range(2):
        for b in range(plan.bands):
            at = (2 * b + half) * plan.width
            packed[half, b] = pack(fields, at, plan.width, plan.slot).astype(BF16)
    for own in range(2):
        half = (rank & 1) ^ 1 ^ own
        for k in range(plan.bands):
            x_refs[own * plan.bands + k][...] = packed[half, me ^ k]


def root_kernel(plan, root, w_ref):
    rank, me = lax.axis_index("mem"), lax.axis_index("band")
    side = plan.bands * plan.slot
    shape = (plan.lon, 2 * side)
    lane = iota(shape, 1)
    half = (lane // side) ^ 1 ^ (rank & 1)
    u = lane % plan.slot
    source = (lane % side // plan.slot ^ me) * (2 * plan.width) + half * plan.width + u
    pick = one_hot((iota(shape, 0) == source) & (u < plan.width))
    w_ref[...] = dot(root[...], pick).astype(BF16)


def prep_kernel(plan, pert, std, lat, perts_p, perts_o, std_p, std_o, lat_k, lat_t, lat_s):
    members, species, rows, total = plan.members, plan.species, plan.rows, plan.lat
    rank, me = lax.axis_index("mem"), lax.axis_index("band")
    for side in range(2):
        @pl.when(rank & 1 == side)
        def _():
            for half, p_ref, s_ref in ((1 - side, perts_p, std_p), (side, perts_o, std_o)):
                at = (half * plan.width, plan.width, plan.slot)
                for m in range(members):
                    pieces = [pert[m, s].astype(F32) for s in range(species)]
                    p_ref[m] = pack(pieces, *at).astype(BF16)
                s_ref[...] = 0.6 * pack([std[s] for s in range(species)], *at)
    row = iota((total, total), 0)
    order = one_hot(iota((total, total), 1) == (row // rows ^ me) * rows + row % rows)
    lat_k[...] = dot_nt(lat[...], order).astype(BF16)
    lat_t[...] = dot_nt(order, lat[...]).astype(BF16)
    row = iota((plan.bands * plan.extra, total), 0)
    t = row % plan.extra
    source = (row // plan.extra ^ me) * rows + (rank // plan.copies) * plan.count + t
    mine = iota((plan.bands * plan.extra, total), 1) == source
    pick = one_hot(mine & (t < plan.count) & (rank % plan.copies == 0))
    lat_s[...] = dot_nt(lat[...], pick).astype(BF16)


def normal_kernel(plan, error, jac, count, mask, h_p, h_o):
    channels, species, rows, lon = jac.shape
    rank = lax.axis_index("mem")
    pairs = [(s, t) for s in range(species) for t in range(s, species)]
    for r in range(0, rows, 8):
        n = min(8, rows - r)
        seen = count[r : r + n].astype(F32)

        def step(c, totals):
            weight = mask[c, r : r + n].astype(F32) * (seen * (1.0 / (error[c] * error[c])))
            j = [jac[c, s, r : r + n].astype(F32) for s in range(species)]
            scaled = [weight * x for x in j]
            return tuple(total + scaled[s] * j[t] for total, (s, t) in zip(totals, pairs))

        zero = tuple(jnp.zeros((n, lon), F32) for _ in pairs)
        sums = dict(zip(pairs, lax.fori_loop(0, channels, step, zero, unroll=2)))
        side = jnp.broadcast_to(rank & 1, (n, plan.width)) == 0
        for i, pair in enumerate(pairs):
            low, high = sums[pair][:, : plan.width], sums[pair][:, plan.width :]
            h_p[i, r : r + n, :] = jnp.where(side, high, low)
            h_o[i, r : r + n, :] = jnp.where(side, low, high)


def lat_kernel(plan, weights, lat_k, lat_s, pert, std, *refs):
    x_refs, out = refs[: plan.bands], refs[plan.bands]
    rows = plan.rows
    factor = factors(plan, weights, lax.axis_index("mem"))
    z = jnp.concatenate([x[plan.members * rows :, :] for x in x_refs], 0)
    acc = std[...] * dot(lat_s[...], z)
    for m in range(plan.members):
        z = jnp.concatenate([x[m * rows : (m + 1) * rows, :] for x in x_refs], 0)
        acc += factor[m] * pert[m].astype(F32) * dot(lat_k[...], z)
    out[...] = acc.astype(out.dtype)


def pair_kernel(plan, own, got, first, *refs):
    others, total = refs[:-1], refs[-1]
    block = lax.axis_index("mem") // 2
    total[...] = own[...] + got[...].astype(F32)
    for k, out in enumerate((first, *others)):
        at = pl.multiple_of((block ^ k) * plan.height, 8)
        out[...] = total[pl.ds(at, plan.height), :].astype(out.dtype)


def pixel_kernel(plan, h_own, h_got, first, *refs):
    got, out = refs[:-1], refs[-1]
    inc = first[...]
    for ref in got:
        inc = inc + ref[...].astype(F32)
    n, species = plan.pixel, plan.species
    pieces = [inc[:, t * plan.slot :][:, : plan.width] for t in range(species)]
    pairs = [(s, t) for s in range(species) for t in range(s, species)]
    rank = lax.axis_index("mem")
    for side in range(2):
        @pl.when(rank & 1 == side)
        def _():
            blocks = []
            for i, h in enumerate((h_own, h_got) if side == 0 else (h_got, h_own)):
                part = [p[i * n : (i + 1) * n] for p in pieces]
                sums = []
                for s in range(species):
                    terms = [h[pairs.index((min(s, t), max(s, t)))] * part[t] for t in range(species)]
                    sums.append(functools.reduce(jnp.add, terms))
                blocks.append(pack(sums, 0, plan.width, plan.slot))
            if plan.height > 2 * n:
                blocks.append(jnp.zeros((plan.height - 2 * n, plan.lanes), F32))
            out[...] = jnp.concatenate(blocks, 0).astype(BF16)


def back_kernel(plan, flip, weights, lat_t, pert, std, *refs):
    got, outs, full = refs[: plan.blocks], refs[plan.blocks : -1], refs[-1]
    rank, rows = lax.axis_index("mem"), plan.rows
    for k, ref in enumerate(got):
        at = pl.multiple_of((rank // 2 ^ k) * plan.height, 8)
        full[pl.ds(at, plan.height), :] = ref[...].astype(F32)
    g = full[...]
    factor = factors(plan, weights, rank ^ flip)
    for m in range(plan.members + 1):
        scale = factor[m] * pert[m].astype(F32) if m < plan.members else std[...]
        y = dot(lat_t[...], (scale * g).astype(BF16)).astype(BF16)
        late, at = m < plan.late, m - plan.late if m >= plan.late else m
        for k in range(plan.bands):
            outs[late * plan.bands + k][at * rows : (at + 1) * rows, :] = y[k * rows : (k + 1) * rows]


def product(plan, xs, w, fixed):
    at = fixed * plan.slot
    pieces = [x[:, at : at + plan.slot].astype(F32) for x in xs]
    return dot_nt(jnp.concatenate(pieces, 1).astype(BF16), w[...])


def early_kernel(plan, alpha, static, w, *refs):
    xs, (grad_alpha, grad_static) = refs[:-2], refs[-2:]
    rows, n = plan.rows, plan.members - plan.late
    for fixed in range(plan.species):
        @pl.when(pl.program_id(0) == fixed)
        def _():
            y = product(plan, xs, w, fixed)
            for m in range(n):
                grad_alpha[m, 0] = alpha[m, 0].astype(F32) + y[m * rows : (m + 1) * rows]
            grad_static[0] = static[0].astype(F32) + y[n * rows :]


def late_kernel(plan, _, alpha, w, *refs):
    xs, grad_alpha = refs[:-1], refs[-1]
    rows = plan.rows
    for fixed in range(plan.species):
        @pl.when(pl.program_id(0) == fixed)
        def _():
            y = product(plan, xs, w, fixed)
            for m in range(plan.late):
                grad_alpha[m, 0] = alpha[m, 0].astype(F32) + y[m * rows : (m + 1) * rows]


def shards(bands, ranks, *args):
    alpha, static_ctl, perturbations, static_std, lon_root, lat_root = args[:6]
    jacobian, obs_count, channel_mask, channel_error, member_weight = args[6:]
    plan = Plan(bands, ranks, alpha, lat_root)
    lanes, members, species = plan.lanes, plan.members, plan.species

    def send(x, axis, k):
        n = bands if axis == "band" else ranks
        return lax.ppermute(x, axis, [(i, i ^ k) for i in range(n)])

    def pad_lat(x, axis):
        if plan.height == 2 * plan.pixel:
            return x
        shape = list(x.shape)
        x = x.reshape(shape[:axis] + [plan.blocks, 2 * plan.pixel] + shape[axis + 1 :])
        widths = [(0, 0)] * x.ndim
        widths[axis + 1] = (0, plan.height - 2 * plan.pixel)
        shape[axis] = plan.padded
        return jnp.pad(x, widths).reshape(shape)

    sent = struct((members * plan.rows + plan.extra, lanes), BF16)
    got = call(
        functools.partial(lon_kernel, plan), [sent] * (2 * bands),
        alpha, static_ctl, lon_root, flops=10**9, spaces=[pl.ANY] * 3,
        scratch=[
            pltpu.VMEM(alpha.shape, BF16),
            pltpu.VMEM(static_ctl.shape, BF16),
            pltpu.VMEM(lon_root.shape, BF16),
            pltpu.VMEM((2, bands) + sent.shape, BF16),
            pltpu.SemaphoreType.DMA((3,)),
        ],
    )
    fields = [list(got[:bands]), list(got[bands:])]
    for own in range(2):
        fields[own][1:] = [send(fields[own][k], "band", k) for k in range(1, bands)]

    block = struct((plan.height, lanes), BF16)
    pert_shape = struct((members, plan.padded, lanes), BF16)
    std_shape = struct((plan.padded, lanes), F32)
    outs = [
        pert_shape, pert_shape, std_shape, std_shape,
        struct((plan.padded, plan.lat), BF16),
        struct((plan.lat, plan.padded), BF16),
        struct((plan.padded, bands * plan.extra), BF16),
    ]
    perts_p, perts_o, std_p, std_o, lat_k, lat_t, lat_s = call(
        functools.partial(prep_kernel, plan), outs,
        pad_lat(perturbations, 2), pad_lat(static_std, 1), pad_lat(lat_root, 0),
    )
    h_shape = struct((species * (species + 1) // 2, plan.pixel, plan.width), F32)
    h_p, h_o = call(
        functools.partial(normal_kernel, plan), [h_shape, h_shape],
        channel_error, jacobian, obs_count, channel_mask, smem=1,
    )
    h_got = send(h_p, "mem", 1)
    perts_got = send(perts_p, "mem", 1)

    sums = []
    for own, pert, std, kind in ((0, perts_p, std_p, BF16), (1, perts_o, std_o, F32)):
        sums += call(
            functools.partial(lat_kernel, plan), [struct((plan.padded, lanes), kind)],
            member_weight, lat_k, lat_s, pert, std, *fields[own], smem=1,
        )
    got = send(sums[0], "mem", 1)
    scratch = [pltpu.VMEM((plan.padded, lanes), F32)]
    parts = call(
        functools.partial(pair_kernel, plan),
        [struct((plan.height, lanes), F32)] + [block] * (plan.blocks - 1),
        sums[1], got, scratch=scratch,
    )
    parts = [parts[0]] + [send(parts[k], "mem", 2 * k) for k in range(1, plan.blocks)]
    (g,) = call(functools.partial(pixel_kernel, plan), [block], h_o, h_got, *parts)
    gs = [g] + [send(g, "mem", 2 * k) for k in range(1, plan.blocks)]

    (w,) = call(
        functools.partial(root_kernel, plan),
        [struct((plan.lon, 2 * bands * plan.slot), BF16)], lon_root, flops=10**9,
    )
    n_late = plan.late
    shapes = [struct(((members + 1 - n_late) * plan.rows, lanes), BF16)] * bands
    shapes += [struct((n_late * plan.rows, lanes), BF16)] * bands
    backs = {}
    for flip, pert in ((1, perts_got), (0, perts_o)):
        got = call(
            functools.partial(back_kernel, plan, flip), shapes,
            member_weight, lat_t, pert, std_o, *gs, smem=1, scratch=scratch,
        )
        for late in range(2):
            for k in range(bands):
                x = got[late * bands + k]
                if flip or k:
                    swap = [
                        (i * bands + j, (i ^ flip) * bands + (j ^ k))
                        for i in range(ranks)
                        for j in range(bands)
                    ]
                    x = lax.ppermute(x, ("mem", "band"), swap)
                backs[late, flip, k] = x
    early, last = [[backs[late, 1 - own, k] for own in range(2) for k in range(bands)] for late in range(2)]

    params = pltpu.CompilerParams(vmem_limit_bytes=24 << 20)
    cost = pl.CostEstimate(flops=10**9, bytes_accessed=10**7, transcendentals=0)
    n_early = members - n_late
    any_space = pl.BlockSpec(memory_space=pl.ANY)

    def block_of(n, first):
        return pl.BlockSpec((n, 1, plan.rows, plan.lon), lambda s: (first, s, 0, 0))

    static_block = pl.BlockSpec((1, plan.rows, plan.lon), lambda s: (s, 0, 0))
    grad_alpha, grad_static = pl.pallas_call(
        functools.partial(early_kernel, plan),
        grid=(species,),
        out_shape=[struct(alpha.shape, F32), struct(static_ctl.shape, F32)],
        in_specs=[block_of(n_early, 1), static_block] + [VMEM] * (1 + 2 * bands),
        out_specs=[block_of(n_early, 1), static_block],
        compiler_params=params, cost_estimate=cost, name="early",
    )(alpha, static_ctl, w, *early)
    grad_alpha = pl.pallas_call(
        functools.partial(late_kernel, plan),
        grid=(species,),
        out_shape=struct(alpha.shape, F32),
        in_specs=[any_space, block_of(n_late, 0)] + [VMEM] * (1 + 2 * bands),
        out_specs=block_of(n_late, 0),
        input_output_aliases={0: 0},
        compiler_params=params, cost_estimate=cost, name="late",
    )(grad_alpha, alpha, w, *last)
    return grad_alpha, grad_static


def solution(mesh):
    bands, ranks = mesh.shape["band"], mesh.shape["mem"]
    in_specs = (
        P("mem", None, "band", None),
        P(None, "band", None),
        P("mem", None, None, "band"),
        P(None, None, "band"),
        P(),
        P(),
        P(None, None, "mem", "band"),
        P("mem", "band"),
        P(None, "mem", "band"),
        P(),
        P(),
    )
    out_specs = (P("mem", None, "band", None), P(None, "band", None))

    def body(*args):
        return shards(bands, ranks, *args)

    return jax.shard_map(body, mesh=mesh, in_specs=in_specs, out_specs=out_specs, check_vma=False)
```

time: 233 us -> 84.6 us (0.36)
  waiting for transfers between devices: 109 us -> 19.3 us
  blocking collectives: 58.6 us -> 0 us
  starting transfers between devices: 4.37 us -> 32 us
  Pallas kernels: 0 us -> 23.3 us
  local copies, waits for them, and re-layouts: 28 us -> 8.78 us
  between operations: 15 us -> 0.92 us
  matrix products: 10.5 us -> 0 us
  other arithmetic: 7.4 us -> 0 us
    psum x1 -> x0, waiting for transfers between devices: 83.2 us -> none  [shards(): summed = lax.psum(ensemble_term, 'mem')]
    ppermute x0 -> x29, starting transfers between devices: none -> 32 us  [the longest x15 17.3 us: send(): return lax.ppermute(x, axis, [(i, i ^ k) for i in range(n)])]
    all_gather x1 -> x0, blocking collectives: 31.8 us -> none  [shards(): lax.all_gather(obs_gradient, 'mem', axis=1, tiled=True).astype(jnp.float32)]
    all_to_all x1 -> x0, blocking collectives: 26.8 us -> none  [shards(): lax.all_to_all(back_lat, 'band', split_axis=2, concat_axis=3, tiled=True)]
    all_to_all x1 -> x0, waiting for transfers between devices: 25.5 us -> none  [shards(): lax.all_to_all(along_lon, 'band', split_axis=3, concat_axis=2, tiled=True)]
    pallas_call x0 -> x12, Pallas kernels: none -> 23.3 us  [the longest x10 17.3 us: call(): pl.pallas_call(kernel, out_shape=outs, in_specs=[SMEM] * smem + [VMEM] *...]
    ppermute x0 -> x29, waiting for transfers between devices: none -> 19.3 us  [the longest x15 13.5 us: send(): return lax.ppermute(x, axis, [(i, i ^ k) for i in range(n)])]
    dot_general x5 -> x0, matrix products: 10.5 us -> none  [the longest x1 2.77 us: shards(): jnp.einsum('msil,jl->msij', returned, lon_root, preferred_element_type=jn...]
  transfers between devices with their start and end apart: 2 -> 29, of which waited for: 2 -> 7; matrix products, arithmetic and copies ran while one was open for 1% -> 4% of each run, Pallas kernels for 0% -> 19%
where the time goes in v1:
time: 84.6 us; the launch traced here: 84.3 us
  starting transfers between devices  32 us (38%)
  Pallas kernels  23.3 us (28%)
  waiting for transfers between devices  19.3 us (23%)
  local copies, waits for them, and re-layouts  8.78 us (10%)
  between operations  0.92 us (1%)
    pallas_call x10, Pallas kernels, call(): pl.pallas_call(kernel, out_shape=outs, in_specs=[SMEM] * smem + [VMEM] *...  17.3 us
    ppermute x15, starting transfers between devices, send(): return lax.ppermute(x, axis, [(i, i ^ k) for i in range(n)])  17.3 us
    ppermute x14, starting transfers between devices, shards(): x = lax.ppermute(x, ('mem', 'band'), swap)  14.8 us
    ppermute x15, waiting for transfers between devices, send(): return lax.ppermute(x, axis, [(i, i ^ k) for i in range(n)])  13.5 us
    unnamed x40, local copies, waits for them, and re-layouts  8.78 us
    ppermute x14, waiting for transfers between devices, shards(): x = lax.ppermute(x, ('mem', 'band'), swap)  5.8 us
    pallas_call x1, Pallas kernels, shards(): pl.pallas_call(functools.partial(early_kernel, plan), grid=(species,), ou...  3.16 us
    pallas_call x1, Pallas kernels, shards(): pl.pallas_call(functools.partial(late_kernel, plan), grid=(species,), out...  2.85 us
  transfers between devices with their start and end apart: 29, of which 7 were waited for; matrix products, arithmetic and copies ran while one was open for 4% of the time, Pallas kernels for 19%

profile of v1, /device:TPU:0, one launch (start us, length us, event | category | flops | bytes accessed | tf_op | source)
XLA Modules:
  0.0 84.3 jit_solution(401419602233736695)
XLA Ops:
  0.6 1.2 %copy-done.2 = bf16[2,4,80,720]{3,2,1,0:T(8,128)(2,1)S(1)} copy-done((bf16[2,4,80,720]{3,2,1,0:T(8,128)(2,1)S(1)}, bf16[2,4,80,720]{3,2,1,0:T(8,128)(2,1)}, u32[]{:S(2)}) %copy-start.2) | copy-done | bytes 921624
  1.8 1.2 %copy-done.8 = bf16[720,720]{1,0:T(8,128)(2,1)S(1)} copy-done((bf16[720,720]{1,0:T(8,128)(2,1)S(1)}, bf16[720,720]{1,0:T(8,128)(2,1)}, u32[]{:S(2)}) %copy-start.8) | copy-done | bytes 1036824
  4.1 3.0 %shard_map.125 = (bf16[176,384]{1,0:T(8,128)(2,1)S(1)}, bf16[176,384]{1,0:T(8,128)(2,1)}, bf16[176,384]{1,0:T(8,128)(2,1)}, bf16[176,384]{1,0:T(8,128)(2,1)}, bf...) custom-call(bf16[2,4,80,720]{3,2,1,0:T(8,128)(2,1)S(1)} %copy-done.2, ...), custom_call_target="tpu_custom_call" | custom-call | flops 1000000000 | bytes 3500544 | tf_op jit(solution)/shard_map/pallas_call | solution.py:29
  9.6 2.5 %collective-permute-start.6 = (bf16[176,384]{1,0:T(8,128)(2,1)}, bf16[176,384]{1,0:T(8,128)(2,1)S(1)}, u32[]{:S(2)}, u32[]{:S(2)}) collective-permute-start(bf16[176,384]{1,0:T(8,128)(2,1)} %get-tuple-element.56), channel_id=1, source_target_pairs={{0,2},{1,3},{2,0},{3,1},{4,6},{5,7},{6,4},{7,5},{8,10},{9,11},{10,... | collective-permute-start | bytes 405512 | tf_op jit(solution)/shard_map/ppermute | solution.py:285
  12.2 1.3 %copy.14.pert = bf16[2,4,320,180]{3,2,1,0:T(8,128)(2,1)S(1)} copy(bf16[2,4,320,180]{2,1,3,0:T(4,128)(2,1)S(1)} %copy-done.18) | data formatting | bytes 1843200 | tf_op args[2]
  13.5 2.0 %copy.15.std = f32[4,320,180]{2,1,0:T(8,128)S(1)} copy(f32[4,320,180]{1,0,2:T(4,128)} %param.14) | data formatting | bytes 1843200 | tf_op args[3]
  15.5 1.6 %shard_map.123 = (bf16[2,320,384]{2,1,0:T(8,128)(2,1)S(1)}, bf16[2,320,384]{2,1,0:T(8,128)(2,1)S(1)}, f32[320,384]{1,0:T(8,128)S(1)}, f32[320,384]{1,0:T(8,128)S...) custom-call(bf16[2,4,320,180]{3,2,1,0:T(8,128)(2,1)S(1)} %copy.14.pert, ...), custom_call_target="tpu_custom_call" | custom-call | flops 100000000 | bytes 4464640 | tf_op jit(solution)/shard_map/pallas_call | solution.py:29
  17.2 2.0 %collective-permute-done.7.refs_3_ = bf16[176,384]{1,0:T(8,128)(2,1)S(1)} collective-permute-done((bf16[176,384]{1,0:T(8,128)(2,1)}, bf16[176,384]{1,0:T(8,128)(2,1)S(1)}, u32[]{:S(2)}, u32[]{:S(2)}) %collective-permute-start.7) | collective-permute-done | bytes 135200 | tf_op jit(solution)/shard_map/ppermute | solution.py:285
  20.4 1.6 %collective-permute-start.8 = (bf16[320,384]{1,0:T(8,128)(2,1)S(1)}, bf16[320,384]{1,0:T(8,128)(2,1)S(1)}, u32[]{:S(2)}, u32[]{:S(2)}) collective-permute-start(bf16[320,384]{1,0:T(8,128)(2,1)S(1)} %shard_map.127), channel_id=1, source_target_pairs={{0,4},{4,0},{8,12},{12,8},{16,20},{20,16},{24,28},{28,24},{1,5},{5... | collective-permute-start | bytes 737288 | tf_op jit(solution)/shard_map/ppermute | solution.py:285
  22.5 1.5 %collective-permute-start.3 = (bf16[176,384]{1,0:T(8,128)(2,1)S(1)}, bf16[176,384]{1,0:T(8,128)(2,1)S(1)}, u32[]{:S(2)}, u32[]{:S(2)}) collective-permute-start(bf16[176,384]{1,0:T(8,128)(2,1)S(1)} %copy-done.15), channel_id=1, source_target_pairs={{0,2},{1,3},{2,0},{3,1},{4,6},{5,7},{6,4},{7,5},{8,10},{9,11},{10,... | collective-permute-start | bytes 405512 | tf_op jit(solution)/shard_map/ppermute | solution.py:285
  24.4 6.4 %shard_map.124 = (f32[10,40,90]{2,1,0:T(8,128)S(1)}, f32[10,40,90]{2,1,0:T(8,128)S(1)}) custom-call(f32[32]{0:T(128)S(1)} %copy-done.7, bf16[32,4,40,180]{3,2,1,0:T(8,128)(2,1)S(1)} %copy-done, s32[40,180]{1,0:T(8,128)S(1)} %copy-done.5, s32[32,40,180]{2,1,0:T(8,128)S(1)} %copy-done.1), custom_call_target="tpu_custom_call" | custom-call | flops 100000000 | bytes 3081728 | tf_op jit(solution)/shard_map/pallas_call | solution.py:29
  30.8 1.6 %collective-permute-start.1 = (f32[10,40,90]{2,1,0:T(8,128)S(1)}, f32[10,40,90]{2,1,0:T(8,128)S(1)}, u32[]{:S(2)}, u32[]{:S(2)}) collective-permute-start(f32[10,40,90]{2,1,0:T(8,128)S(1)} %get-tuple-element.45), channel_id=1, source_target_pairs={{0,4},{4,0},{8,12},{12,8},{16,20},{20,16},{24,28},{28,24},{1,5},{5... | collective-permute-start | bytes 432008 | tf_op jit(solution)/shard_map/ppermute | solution.py:285
  33.6 2.7 %collective-permute-start.10 = (bf16[80,384]{1,0:T(8,128)(2,1)S(1)}, bf16[80,384]{1,0:T(8,128)(2,1)S(1)}, u32[]{:S(2)}, u32[]{:S(2)}) collective-permute-start(bf16[80,384]{1,0:T(8,128)(2,1)S(1)} %get-tuple-element.60), channel_id=1, source_target_pairs={{0,16},{4,20},{8,24},{12,28},{16,0},{20,4},{24,8},{28,12},{1,17},{... | collective-permute-start | bytes 184328 | tf_op jit(solution)/shard_map/ppermute | solution.py:285
  36.3 1.3 %collective-permute-start.11 = (bf16[80,384]{1,0:T(8,128)(2,1)S(1)}, bf16[80,384]{1,0:T(8,128)(2,1)S(1)}, u32[]{:S(2)}, u32[]{:S(2)}) collective-permute-start(bf16[80,384]{1,0:T(8,128)(2,1)S(1)} %get-tuple-element.61), channel_id=1, source_target_pairs={{0,24},{4,28},{8,16},{12,20},{16,8},{20,12},{24,0},{28,4},{1,25},{... | collective-permute-start | bytes 184328 | tf_op jit(solution)/shard_map/ppermute | solution.py:285
  37.8 5.5 %collective-permute-done.1.h_got = f32[10,40,90]{2,1,0:T(8,128)S(1)} collective-permute-done((f32[10,40,90]{2,1,0:T(8,128)S(1)}, f32[10,40,90]{2,1,0:T(8,128)S(1)}, u32[]{:S(2)}, u32[]{:S(2)}) %collective-permute-start.1) | collective-permute-done | bytes 144032 | tf_op jit(solution)/shard_map/ppermute | solution.py:285
  43.8 1.8 %collective-permute-start.12 = (bf16[80,384]{1,0:T(8,128)(2,1)S(1)}, bf16[80,384]{1,0:T(8,128)(2,1)S(1)}, u32[]{:S(2)}, u32[]{:S(2)}) collective-permute-start(bf16[80,384]{1,0:T(8,128)(2,1)S(1)} %shard_map.129.refs_0_), channel_id=1, source_target_pairs={{0,8},{4,12},{8,0},{12,4},{16,24},{20,28},{24,16},{28,20},{1,9},{5... | collective-permute-start | bytes 184328 | tf_op jit(solution)/shard_map/ppermute | solution.py:285
  45.6 2.6 %collective-permute-start.13 = (bf16[80,384]{1,0:T(8,128)(2,1)S(1)}, bf16[80,384]{1,0:T(8,128)(2,1)S(1)}, u32[]{:S(2)}, u32[]{:S(2)}) collective-permute-start(bf16[80,384]{1,0:T(8,128)(2,1)S(1)} %shard_map.129.refs_0_), channel_id=1, source_target_pairs={{0,16},{4,20},{8,24},{12,28},{16,0},{20,4},{24,8},{28,12},{1,17},{... | collective-permute-start | bytes 184328 | tf_op jit(solution)/shard_map/ppermute | solution.py:285
  48.2 3.9 %collective-permute-done.13.refs_2_ = bf16[80,384]{1,0:T(8,128)(2,1)S(1)} collective-permute-done((bf16[80,384]{1,0:T(8,128)(2,1)S(1)}, bf16[80,384]{1,0:T(8,128)(2,1)S(1)}, u32[]{:S(2)}, u32[]{:S(2)}) %collective-permute-start.13) | collective-permute-done | bytes 61472 | tf_op jit(solution)/shard_map/ppermute | solution.py:285
  52.2 2.0 %collective-permute-done.14.refs_3_ = bf16[80,384]{1,0:T(8,128)(2,1)S(1)} collective-permute-done((bf16[80,384]{1,0:T(8,128)(2,1)S(1)}, bf16[80,384]{1,0:T(8,128)(2,1)S(1)}, u32[]{:S(2)}, u32[]{:S(2)}) %collective-permute-start.14) | collective-permute-done | bytes 61472 | tf_op jit(solution)/shard_map/ppermute | solution.py:285
  54.2 1.2 %shard_map.131 = (bf16[160,384]{1,0:T(8,128)(2,1)S(1)}, bf16[160,384]{1,0:T(8,128)(2,1)S(1)}, bf16[160,384]{1,0:T(8,128)(2,1)S(1)}, bf16[160,384]{1,0:T(8,128)(2...) custom-call(s32[16]{0:T(128)S(1)} %copy-done.6, ...), custom_call_target="tpu_custom_call" | custom-call | flops 100000000 | bytes 2170944 | tf_op jit(solution)/shard_map/pallas_call | solution.py:29
  55.5 1.6 %collective-permute-start.20 = (bf16[160,384]{1,0:T(8,128)(2,1)S(1)}, bf16[160,384]{1,0:T(8,128)(2,1)S(1)}, u32[]{:S(2)}, u32[]{:S(2)}) collective-permute-start(bf16[160,384]{1,0:T(8,128)(2,1)S(1)} %get-tuple-element.68), channel_id=1, source_target_pairs={{0,2},{1,3},{2,0},{3,1},{4,6},{5,7},{6,4},{7,5},{8,10},{9,11},{10,... | collective-permute-start | bytes 368648 | tf_op jit(solution)/shard_map/ppermute | solution.py:373
  58.9 1.2 %shard_map.130 = (bf16[160,384]{1,0:T(8,128)(2,1)S(1)}, bf16[160,384]{1,0:T(8,128)(2,1)S(1)}, bf16[160,384]{1,0:T(8,128)(2,1)S(1)}, bf16[160,384]{1,0:T(8,128)(2...) custom-call(s32[16]{0:T(128)S(1)} %copy-done.6, ...), custom_call_target="tpu_custom_call" | custom-call | flops 100000000 | bytes 2170944 | tf_op jit(solution)/shard_map/pallas_call | solution.py:29
  60.2 1.6 %collective-permute-start.15 = (bf16[160,384]{1,0:T(8,128)(2,1)S(1)}, bf16[160,384]{1,0:T(8,128)(2,1)S(1)}, u32[]{:S(2)}, u32[]{:S(2)}) collective-permute-start(bf16[160,384]{1,0:T(8,128)(2,1)S(1)} %get-tuple-element.62), channel_id=1, source_target_pairs={{0,4},{1,5},{2,6},{3,7},{4,0},{5,1},{6,2},{7,3},{8,12},{9,13},{10,... | collective-permute-start | bytes 368648 | tf_op jit(solution)/shard_map/ppermute | solution.py:373
  61.7 1.3 %collective-permute-done.27.refs_6_ = bf16[80,384]{1,0:T(8,128)(2,1)S(1)} collective-permute-done((bf16[80,384]{1,0:T(8,128)(2,1)S(1)}, bf16[80,384]{1,0:T(8,128)(2,1)S(1)}, u32[]{:S(2)}, u32[]{:S(2)}) %collective-permute-start.27) | collective-permute-done | bytes 61472 | tf_op jit(solution)/shard_map/ppermute | solution.py:373
  63.2 2.3 %collective-permute-start.17 = (bf16[160,384]{1,0:T(8,128)(2,1)S(1)}, bf16[160,384]{1,0:T(8,128)(2,1)S(1)}, u32[]{:S(2)}, u32[]{:S(2)}) collective-permute-start(bf16[160,384]{1,0:T(8,128)(2,1)S(1)} %get-tuple-element.64), channel_id=1, source_target_pairs={{0,6},{1,7},{2,4},{3,5},{4,2},{5,3},{6,0},{7,1},{8,14},{9,15},{10,... | collective-permute-start | bytes 368648 | tf_op jit(solution)/shard_map/ppermute | solution.py:373
  65.5 1.4 %collective-permute-start.18 = (bf16[160,384]{1,0:T(8,128)(2,1)S(1)}, bf16[160,384]{1,0:T(8,128)(2,1)S(1)}, u32[]{:S(2)}, u32[]{:S(2)}) collective-permute-start(bf16[160,384]{1,0:T(8,128)(2,1)S(1)} %get-tuple-element.65), channel_id=1, source_target_pairs={{0,7},{1,6},{2,5},{3,4},{4,3},{5,2},{6,1},{7,0},{8,15},{9,14},{10,... | collective-permute-start | bytes 368648 | tf_op jit(solution)/shard_map/ppermute | solution.py:373
  68.5 1.4 %collective-permute-start.22 = (bf16[80,384]{1,0:T(8,128)(2,1)S(1)}, bf16[80,384]{1,0:T(8,128)(2,1)S(1)}, u32[]{:S(2)}, u32[]{:S(2)}) collective-permute-start(bf16[80,384]{1,0:T(8,128)(2,1)S(1)} %get-tuple-element.71), channel_id=1, source_target_pairs={{0,4},{1,5},{2,6},{3,7},{4,0},{5,1},{6,2},{7,3},{8,12},{9,13},{10,... | collective-permute-start | bytes 184328 | tf_op jit(solution)/shard_map/ppermute | solution.py:373
  69.9 4.0 %collective-permute-done.16.refs_1_ = bf16[160,384]{1,0:T(8,128)(2,1)S(1)} collective-permute-done((bf16[160,384]{1,0:T(8,128)(2,1)S(1)}, bf16[160,384]{1,0:T(8,128)(2,1)S(1)}, u32[]{:S(2)}, u32[]{:S(2)}) %collective-permute-start.16) | collective-permute-done | bytes 122912 | tf_op jit(solution)/shard_map/ppermute | solution.py:373
  74.8 1.8 %collective-permute-start.24 = (bf16[80,384]{1,0:T(8,128)(2,1)S(1)}, bf16[80,384]{1,0:T(8,128)(2,1)S(1)}, u32[]{:S(2)}, u32[]{:S(2)}) collective-permute-start(bf16[80,384]{1,0:T(8,128)(2,1)S(1)} %get-tuple-element.73), channel_id=1, source_target_pairs={{0,6},{1,7},{2,4},{3,5},{4,2},{5,3},{6,0},{7,1},{8,14},{9,15},{10,... | collective-permute-start | bytes 184328 | tf_op jit(solution)/shard_map/ppermute | solution.py:373
  76.6 1.3 %collective-permute-start.25 = (bf16[80,384]{1,0:T(8,128)(2,1)S(1)}, bf16[80,384]{1,0:T(8,128)(2,1)S(1)}, u32[]{:S(2)}, u32[]{:S(2)}) collective-permute-start(bf16[80,384]{1,0:T(8,128)(2,1)S(1)} %get-tuple-element.74), channel_id=1, source_target_pairs={{0,7},{1,6},{2,5},{3,4},{4,3},{5,2},{6,1},{7,0},{8,15},{9,14},{10,... | collective-permute-start | bytes 184328 | tf_op jit(solution)/shard_map/ppermute | solution.py:373
  77.9 3.2 %early.1 = (f32[2,4,80,720]{3,2,1,0:T(8,128)}, f32[4,80,720]{2,1,0:T(8,128)}) custom-call(bf16[2,4,80,720]{3,2,1,0:T(8,128)(2,1)S(1)} %copy-done.3, bf16[4,80,720]{2,1,0:T(8,128)(2,1)S(1)} %copy-done.11, bf16[720,768]{1,0:T(8,128)(2,1)S(1)} %shard_map.122.w, bf16[160,384]{1,0:T(8,128)(2,1)S(1)} %collective-permute-done.15.refs_0_, ...), custom_call_target="tpu_custom_call" | custom-call | flops 1000000000 | bytes 10000000 | tf_op jit(solution)/shard_map/early/pallas_call | solution.py:386
  81.5 2.9 %late.1 = f32[2,4,80,720]{3,2,1,0:T(8,128)} custom-call(f32[2,4,80,720]{3,2,1,0:T(8,128)} %get-tuple-element.70._, bf16[2,4,80,720]{3,2,1,0:T(8,128)(2,1)S(1)} %copy-done.3, bf16[720,768]{1,0:T(8,128)(2,1)S(1)} %shard_map.122.w, bf16[80,384]{1,0:T(8,128)(2,1)S(1)} %collective-permute-done.22.refs_0_, ...), custom_call_target="tpu_custom_call", output_to_operand_aliasing={{}: (0, {})} | custom-call | flops 1000000000 | bytes 10000000 | tf_op jit(solution)/shard_map/late/pallas_call | solution.py:394
  (78 shorter events, 12.6 us)
Async XLA Ops:
  9.1 8.1 %collective-permute-start.5 = (bf16[176,384]{1,0:T(8,128)(2,1)}, bf16[176,384]{1,0:T(8,128)(2,1)S(1)}, u32[]{:S(2)}, u32[]{:S(2)}) collective-permute-start(bf16[176,384]{1,0:T(8,128)(2,1)} %get-tuple-element.55), channel_id=1, source_target_pairs={{0,1},{1,0},{2,3},{3,2},{4,5},{5,4},{6,7},{7,6},{8,9},{9,8},{10,11... | collective-permute-start | bytes 405512 | tf_op jit(solution)/shard_map/ppermute | solution.py:285
  9.6 7.6 %collective-permute-start.6 = (bf16[176,384]{1,0:T(8,128)(2,1)}, bf16[176,384]{1,0:T(8,128)(2,1)S(1)}, u32[]{:S(2)}, u32[]{:S(2)}) collective-permute-start(bf16[176,384]{1,0:T(8,128)(2,1)} %get-tuple-element.56), channel_id=1, source_target_pairs={{0,2},{1,3},{2,0},{3,1},{4,6},{5,7},{6,4},{7,5},{8,10},{9,11},{10,... | collective-permute-start | bytes 405512 | tf_op jit(solution)/shard_map/ppermute | solution.py:285
  12.1 7.2 %collective-permute-start.7 = (bf16[176,384]{1,0:T(8,128)(2,1)}, bf16[176,384]{1,0:T(8,128)(2,1)S(1)}, u32[]{:S(2)}, u32[]{:S(2)}) collective-permute-start(bf16[176,384]{1,0:T(8,128)(2,1)} %get-tuple-element.57), channel_id=1, source_target_pairs={{0,3},{1,2},{2,1},{3,0},{4,7},{5,6},{6,5},{7,4},{8,11},{9,10},{10,... | collective-permute-start | bytes 405512 | tf_op jit(solution)/shard_map/ppermute | solution.py:285
  20.4 13.1 %collective-permute-start.8 = (bf16[320,384]{1,0:T(8,128)(2,1)S(1)}, bf16[320,384]{1,0:T(8,128)(2,1)S(1)}, u32[]{:S(2)}, u32[]{:S(2)}) collective-permute-start(bf16[320,384]{1,0:T(8,128)(2,1)S(1)} %shard_map.127), channel_id=1, source_target_pairs={{0,4},{4,0},{8,12},{12,8},{16,20},{20,16},{24,28},{28,24},{1,5},{5... | collective-permute-start | bytes 737288 | tf_op jit(solution)/shard_map/ppermute | solution.py:285
  21.9 35.8 %collective-permute-start = (bf16[2,320,384]{2,1,0:T(8,128)(2,1)S(1)}, bf16[2,320,384]{2,1,0:T(8,128)(2,1)S(1)}, u32[]{:S(2)}, u32[]{:S(2)}) collective-permute-start(bf16[2,320,384]{2,1,0:T(8,128)(2,1)S(1)} %get-tuple-element.42.pert), channel_id=1, source_target_pairs={{0,4},{4,0},{8,12},{12,8},{16,20},{20,16},{24,28},{28,24},{1,5},{5... | collective-permute-start | bytes 1474568 | tf_op jit(solution)/shard_map/ppermute | solution.py:285
  22.5 8.3 %collective-permute-start.2 = (bf16[176,384]{1,0:T(8,128)(2,1)S(1)}, bf16[176,384]{1,0:T(8,128)(2,1)S(1)}, u32[]{:S(2)}, u32[]{:S(2)}) collective-permute-start(bf16[176,384]{1,0:T(8,128)(2,1)S(1)} %copy-done.17), channel_id=1, source_target_pairs={{0,1},{1,0},{2,3},{3,2},{4,5},{5,4},{6,7},{7,6},{8,9},{9,8},{10,11... | collective-permute-start | bytes 405512 | tf_op jit(solution)/shard_map/ppermute | solution.py:285
  22.5 9.9 %collective-permute-start.3 = (bf16[176,384]{1,0:T(8,128)(2,1)S(1)}, bf16[176,384]{1,0:T(8,128)(2,1)S(1)}, u32[]{:S(2)}, u32[]{:S(2)}) collective-permute-start(bf16[176,384]{1,0:T(8,128)(2,1)S(1)} %copy-done.15), channel_id=1, source_target_pairs={{0,2},{1,3},{2,0},{3,1},{4,6},{5,7},{6,4},{7,5},{8,10},{9,11},{10,... | collective-permute-start | bytes 405512 | tf_op jit(solution)/shard_map/ppermute | solution.py:285
  24.0 8.4 %collective-permute-start.4 = (bf16[176,384]{1,0:T(8,128)(2,1)S(1)}, bf16[176,384]{1,0:T(8,128)(2,1)S(1)}, u32[]{:S(2)}, u32[]{:S(2)}) collective-permute-start(bf16[176,384]{1,0:T(8,128)(2,1)S(1)} %copy-done.13), channel_id=1, source_target_pairs={{0,3},{1,2},{2,1},{3,0},{4,7},{5,6},{6,5},{7,4},{8,11},{9,10},{10,... | collective-permute-start | bytes 405512 | tf_op jit(solution)/shard_map/ppermute | solution.py:285
  30.8 12.5 %collective-permute-start.1 = (f32[10,40,90]{2,1,0:T(8,128)S(1)}, f32[10,40,90]{2,1,0:T(8,128)S(1)}, u32[]{:S(2)}, u32[]{:S(2)}) collective-permute-start(f32[10,40,90]{2,1,0:T(8,128)S(1)} %get-tuple-element.45), channel_id=1, source_target_pairs={{0,4},{4,0},{8,12},{12,8},{16,20},{20,16},{24,28},{28,24},{1,5},{5... | collective-permute-start | bytes 432008 | tf_op jit(solution)/shard_map/ppermute | solution.py:285
  33.6 9.7 %collective-permute-start.10 = (bf16[80,384]{1,0:T(8,128)(2,1)S(1)}, bf16[80,384]{1,0:T(8,128)(2,1)S(1)}, u32[]{:S(2)}, u32[]{:S(2)}) collective-permute-start(bf16[80,384]{1,0:T(8,128)(2,1)S(1)} %get-tuple-element.60), channel_id=1, source_target_pairs={{0,16},{4,20},{8,24},{12,28},{16,0},{20,4},{24,8},{28,12},{1,17},{... | collective-permute-start | bytes 184328 | tf_op jit(solution)/shard_map/ppermute | solution.py:285
  36.3 7.1 %collective-permute-start.11 = (bf16[80,384]{1,0:T(8,128)(2,1)S(1)}, bf16[80,384]{1,0:T(8,128)(2,1)S(1)}, u32[]{:S(2)}, u32[]{:S(2)}) collective-permute-start(bf16[80,384]{1,0:T(8,128)(2,1)S(1)} %get-tuple-element.61), channel_id=1, source_target_pairs={{0,24},{4,28},{8,16},{12,20},{16,8},{20,12},{24,0},{28,4},{1,25},{... | collective-permute-start | bytes 184328 | tf_op jit(solution)/shard_map/ppermute | solution.py:285
  37.6 5.8 %collective-permute-start.9 = (bf16[80,384]{1,0:T(8,128)(2,1)S(1)}, bf16[80,384]{1,0:T(8,128)(2,1)S(1)}, u32[]{:S(2)}, u32[]{:S(2)}) collective-permute-start(bf16[80,384]{1,0:T(8,128)(2,1)S(1)} %get-tuple-element.59), channel_id=1, source_target_pairs={{0,8},{4,12},{8,0},{12,4},{16,24},{20,28},{24,16},{28,20},{1,9},{5... | collective-permute-start | bytes 184328 | tf_op jit(solution)/shard_map/ppermute | solution.py:285
  43.8 4.5 %collective-permute-start.12 = (bf16[80,384]{1,0:T(8,128)(2,1)S(1)}, bf16[80,384]{1,0:T(8,128)(2,1)S(1)}, u32[]{:S(2)}, u32[]{:S(2)}) collective-permute-start(bf16[80,384]{1,0:T(8,128)(2,1)S(1)} %shard_map.129.refs_0_), channel_id=1, source_target_pairs={{0,8},{4,12},{8,0},{12,4},{16,24},{20,28},{24,16},{28,20},{1,9},{5... | collective-permute-start | bytes 184328 | tf_op jit(solution)/shard_map/ppermute | solution.py:285
  45.6 6.6 %collective-permute-start.13 = (bf16[80,384]{1,0:T(8,128)(2,1)S(1)}, bf16[80,384]{1,0:T(8,128)(2,1)S(1)}, u32[]{:S(2)}, u32[]{:S(2)}) collective-permute-start(bf16[80,384]{1,0:T(8,128)(2,1)S(1)} %shard_map.129.refs_0_), channel_id=1, source_target_pairs={{0,16},{4,20},{8,24},{12,28},{16,0},{20,4},{24,8},{28,12},{1,17},{... | collective-permute-start | bytes 184328 | tf_op jit(solution)/shard_map/ppermute | solution.py:285
  48.2 6.0 %collective-permute-start.14 = (bf16[80,384]{1,0:T(8,128)(2,1)S(1)}, bf16[80,384]{1,0:T(8,128)(2,1)S(1)}, u32[]{:S(2)}, u32[]{:S(2)}) collective-permute-start(bf16[80,384]{1,0:T(8,128)(2,1)S(1)} %shard_map.129.refs_0_), channel_id=1, source_target_pairs={{0,24},{4,28},{8,16},{12,20},{16,8},{20,12},{24,0},{28,4},{1,25},{... | collective-permute-start | bytes 184328 | tf_op jit(solution)/shard_map/ppermute | solution.py:285
  54.2 12.8 %copy-start.9 = (bf16[720,720]{1,0:T(8,128)(2,1)S(1)}, bf16[720,720]{1,0:T(8,128)(2,1)}, u32[]{:S(2)}) copy-start(bf16[720,720]{1,0:T(8,128)(2,1)} %root.3) | copy-start | bytes 3110404
  55.4 7.8 %collective-permute-start.19 = (bf16[160,384]{1,0:T(8,128)(2,1)S(1)}, bf16[160,384]{1,0:T(8,128)(2,1)S(1)}, u32[]{:S(2)}, u32[]{:S(2)}) collective-permute-start(bf16[160,384]{1,0:T(8,128)(2,1)S(1)} %get-tuple-element.67), channel_id=1, source_target_pairs={{0,1},{1,0},{2,3},{3,2},{4,5},{5,4},{6,7},{7,6},{8,9},{9,8},{10,11... | collective-permute-start | bytes 368648 | tf_op jit(solution)/shard_map/ppermute | solution.py:373
  55.5 10.0 %collective-permute-start.20 = (bf16[160,384]{1,0:T(8,128)(2,1)S(1)}, bf16[160,384]{1,0:T(8,128)(2,1)S(1)}, u32[]{:S(2)}, u32[]{:S(2)}) collective-permute-start(bf16[160,384]{1,0:T(8,128)(2,1)S(1)} %get-tuple-element.68), channel_id=1, source_target_pairs={{0,2},{1,3},{2,0},{3,1},{4,6},{5,7},{6,4},{7,5},{8,10},{9,11},{10,... | collective-permute-start | bytes 368648 | tf_op jit(solution)/shard_map/ppermute | solution.py:373
  57.1 3.1 %collective-permute-start.26 = (bf16[80,384]{1,0:T(8,128)(2,1)S(1)}, bf16[80,384]{1,0:T(8,128)(2,1)S(1)}, u32[]{:S(2)}, u32[]{:S(2)}) collective-permute-start(bf16[80,384]{1,0:T(8,128)(2,1)S(1)} %get-tuple-element.76), channel_id=1, source_target_pairs={{0,1},{1,0},{2,3},{3,2},{4,5},{5,4},{6,7},{7,6},{8,9},{9,8},{10,11... | collective-permute-start | bytes 184328 | tf_op jit(solution)/shard_map/ppermute | solution.py:373
  57.2 5.9 %collective-permute-start.27 = (bf16[80,384]{1,0:T(8,128)(2,1)S(1)}, bf16[80,384]{1,0:T(8,128)(2,1)S(1)}, u32[]{:S(2)}, u32[]{:S(2)}) collective-permute-start(bf16[80,384]{1,0:T(8,128)(2,1)S(1)} %get-tuple-element.77), channel_id=1, source_target_pairs={{0,2},{1,3},{2,0},{3,1},{4,6},{5,7},{6,4},{7,5},{8,10},{9,11},{10,... | collective-permute-start | bytes 184328 | tf_op jit(solution)/shard_map/ppermute | solution.py:373
  57.7 10.3 %collective-permute-start.21 = (bf16[160,384]{1,0:T(8,128)(2,1)S(1)}, bf16[160,384]{1,0:T(8,128)(2,1)S(1)}, u32[]{:S(2)}, u32[]{:S(2)}) collective-permute-start(bf16[160,384]{1,0:T(8,128)(2,1)S(1)} %get-tuple-element.69), channel_id=1, source_target_pairs={{0,3},{1,2},{2,1},{3,0},{4,7},{5,6},{6,5},{7,4},{8,11},{9,10},{10,... | collective-permute-start | bytes 368648 | tf_op jit(solution)/shard_map/ppermute | solution.py:373
  60.2 8.4 %collective-permute-start.15 = (bf16[160,384]{1,0:T(8,128)(2,1)S(1)}, bf16[160,384]{1,0:T(8,128)(2,1)S(1)}, u32[]{:S(2)}, u32[]{:S(2)}) collective-permute-start(bf16[160,384]{1,0:T(8,128)(2,1)S(1)} %get-tuple-element.62), channel_id=1, source_target_pairs={{0,4},{1,5},{2,6},{3,7},{4,0},{5,1},{6,2},{7,3},{8,12},{9,13},{10,... | collective-permute-start | bytes 368648 | tf_op jit(solution)/shard_map/ppermute | solution.py:373
  63.1 10.8 %collective-permute-start.16 = (bf16[160,384]{1,0:T(8,128)(2,1)S(1)}, bf16[160,384]{1,0:T(8,128)(2,1)S(1)}, u32[]{:S(2)}, u32[]{:S(2)}) collective-permute-start(bf16[160,384]{1,0:T(8,128)(2,1)S(1)} %get-tuple-element.63), channel_id=1, source_target_pairs={{0,5},{1,4},{2,7},{3,6},{4,1},{5,0},{6,3},{7,2},{8,13},{9,12},{10,... | collective-permute-start | bytes 368648 | tf_op jit(solution)/shard_map/ppermute | solution.py:373
  63.2 11.6 %collective-permute-start.17 = (bf16[160,384]{1,0:T(8,128)(2,1)S(1)}, bf16[160,384]{1,0:T(8,128)(2,1)S(1)}, u32[]{:S(2)}, u32[]{:S(2)}) collective-permute-start(bf16[160,384]{1,0:T(8,128)(2,1)S(1)} %get-tuple-element.64), channel_id=1, source_target_pairs={{0,6},{1,7},{2,4},{3,5},{4,2},{5,3},{6,0},{7,1},{8,14},{9,15},{10,... | collective-permute-start | bytes 368648 | tf_op jit(solution)/shard_map/ppermute | solution.py:373
  65.5 12.3 %copy-start.3 = (bf16[2,4,80,720]{3,2,1,0:T(8,128)(2,1)S(1)}, bf16[2,4,80,720]{3,2,1,0:T(8,128)(2,1)}, u32[]{:S(2)}) copy-start(bf16[2,4,80,720]{3,2,1,0:T(8,128)(2,1)} %alpha.5) | copy-start | bytes 2764804
  65.5 12.3 %copy-start.11 = (bf16[4,80,720]{2,1,0:T(8,128)(2,1)S(1)}, bf16[4,80,720]{2,1,0:T(8,128)(2,1)}, u32[]{:S(2)}) copy-start(bf16[4,80,720]{2,1,0:T(8,128)(2,1)} %static.3) | copy-start | bytes 1382404
  65.5 11.0 %collective-permute-start.18 = (bf16[160,384]{1,0:T(8,128)(2,1)S(1)}, bf16[160,384]{1,0:T(8,128)(2,1)S(1)}, u32[]{:S(2)}, u32[]{:S(2)}) collective-permute-start(bf16[160,384]{1,0:T(8,128)(2,1)S(1)} %get-tuple-element.65), channel_id=1, source_target_pairs={{0,7},{1,6},{2,5},{3,4},{4,3},{5,2},{6,1},{7,0},{8,15},{9,14},{10,... | collective-permute-start | bytes 368648 | tf_op jit(solution)/shard_map/ppermute | solution.py:373
  68.1 13.0 %collective-permute-start.28 = (bf16[80,384]{1,0:T(8,128)(2,1)S(1)}, bf16[80,384]{1,0:T(8,128)(2,1)S(1)}, u32[]{:S(2)}, u32[]{:S(2)}) collective-permute-start(bf16[80,384]{1,0:T(8,128)(2,1)S(1)} %get-tuple-element.78), channel_id=1, source_target_pairs={{0,3},{1,2},{2,1},{3,0},{4,7},{5,6},{6,5},{7,4},{8,11},{9,10},{10,... | collective-permute-start | bytes 184328 | tf_op jit(solution)/shard_map/ppermute | solution.py:373
  68.5 12.5 %collective-permute-start.22 = (bf16[80,384]{1,0:T(8,128)(2,1)S(1)}, bf16[80,384]{1,0:T(8,128)(2,1)S(1)}, u32[]{:S(2)}, u32[]{:S(2)}) collective-permute-start(bf16[80,384]{1,0:T(8,128)(2,1)S(1)} %get-tuple-element.71), channel_id=1, source_target_pairs={{0,4},{1,5},{2,6},{3,7},{4,0},{5,1},{6,2},{7,3},{8,12},{9,13},{10,... | collective-permute-start | bytes 184328 | tf_op jit(solution)/shard_map/ppermute | solution.py:373
  73.9 7.1 %collective-permute-start.23 = (bf16[80,384]{1,0:T(8,128)(2,1)S(1)}, bf16[80,384]{1,0:T(8,128)(2,1)S(1)}, u32[]{:S(2)}, u32[]{:S(2)}) collective-permute-start(bf16[80,384]{1,0:T(8,128)(2,1)S(1)} %get-tuple-element.72), channel_id=1, source_target_pairs={{0,5},{1,4},{2,7},{3,6},{4,1},{5,0},{6,3},{7,2},{8,13},{9,12},{10,... | collective-permute-start | bytes 184328 | tf_op jit(solution)/shard_map/ppermute | solution.py:373
  74.8 6.2 %collective-permute-start.24 = (bf16[80,384]{1,0:T(8,128)(2,1)S(1)}, bf16[80,384]{1,0:T(8,128)(2,1)S(1)}, u32[]{:S(2)}, u32[]{:S(2)}) collective-permute-start(bf16[80,384]{1,0:T(8,128)(2,1)S(1)} %get-tuple-element.73), channel_id=1, source_target_pairs={{0,6},{1,7},{2,4},{3,5},{4,2},{5,3},{6,0},{7,1},{8,14},{9,15},{10,... | collective-permute-start | bytes 184328 | tf_op jit(solution)/shard_map/ppermute | solution.py:373
  76.6 4.9 %collective-permute-start.25 = (bf16[80,384]{1,0:T(8,128)(2,1)S(1)}, bf16[80,384]{1,0:T(8,128)(2,1)S(1)}, u32[]{:S(2)}, u32[]{:S(2)}) collective-permute-start(bf16[80,384]{1,0:T(8,128)(2,1)S(1)} %get-tuple-element.74), channel_id=1, source_target_pairs={{0,7},{1,6},{2,5},{3,4},{4,3},{5,2},{6,1},{7,0},{8,15},{9,14},{10,... | collective-permute-start | bytes 184328 | tf_op jit(solution)/shard_map/ppermute | solution.py:373
  (16 other events, 67.1 us)

commit v2 on v1

--- a/solution.py
+++ b/solution.py
@@ -10,6 +10,7 @@
 
 
 F32 = jnp.float32
+VMEM_BYTES = 67043328
 BF16 = jnp.bfloat16
 VMEM = pl.BlockSpec(memory_space=pltpu.VMEM)
 SMEM = pl.BlockSpec(memory_space=pltpu.SMEM)
@@ -93,14 +94,13 @@
     ]
 
 
-def lon_kernel(plan, alpha, static, root, *refs):
+def lon_kernel(plan, alpha, static, root, lat, *refs):
     n = 2 * plan.bands
-    x_refs, (a_buf, s_buf, r_buf, packed, sems) = refs[:n], refs[n:]
+    x_refs, (lat_out, a_buf, s_buf, r_buf, packed, sems) = refs[:n], refs[n:]
     species, rows, extra, members = plan.species, plan.rows, plan.extra, plan.members
-    copies = [
-        pltpu.make_async_copy(src, dst, sems.at[i])
-        for i, (src, dst) in enumerate(((root, r_buf), (alpha, a_buf), (static, s_buf)))
-    ]
+    moves = [(root, r_buf)] + [(alpha.at[m], a_buf.at[m]) for m in range(members)]
+    moves += [(static, s_buf), (lat, lat_out)]
+    copies = [pltpu.make_async_copy(src, dst, sems.at[i]) for i, (src, dst) in enumerate(moves)]
     for copy in copies:
         copy.start()
     rank, me = lax.axis_index("mem"), lax.axis_index("band")
@@ -109,11 +109,12 @@
     select = one_hot(mine & (t < plan.count) & (rank % plan.copies == 0))
     for copy in copies:
         copy.wait()
-    fields = []
+    left = []
     for s in range(species):
-        short = dot(select, s_buf[s]).astype(BF16)
-        left = jnp.concatenate([a_buf[m, s] for m in range(members)] + [short], 0)
-        fields.append(dot(left, r_buf[...]))
+        left += [a_buf[m, s] for m in range(members)] + [dot(select, s_buf[s]).astype(BF16)]
+    y = dot(jnp.concatenate(left, 0), r_buf[...])
+    size = members * rows + extra
+    fields = [y[s * size : (s + 1) * size] for s in range(species)]
     for half in range(2):
         for b in range(plan.bands):
             at = (2 * b + half) * plan.width
@@ -124,7 +125,8 @@
             x_refs[own * plan.bands + k][...] = packed[half, me ^ k]
 
 
-def root_kernel(plan, root, w_ref):
+def root_kernel(plan, root, lat, w_ref, lat_t):
+    lat_t[...] = dot_nt(order_matrix(plan), lat[...]).astype(BF16)
     rank, me = lax.axis_index("mem"), lax.axis_index("band")
     side = plan.bands * plan.slot
     shape = (plan.lon, 2 * side)
@@ -136,46 +138,54 @@
     w_ref[...] = dot(root[...], pick).astype(BF16)
 
 
-def prep_kernel(plan, pert, std, lat, perts_p, perts_o, std_p, std_o, lat_k, lat_t, lat_s):
-    members, species, rows, total = plan.members, plan.species, plan.rows, plan.lat
-    rank, me = lax.axis_index("mem"), lax.axis_index("band")
+def prep_kernel(plan, own, pert, std, p_ref, s_ref):
+    rank = lax.axis_index("mem")
     for side in range(2):
         @pl.when(rank & 1 == side)
         def _():
-            for half, p_ref, s_ref in ((1 - side, perts_p, std_p), (side, perts_o, std_o)):
-                at = (half * plan.width, plan.width, plan.slot)
-                for m in range(members):
-                    pieces = [pert[m, s].astype(F32) for s in range(species)]
-                    p_ref[m] = pack(pieces, *at).astype(BF16)
-                s_ref[...] = 0.6 * pack([std[s] for s in range(species)], *at)
-    row = iota((total, total), 0)
-    order = one_hot(iota((total, total), 1) == (row // rows ^ me) * rows + row % rows)
-    lat_k[...] = dot_nt(lat[...], order).astype(BF16)
-    lat_t[...] = dot_nt(order, lat[...]).astype(BF16)
-    row = iota((plan.bands * plan.extra, total), 0)
+            half = side if own else 1 - side
+            at = (half * plan.width, plan.width, plan.slot)
+            for m in range(plan.members):
+                pieces = [pert[m, s].astype(F32) for s in range(plan.species)]
+                p_ref[m] = pack(pieces, *at).astype(BF16)
+            s_ref[...] = 0.6 * pack([std[s] for s in range(plan.species)], *at)
+
+
+def order_matrix(plan):
+    row = iota((plan.lat, plan.lat), 0)
+    source = (row // plan.rows ^ lax.axis_index("band")) * plan.rows + row % plan.rows
+    return one_hot(iota((plan.lat, plan.lat), 1) == source)
+
+
+def forward_kernel(plan, lat, lat_k, lat_s):
+    rank, me = lax.axis_index("mem"), lax.axis_index("band")
+    lat_k[...] = dot_nt(lat[...], order_matrix(plan)).astype(BF16)
+    shape = (plan.bands * plan.extra, plan.lat)
+    row = iota(shape, 0)
     t = row % plan.extra
-    source = (row // plan.extra ^ me) * rows + (rank // plan.copies) * plan.count + t
-    mine = iota((plan.bands * plan.extra, total), 1) == source
-    pick = one_hot(mine & (t < plan.count) & (rank % plan.copies == 0))
+    source = (row // plan.extra ^ me) * plan.rows + (rank // plan.copies) * plan.count + t
+    pick = one_hot((iota(shape, 1) == source) & (t < plan.count) & (rank % plan.copies == 0))
     lat_s[...] = dot_nt(lat[...], pick).astype(BF16)
 
 
-def normal_kernel(plan, error, jac, count, mask, h_p, h_o):
+def normal_kernel(plan, error, jac, count, mask, h_p, h_o, inverse):
     channels, species, rows, lon = jac.shape
     rank = lax.axis_index("mem")
     pairs = [(s, t) for s in range(species) for t in range(s, species)]
+    for c in range(channels):
+        inverse[c] = 1.0 / (error[c] * error[c])
     for r in range(0, rows, 8):
         n = min(8, rows - r)
         seen = count[r : r + n].astype(F32)
 
         def step(c, totals):
-            weight = mask[c, r : r + n].astype(F32) * (seen * (1.0 / (error[c] * error[c])))
+            weight = mask[c, r : r + n].astype(F32) * (seen * inverse[c])
             j = [jac[c, s, r : r + n].astype(F32) for s in range(species)]
             scaled = [weight * x for x in j]
             return tuple(total + scaled[s] * j[t] for total, (s, t) in zip(totals, pairs))
 
         zero = tuple(jnp.zeros((n, lon), F32) for _ in pairs)
-        sums = dict(zip(pairs, lax.fori_loop(0, channels, step, zero, unroll=2)))
+        sums = dict(zip(pairs, lax.fori_loop(0, channels, step, zero, unroll=8)))
         side = jnp.broadcast_to(rank & 1, (n, plan.width)) == 0
         for i, pair in enumerate(pairs):
             low, high = sums[pair][:, : plan.width], sums[pair][:, plan.width :]
@@ -245,33 +255,47 @@
             outs[late * plan.bands + k][at * rows : (at + 1) * rows, :] = y[k * rows : (k + 1) * rows]
 
 
-def product(plan, xs, w, fixed):
-    at = fixed * plan.slot
-    pieces = [x[:, at : at + plan.slot].astype(F32) for x in xs]
-    return dot_nt(jnp.concatenate(pieces, 1).astype(BF16), w[...])
+def product(plan, xs, w):
+    rows = []
+    for s in range(plan.species):
+        pieces = [x[:, s * plan.slot : (s + 1) * plan.slot].astype(F32) for x in xs]
+        rows.append(jnp.concatenate(pieces, 1).astype(BF16))
+    return dot_nt(jnp.concatenate(rows, 0), w[...])
+
+
+def finish(outs):
+    copies = [pltpu.make_async_copy(src, dst, sem) for src, dst, sem in outs]
+    for copy in copies:
+        copy.start()
+    return copies
 
 
 def early_kernel(plan, alpha, static, w, *refs):
-    xs, (grad_alpha, grad_static) = refs[:-2], refs[-2:]
-    rows, n = plan.rows, plan.members - plan.late
-    for fixed in range(plan.species):
-        @pl.when(pl.program_id(0) == fixed)
-        def _():
-            y = product(plan, xs, w, fixed)
-            for m in range(n):
-                grad_alpha[m, 0] = alpha[m, 0].astype(F32) + y[m * rows : (m + 1) * rows]
-            grad_static[0] = static[0].astype(F32) + y[n * rows :]
+    xs, (grad_alpha, grad_static, a_buf, s_buf, sems) = refs[:-5], refs[-5:]
+    rows, n, first = plan.rows, plan.members - plan.late, plan.late
+    y = product(plan, xs, w)
+    size, started = (n + 1) * rows, []
+    for s in range(plan.species):
+        for m in range(n):
+            a_buf[m, s] = alpha[first + m, s].astype(F32) + y[s * size + m * rows :][:rows]
+            started += finish([(a_buf.at[m, s], grad_alpha.at[first + m, s], sems.at[s, m])])
+        s_buf[s] = static[s].astype(F32) + y[s * size + n * rows :][:rows]
+        started += finish([(s_buf.at[s], grad_static.at[s], sems.at[s, n])])
+    for copy in started:
+        copy.wait()
 
 
 def late_kernel(plan, _, alpha, w, *refs):
-    xs, grad_alpha = refs[:-1], refs[-1]
-    rows = plan.rows
-    for fixed in range(plan.species):
-        @pl.when(pl.program_id(0) == fixed)
-        def _():
-            y = product(plan, xs, w, fixed)
-            for m in range(plan.late):
-                grad_alpha[m, 0] = alpha[m, 0].astype(F32) + y[m * rows : (m + 1) * rows]
+    xs, (grad_alpha, a_buf, sems) = refs[:-3], refs[-3:]
+    rows, n = plan.rows, plan.late
+    y = product(plan, xs, w)
+    started = []
+    for s in range(plan.species):
+        for m in range(n):
+            a_buf[m, s] = alpha[m, s].astype(F32) + y[(s * n + m) * rows :][:rows]
+            started += finish([(a_buf.at[m, s], grad_alpha.at[m, s], sems.at[s, m])])
+    for copy in started:
+        copy.wait()
 
 
 def shards(bands, ranks, *args):
@@ -295,15 +319,17 @@
         return jnp.pad(x, widths).reshape(shape)
 
     sent = struct((members * plan.rows + plan.extra, lanes), BF16)
-    got = call(
-        functools.partial(lon_kernel, plan), [sent] * (2 * bands),
-        alpha, static_ctl, lon_root, flops=10**9, spaces=[pl.ANY] * 3,
+    lat = pad_lat(lat_root, 0)
+    *got, lat = call(
+        functools.partial(lon_kernel, plan), [sent] * (2 * bands) + [struct(lat.shape, BF16)],
+        alpha, static_ctl, lon_root, lat, flops=10**9, spaces=[pltpu.HBM] * 4,
+        vmem=VMEM_BYTES - 2 * (2 * bands * math.prod(sent.shape) + math.prod(lat.shape)) - (3 << 17),
         scratch=[
             pltpu.VMEM(alpha.shape, BF16),
             pltpu.VMEM(static_ctl.shape, BF16),
             pltpu.VMEM(lon_root.shape, BF16),
             pltpu.VMEM((2, bands) + sent.shape, BF16),
-            pltpu.SemaphoreType.DMA((3,)),
+            pltpu.SemaphoreType.DMA((members + 3,)),
         ],
     )
     fields = [list(got[:bands]), list(got[bands:])]
@@ -313,20 +339,18 @@
     block = struct((plan.height, lanes), BF16)
     pert_shape = struct((members, plan.padded, lanes), BF16)
     std_shape = struct((plan.padded, lanes), F32)
-    outs = [
-        pert_shape, pert_shape, std_shape, std_shape,
-        struct((plan.padded, plan.lat), BF16),
-        struct((plan.lat, plan.padded), BF16),
-        struct((plan.padded, bands * plan.extra), BF16),
-    ]
-    perts_p, perts_o, std_p, std_o, lat_k, lat_t, lat_s = call(
-        functools.partial(prep_kernel, plan), outs,
-        pad_lat(perturbations, 2), pad_lat(static_std, 1), pad_lat(lat_root, 0),
-    )
+    pert, std = pad_lat(perturbations, 2), pad_lat(static_std, 1)
+    lat_k, lat_s = call(
+        functools.partial(forward_kernel, plan),
+        [struct((plan.padded, plan.lat), BF16), struct((plan.padded, bands * plan.extra), BF16)], lat,
+    )
+    perts_p, std_p = call(functools.partial(prep_kernel, plan, 0), [pert_shape, std_shape], pert, std)
+    perts_o, std_o = call(functools.partial(prep_kernel, plan, 1), [pert_shape, std_shape], pert, std)
     h_shape = struct((species * (species + 1) // 2, plan.pixel, plan.width), F32)
     h_p, h_o = call(
         functools.partial(normal_kernel, plan), [h_shape, h_shape],
         channel_error, jacobian, obs_count, channel_mask, smem=1,
+        scratch=[pltpu.SMEM(channel_error.shape, F32)],
     )
     h_got = send(h_p, "mem", 1)
     perts_got = send(perts_p, "mem", 1)
@@ -348,9 +372,10 @@
     (g,) = call(functools.partial(pixel_kernel, plan), [block], h_o, h_got, *parts)
     gs = [g] + [send(g, "mem", 2 * k) for k in range(1, plan.blocks)]
 
-    (w,) = call(
+    w, lat_t = call(
         functools.partial(root_kernel, plan),
-        [struct((plan.lon, 2 * bands * plan.slot), BF16)], lon_root, flops=10**9,
+        [struct((plan.lon, 2 * bands * plan.slot), BF16), struct((plan.lat, plan.padded), BF16)],
+        lon_root, lat, flops=10**9,
     )
     n_late = plan.late
     shapes = [struct(((members + 1 - n_late) * plan.rows, lanes), BF16)] * bands
@@ -365,11 +390,7 @@
             for k in range(bands):
                 x = got[late * bands + k]
                 if flip or k:
-                    swap = [
-                        (i * bands + j, (i ^ flip) * bands + (j ^ k))
-                        for i in range(ranks)
-                        for j in range(bands)
-                    ]
+                    swap = [(i * bands + j, (i ^ flip) * bands + (j ^ k)) for i in range(ranks) for j in range(bands)]
                     x = lax.ppermute(x, ("mem", "band"), swap)
                 backs[late, flip, k] = x
     early, last = [[backs[late, 1 - own, k] for own in range(2) for k in range(bands)] for late in range(2)]
@@ -377,26 +398,26 @@
     params = pltpu.CompilerParams(vmem_limit_bytes=24 << 20)
     cost = pl.CostEstimate(flops=10**9, bytes_accessed=10**7, transcendentals=0)
     n_early = members - n_late
-    any_space = pl.BlockSpec(memory_space=pl.ANY)
-
-    def block_of(n, first):
-        return pl.BlockSpec((n, 1, plan.rows, plan.lon), lambda s: (first, s, 0, 0))
-
-    static_block = pl.BlockSpec((1, plan.rows, plan.lon), lambda s: (s, 0, 0))
+    hbm = pl.BlockSpec(memory_space=pltpu.HBM)
+    tile = (species, plan.rows, plan.lon)
     grad_alpha, grad_static = pl.pallas_call(
         functools.partial(early_kernel, plan),
-        grid=(species,),
         out_shape=[struct(alpha.shape, F32), struct(static_ctl.shape, F32)],
-        in_specs=[block_of(n_early, 1), static_block] + [VMEM] * (1 + 2 * bands),
-        out_specs=[block_of(n_early, 1), static_block],
+        in_specs=[VMEM] * (3 + 2 * bands),
+        out_specs=[hbm, hbm],
+        scratch_shapes=[
+            pltpu.VMEM((n_early,) + tile, F32),
+            pltpu.VMEM(tile, F32),
+            pltpu.SemaphoreType.DMA((species, n_early + 1)),
+        ],
         compiler_params=params, cost_estimate=cost, name="early",
     )(alpha, static_ctl, w, *early)
     grad_alpha = pl.pallas_call(
         functools.partial(late_kernel, plan),
-        grid=(species,),
         out_shape=struct(alpha.shape, F32),
-        in_specs=[any_space, block_of(n_late, 0)] + [VMEM] * (1 + 2 * bands),
-        out_specs=block_of(n_late, 0),
+        in_specs=[hbm] + [VMEM] * (2 + 2 * bands),
+        out_specs=hbm,
+        scratch_shapes=[pltpu.VMEM((n_late,) + tile, F32), pltpu.SemaphoreType.DMA((species, n_late))],
         input_output_aliases={0: 0},
         compiler_params=params, cost_estimate=cost, name="late",
     )(grad_alpha, alpha, w, *last)

time: 84.6 us -> 77.9 us (0.921)
  Pallas kernels: 23.3 us -> 19 us
  local copies, waits for them, and re-layouts: 8.78 us -> 4.62 us
  waiting for transfers between devices: 19.3 us -> 20.9 us
    unnamed x40 -> x30, local copies, waits for them, and re-layouts: 8.78 us -> 4.62 us
    pallas_call x10 -> x12, Pallas kernels: 17.3 us -> 15.1 us  [call(): pl.pallas_call(kernel, out_shape=outs, in_specs=[SMEM] * smem + [VMEM] *...]
    pallas_call x2, Pallas kernels: 6.02 us -> 3.98 us  [the longest x1 2.37 us: shards(): pl.pallas_call(functools.partial(early_kernel, plan), out_shape=[struct(a...]
    ppermute x14, waiting for transfers between devices: 5.8 us -> 7.71 us  [shards(): x = lax.ppermute(x, ('mem', 'band'), swap)]
  transfers between devices with their start and end apart: 29 -> 29, of which waited for: 7 -> 10; matrix products, arithmetic and copies ran while one was open for 4% -> 6% of each run, Pallas kernels for 19% -> 15%
where the time goes in v2:
time: 77.9 us; the launch traced here: 77.7 us
  starting transfers between devices  32.1 us (41%)
  waiting for transfers between devices  20.9 us (27%)
  Pallas kernels  19 us (24%)
  local copies, waits for them, and re-layouts  4.62 us (6%)
  between operations  1.11 us (1%)
    ppermute x15, starting transfers between devices, send(): return lax.ppermute(x, axis, [(i, i ^ k) for i in range(n)])  17.4 us
    pallas_call x12, Pallas kernels, call(): pl.pallas_call(kernel, out_shape=outs, in_specs=[SMEM] * smem + [VMEM] *...  15.1 us
    ppermute x14, starting transfers between devices, shards(): x = lax.ppermute(x, ('mem', 'band'), swap)  14.7 us
    ppermute x15, waiting for transfers between devices, send(): return lax.ppermute(x, axis, [(i, i ^ k) for i in range(n)])  13.1 us
    ppermute x14, waiting for transfers between devices, shards(): x = lax.ppermute(x, ('mem', 'band'), swap)  7.71 us
    unnamed x30, local copies, waits for them, and re-layouts  4.62 us
    pallas_call x1, Pallas kernels, shards(): pl.pallas_call(functools.partial(early_kernel, plan), out_shape=[struct(a...  2.37 us
    pallas_call x1, Pallas kernels, shards(): pl.pallas_call(functools.partial(late_kernel, plan), out_shape=struct(alp...  1.61 us
  transfers between devices with their start and end apart: 29, of which 10 were waited for; matrix products, arithmetic and copies ran while one was open for 6% of the time, Pallas kernels for 15%

profile of v2, /device:TPU:0, one launch (start us, length us, event | category | flops | bytes accessed | tf_op | source)
XLA Modules:
  0.0 77.7 jit_solution(8463860641221453887)
XLA Ops:
  0.6 4.3 %shard_map.122 = (bf16[176,384]{1,0:T(8,128)(2,1)}, bf16[176,384]{1,0:T(8,128)(2,1)}, bf16[176,384]{1,0:T(8,128)(2,1)}, bf16[176,384]{1,0:T(8,128)(2,1)}, bf16[1...) custom-call(bf16[2,4,80,720]{3,2,1,0:T(8,128)(2,1)} %alpha.5, ...), custom_call_target="tpu_custom_call" | custom-call | flops 1000000000 | bytes 3910144 | tf_op jit(solution)/shard_map/pallas_call | solution.py:30
  5.5 2.6 %collective-permute-start.6 = (bf16[176,384]{1,0:T(8,128)(2,1)}, bf16[176,384]{1,0:T(8,128)(2,1)S(1)}, u32[]{:S(2)}, u32[]{:S(2)}) collective-permute-start(bf16[176,384]{1,0:T(8,128)(2,1)} %get-tuple-element.60), channel_id=1, source_target_pairs={{0,2},{1,3},{2,0},{3,1},{4,6},{5,7},{6,4},{7,5},{8,10},{9,11},{10,... | collective-permute-start | bytes 405512 | tf_op jit(solution)/shard_map/ppermute | solution.py:309
  8.1 2.6 %copy.14.pert = bf16[2,4,320,180]{3,2,1,0:T(8,128)(2,1)S(1)} copy(bf16[2,4,320,180]{2,1,3,0:T(4,128)(2,1)} %param.13) | data formatting | bytes 1843200 | tf_op args[2]
  10.7 2.0 %copy.15.std = f32[4,320,180]{2,1,0:T(8,128)S(1)} copy(f32[4,320,180]{1,0,2:T(4,128)} %param.14) | data formatting | bytes 1843200 | tf_op args[3]
  14.0 1.1 %collective-permute-done.7.refs_3_ = bf16[176,384]{1,0:T(8,128)(2,1)S(1)} collective-permute-done((bf16[176,384]{1,0:T(8,128)(2,1)}, bf16[176,384]{1,0:T(8,128)(2,1)S(1)}, u32[]{:S(2)}, u32[]{:S(2)}) %collective-permute-start.7) | collective-permute-done | bytes 135200 | tf_op jit(solution)/shard_map/ppermute | solution.py:309
  15.1 1.1 %shard_map.129 = bf16[320,384]{1,0:T(8,128)(2,1)S(1)} custom-call(s32[16]{0:T(128)S(1)} %copy-done.6, bf16[320,320]{1,0:T(8,128)(2,1)S(1)} %get-tuple-element.50.lat_k, bf16[320,64]{1,0:T(8,128)(2,1)S(1)} %get-tuple-element.51.lat_s, bf16[2,320,384]{2,1,0:T(8,128)(2,1)S(1)} %get-tuple-element.46.pert, f32[320,384]{1,0:T(8,128)S(1)} %get-tuple-element.57.std, ...), custom_call_target="tpu_custom_call" | custom-call | flops 100000000 | bytes 2015296 | tf_op jit(solution)/shard_map/pallas_call | solution.py:30
  16.2 1.6 %collective-permute-start.8 = (bf16[320,384]{1,0:T(8,128)(2,1)S(1)}, bf16[320,384]{1,0:T(8,128)(2,1)S(1)}, u32[]{:S(2)}, u32[]{:S(2)}) collective-permute-start(bf16[320,384]{1,0:T(8,128)(2,1)S(1)} %shard_map.129), channel_id=1, source_target_pairs={{0,4},{4,0},{8,12},{12,8},{16,20},{20,16},{24,28},{28,24},{1,5},{5... | collective-permute-start | bytes 737288 | tf_op jit(solution)/shard_map/ppermute | solution.py:309
  18.3 1.5 %collective-permute-start.3 = (bf16[176,384]{1,0:T(8,128)(2,1)S(1)}, bf16[176,384]{1,0:T(8,128)(2,1)S(1)}, u32[]{:S(2)}, u32[]{:S(2)}) collective-permute-start(bf16[176,384]{1,0:T(8,128)(2,1)S(1)} %copy-done.12), channel_id=1, source_target_pairs={{0,2},{1,3},{2,0},{3,1},{4,6},{5,7},{6,4},{7,5},{8,10},{9,11},{10,... | collective-permute-start | bytes 405512 | tf_op jit(solution)/shard_map/ppermute | solution.py:309
  19.9 2.8 %shard_map.126 = (f32[10,40,90]{2,1,0:T(8,128)S(1)}, f32[10,40,90]{2,1,0:T(8,128)S(1)}) custom-call(f32[32]{0:T(128)S(1)} %copy-done.7, bf16[32,4,40,180]{3,2,1,0:T(8,128)(2,1)S(1)} %copy-done, s32[40,180]{1,0:T(8,128)S(1)} %copy-done.5, s32[32,40,180]{2,1,0:T(8,128)S(1)} %copy-done.1), custom_call_target="tpu_custom_call" | custom-call | flops 100000000 | bytes 3081728 | tf_op jit(solution)/shard_map/pallas_call | solution.py:30
  22.7 1.6 %collective-permute-start.1 = (f32[10,40,90]{2,1,0:T(8,128)S(1)}, f32[10,40,90]{2,1,0:T(8,128)S(1)}, u32[]{:S(2)}, u32[]{:S(2)}) collective-permute-start(f32[10,40,90]{2,1,0:T(8,128)S(1)} %get-tuple-element.49), channel_id=1, source_target_pairs={{0,4},{4,0},{8,12},{12,8},{16,20},{20,16},{24,28},{28,24},{1,5},{5... | collective-permute-start | bytes 432008 | tf_op jit(solution)/shard_map/ppermute | solution.py:309
  24.8 1.4 %collective-permute-done.4.refs_3_ = bf16[176,384]{1,0:T(8,128)(2,1)S(1)} collective-permute-done((bf16[176,384]{1,0:T(8,128)(2,1)S(1)}, bf16[176,384]{1,0:T(8,128)(2,1)S(1)}, u32[]{:S(2)}, u32[]{:S(2)}) %collective-permute-start.4) | collective-permute-done | bytes 135200 | tf_op jit(solution)/shard_map/ppermute | solution.py:309
  26.2 1.1 %shard_map.128.own = f32[320,384]{1,0:T(8,128)S(1)} custom-call(s32[16]{0:T(128)S(1)} %copy-done.6, bf16[320,320]{1,0:T(8,128)(2,1)S(1)} %get-tuple-element.50.lat_k, bf16[320,64]{1,0:T(8,128)(2,1)S(1)} %get-tuple-element.51.lat_s, bf16[2,320,384]{2,1,0:T(8,128)(2,1)S(1)} %get-tuple-element.52.pert, f32[320,384]{1,0:T(8,128)S(1)} %get-tuple-element.47.std, ...), custom_call_target="tpu_custom_call" | custom-call | flops 100000000 | bytes 2261056 | tf_op jit(solution)/shard_map/pallas_call | solution.py:30
  27.4 1.5 %collective-permute-start.9 = (bf16[80,384]{1,0:T(8,128)(2,1)S(1)}, bf16[80,384]{1,0:T(8,128)(2,1)S(1)}, u32[]{:S(2)}, u32[]{:S(2)}) collective-permute-start(bf16[80,384]{1,0:T(8,128)(2,1)S(1)} %get-tuple-element.63), channel_id=1, source_target_pairs={{0,8},{4,12},{8,0},{12,4},{16,24},{20,28},{24,16},{28,20},{1,9},{5... | collective-permute-start | bytes 184328 | tf_op jit(solution)/shard_map/ppermute | solution.py:309
  28.9 2.6 %collective-permute-start.10 = (bf16[80,384]{1,0:T(8,128)(2,1)S(1)}, bf16[80,384]{1,0:T(8,128)(2,1)S(1)}, u32[]{:S(2)}, u32[]{:S(2)}) collective-permute-start(bf16[80,384]{1,0:T(8,128)(2,1)S(1)} %get-tuple-element.64), channel_id=1, source_target_pairs={{0,16},{4,20},{8,24},{12,28},{16,0},{20,4},{24,8},{28,12},{1,17},{... | collective-permute-start | bytes 184328 | tf_op jit(solution)/shard_map/ppermute | solution.py:309
  31.9 7.3 %collective-permute-done.1.h_got = f32[10,40,90]{2,1,0:T(8,128)S(1)} collective-permute-done((f32[10,40,90]{2,1,0:T(8,128)S(1)}, f32[10,40,90]{2,1,0:T(8,128)S(1)}, u32[]{:S(2)}, u32[]{:S(2)}) %collective-permute-start.1) | collective-permute-done | bytes 144032 | tf_op jit(solution)/shard_map/ppermute | solution.py:309
  39.6 3.9 %collective-permute-start.14 = (bf16[80,384]{1,0:T(8,128)(2,1)S(1)}, bf16[80,384]{1,0:T(8,128)(2,1)S(1)}, u32[]{:S(2)}, u32[]{:S(2)}) collective-permute-start(bf16[80,384]{1,0:T(8,128)(2,1)S(1)} %shard_map.131.refs_0_), channel_id=1, source_target_pairs={{0,24},{4,28},{8,16},{12,20},{16,8},{20,12},{24,0},{28,4},{1,25},{... | collective-permute-start | bytes 184328 | tf_op jit(solution)/shard_map/ppermute | solution.py:309
  44.1 1.3 %shard_map.123 = (bf16[720,768]{1,0:T(8,128)(2,1)S(1)}, bf16[320,320]{1,0:T(8,128)(2,1)S(1)}) custom-call(bf16[720,720]{1,0:T(8,128)(2,1)S(1)} %copy-done.8, bf16[320,320]{1,0:T(8,128)(2,1)S(1)} %copy-done.10), custom_call_target="tpu_custom_call" | custom-call | flops 1000000000 | bytes 2552320 | tf_op jit(solution)/shard_map/pallas_call | solution.py:30
  46.3 2.3 %collective-permute-done.13.refs_2_ = bf16[80,384]{1,0:T(8,128)(2,1)S(1)} collective-permute-done((bf16[80,384]{1,0:T(8,128)(2,1)S(1)}, bf16[80,384]{1,0:T(8,128)(2,1)S(1)}, u32[]{:S(2)}, u32[]{:S(2)}) %collective-permute-start.13) | collective-permute-done | bytes 61472 | tf_op jit(solution)/shard_map/ppermute | solution.py:309
  48.6 1.2 %shard_map.133 = (bf16[160,384]{1,0:T(8,128)(2,1)S(1)}, bf16[160,384]{1,0:T(8,128)(2,1)S(1)}, bf16[160,384]{1,0:T(8,128)(2,1)S(1)}, bf16[160,384]{1,0:T(8,128)(2...) custom-call(s32[16]{0:T(128)S(1)} %copy-done.6, ...), custom_call_target="tpu_custom_call" | custom-call | flops 100000000 | bytes 2170944 | tf_op jit(solution)/shard_map/pallas_call | solution.py:30
  49.9 1.6 %collective-permute-start.20 = (bf16[160,384]{1,0:T(8,128)(2,1)S(1)}, bf16[160,384]{1,0:T(8,128)(2,1)S(1)}, u32[]{:S(2)}, u32[]{:S(2)}) collective-permute-start(bf16[160,384]{1,0:T(8,128)(2,1)S(1)} %get-tuple-element.72), channel_id=1, source_target_pairs={{0,2},{1,3},{2,0},{3,1},{4,6},{5,7},{6,4},{7,5},{8,10},{9,11},{10,... | collective-permute-start | bytes 368648 | tf_op jit(solution)/shard_map/ppermute | solution.py:394
  52.2 1.2 %collective-permute-start.21 = (bf16[160,384]{1,0:T(8,128)(2,1)S(1)}, bf16[160,384]{1,0:T(8,128)(2,1)S(1)}, u32[]{:S(2)}, u32[]{:S(2)}) collective-permute-start(bf16[160,384]{1,0:T(8,128)(2,1)S(1)} %get-tuple-element.73), channel_id=1, source_target_pairs={{0,3},{1,2},{2,1},{3,0},{4,7},{5,6},{6,5},{7,4},{8,11},{9,10},{10,... | collective-permute-start | bytes 368648 | tf_op jit(solution)/shard_map/ppermute | solution.py:394
  53.4 1.2 %shard_map.132 = (bf16[160,384]{1,0:T(8,128)(2,1)S(1)}, bf16[160,384]{1,0:T(8,128)(2,1)S(1)}, bf16[160,384]{1,0:T(8,128)(2,1)S(1)}, bf16[160,384]{1,0:T(8,128)(2...) custom-call(s32[16]{0:T(128)S(1)} %copy-done.6, ...), custom_call_target="tpu_custom_call" | custom-call | flops 100000000 | bytes 2170944 | tf_op jit(solution)/shard_map/pallas_call | solution.py:30
  54.6 1.6 %collective-permute-start.15 = (bf16[160,384]{1,0:T(8,128)(2,1)S(1)}, bf16[160,384]{1,0:T(8,128)(2,1)S(1)}, u32[]{:S(2)}, u32[]{:S(2)}) collective-permute-start(bf16[160,384]{1,0:T(8,128)(2,1)S(1)} %get-tuple-element.66), channel_id=1, source_target_pairs={{0,4},{1,5},{2,6},{3,7},{4,0},{5,1},{6,2},{7,3},{8,12},{9,13},{10,... | collective-permute-start | bytes 368648 | tf_op jit(solution)/shard_map/ppermute | solution.py:394
  56.2 1.3 %collective-permute-done.27.refs_6_ = bf16[80,384]{1,0:T(8,128)(2,1)S(1)} collective-permute-done((bf16[80,384]{1,0:T(8,128)(2,1)S(1)}, bf16[80,384]{1,0:T(8,128)(2,1)S(1)}, u32[]{:S(2)}, u32[]{:S(2)}) %collective-permute-start.27) | collective-permute-done | bytes 61472 | tf_op jit(solution)/shard_map/ppermute | solution.py:394
  57.7 2.3 %collective-permute-start.17 = (bf16[160,384]{1,0:T(8,128)(2,1)S(1)}, bf16[160,384]{1,0:T(8,128)(2,1)S(1)}, u32[]{:S(2)}, u32[]{:S(2)}) collective-permute-start(bf16[160,384]{1,0:T(8,128)(2,1)S(1)} %get-tuple-element.68), channel_id=1, source_target_pairs={{0,6},{1,7},{2,4},{3,5},{4,2},{5,3},{6,0},{7,1},{8,14},{9,15},{10,... | collective-permute-start | bytes 368648 | tf_op jit(solution)/shard_map/ppermute | solution.py:394
  60.0 1.4 %collective-permute-start.18 = (bf16[160,384]{1,0:T(8,128)(2,1)S(1)}, bf16[160,384]{1,0:T(8,128)(2,1)S(1)}, u32[]{:S(2)}, u32[]{:S(2)}) collective-permute-start(bf16[160,384]{1,0:T(8,128)(2,1)S(1)} %get-tuple-element.69), channel_id=1, source_target_pairs={{0,7},{1,6},{2,5},{3,4},{4,3},{5,2},{6,1},{7,0},{8,15},{9,14},{10,... | collective-permute-start | bytes 368648 | tf_op jit(solution)/shard_map/ppermute | solution.py:394
  61.8 1.4 %collective-permute-start.22 = (bf16[80,384]{1,0:T(8,128)(2,1)S(1)}, bf16[80,384]{1,0:T(8,128)(2,1)S(1)}, u32[]{:S(2)}, u32[]{:S(2)}) collective-permute-start(bf16[80,384]{1,0:T(8,128)(2,1)S(1)} %get-tuple-element.75), channel_id=1, source_target_pairs={{0,4},{1,5},{2,6},{3,7},{4,0},{5,1},{6,2},{7,3},{8,12},{9,13},{10,... | collective-permute-start | bytes 184328 | tf_op jit(solution)/shard_map/ppermute | solution.py:394
  63.2 5.1 %collective-permute-done.16.refs_1_ = bf16[160,384]{1,0:T(8,128)(2,1)S(1)} collective-permute-done((bf16[160,384]{1,0:T(8,128)(2,1)S(1)}, bf16[160,384]{1,0:T(8,128)(2,1)S(1)}, u32[]{:S(2)}, u32[]{:S(2)}) %collective-permute-start.16) | collective-permute-done | bytes 122912 | tf_op jit(solution)/shard_map/ppermute | solution.py:394
  69.3 1.7 %collective-permute-start.24 = (bf16[80,384]{1,0:T(8,128)(2,1)S(1)}, bf16[80,384]{1,0:T(8,128)(2,1)S(1)}, u32[]{:S(2)}, u32[]{:S(2)}) collective-permute-start(bf16[80,384]{1,0:T(8,128)(2,1)S(1)} %get-tuple-element.77), channel_id=1, source_target_pairs={{0,6},{1,7},{2,4},{3,5},{4,2},{5,3},{6,0},{7,1},{8,14},{9,15},{10,... | collective-permute-start | bytes 184328 | tf_op jit(solution)/shard_map/ppermute | solution.py:394
  71.0 1.3 %collective-permute-start.25 = (bf16[80,384]{1,0:T(8,128)(2,1)S(1)}, bf16[80,384]{1,0:T(8,128)(2,1)S(1)}, u32[]{:S(2)}, u32[]{:S(2)}) collective-permute-start(bf16[80,384]{1,0:T(8,128)(2,1)S(1)} %get-tuple-element.78), channel_id=1, source_target_pairs={{0,7},{1,6},{2,5},{3,4},{4,3},{5,2},{6,1},{7,0},{8,15},{9,14},{10,... | collective-permute-start | bytes 184328 | tf_op jit(solution)/shard_map/ppermute | solution.py:394
  72.3 2.4 %early.1 = (f32[2,4,80,720]{3,2,1,0:T(8,128)}, f32[4,80,720]{2,1,0:T(8,128)}) custom-call(bf16[2,4,80,720]{3,2,1,0:T(8,128)(2,1)S(1)} %copy-done.2, bf16[4,80,720]{2,1,0:T(8,128)(2,1)S(1)} %copy-done.9, bf16[720,768]{1,0:T(8,128)(2,1)S(1)} %get-tuple-element.44.w, bf16[160,384]{1,0:T(8,128)(2,1)S(1)} %collective-permute-done.15.refs_0_, ...), custom_call_target="tpu_custom_call" | custom-call | flops 1000000000 | bytes 10000000 | tf_op jit(solution)/shard_map/early/pallas_call | solution.py:403
  75.9 1.6 %late.1 = f32[2,4,80,720]{3,2,1,0:T(8,128)} custom-call(f32[2,4,80,720]{3,2,1,0:T(8,128)} %get-tuple-element.74._, bf16[2,4,80,720]{3,2,1,0:T(8,128)(2,1)S(1)} %copy-done.2, bf16[720,768]{1,0:T(8,128)(2,1)S(1)} %get-tuple-element.44.w, bf16[80,384]{1,0:T(8,128)(2,1)S(1)} %collective-permute-done.22.refs_0_, ...), custom_call_target="tpu_custom_call", output_to_operand_aliasing={{}: (0, {})} | custom-call | flops 1000000000 | bytes 10000000 | tf_op jit(solution)/shard_map/late/pallas_call | solution.py:415
  (70 shorter events, 8.7 us)
Async XLA Ops:
  4.9 9.0 %collective-permute-start.5 = (bf16[176,384]{1,0:T(8,128)(2,1)}, bf16[176,384]{1,0:T(8,128)(2,1)S(1)}, u32[]{:S(2)}, u32[]{:S(2)}) collective-permute-start(bf16[176,384]{1,0:T(8,128)(2,1)} %get-tuple-element.59), channel_id=1, source_target_pairs={{0,1},{1,0},{2,3},{3,2},{4,5},{5,4},{6,7},{7,6},{8,9},{9,8},{10,11... | collective-permute-start | bytes 405512 | tf_op jit(solution)/shard_map/ppermute | solution.py:309
  5.5 8.5 %collective-permute-start.6 = (bf16[176,384]{1,0:T(8,128)(2,1)}, bf16[176,384]{1,0:T(8,128)(2,1)S(1)}, u32[]{:S(2)}, u32[]{:S(2)}) collective-permute-start(bf16[176,384]{1,0:T(8,128)(2,1)} %get-tuple-element.60), channel_id=1, source_target_pairs={{0,2},{1,3},{2,0},{3,1},{4,6},{5,7},{6,4},{7,5},{8,10},{9,11},{10,... | collective-permute-start | bytes 405512 | tf_op jit(solution)/shard_map/ppermute | solution.py:309
  8.0 7.0 %collective-permute-start.7 = (bf16[176,384]{1,0:T(8,128)(2,1)}, bf16[176,384]{1,0:T(8,128)(2,1)S(1)}, u32[]{:S(2)}, u32[]{:S(2)}) collective-permute-start(bf16[176,384]{1,0:T(8,128)(2,1)} %get-tuple-element.61), channel_id=1, source_target_pairs={{0,3},{1,2},{2,1},{3,0},{4,7},{5,6},{6,5},{7,4},{8,11},{9,10},{10,... | collective-permute-start | bytes 405512 | tf_op jit(solution)/shard_map/ppermute | solution.py:309
  16.2 11.1 %collective-permute-start.8 = (bf16[320,384]{1,0:T(8,128)(2,1)S(1)}, bf16[320,384]{1,0:T(8,128)(2,1)S(1)}, u32[]{:S(2)}, u32[]{:S(2)}) collective-permute-start(bf16[320,384]{1,0:T(8,128)(2,1)S(1)} %shard_map.129), channel_id=1, source_target_pairs={{0,4},{4,0},{8,12},{12,8},{16,20},{20,16},{24,28},{28,24},{1,5},{5... | collective-permute-start | bytes 737288 | tf_op jit(solution)/shard_map/ppermute | solution.py:309
  17.8 5.0 %collective-permute-start.2 = (bf16[176,384]{1,0:T(8,128)(2,1)S(1)}, bf16[176,384]{1,0:T(8,128)(2,1)S(1)}, u32[]{:S(2)}, u32[]{:S(2)}) collective-permute-start(bf16[176,384]{1,0:T(8,128)(2,1)S(1)} %copy-done.13), channel_id=1, source_target_pairs={{0,1},{1,0},{2,3},{3,2},{4,5},{5,4},{6,7},{7,6},{8,9},{9,8},{10,11... | collective-permute-start | bytes 405512 | tf_op jit(solution)/shard_map/ppermute | solution.py:309
  17.8 34.3 %collective-permute-start = (bf16[2,320,384]{2,1,0:T(8,128)(2,1)S(1)}, bf16[2,320,384]{2,1,0:T(8,128)(2,1)S(1)}, u32[]{:S(2)}, u32[]{:S(2)}) collective-permute-start(bf16[2,320,384]{2,1,0:T(8,128)(2,1)S(1)} %get-tuple-element.46.pert), channel_id=1, source_target_pairs={{0,4},{4,0},{8,12},{12,8},{16,20},{20,16},{24,28},{28,24},{1,5},{5... | collective-permute-start | bytes 1474568 | tf_op jit(solution)/shard_map/ppermute | solution.py:309
  18.3 6.5 %collective-permute-start.3 = (bf16[176,384]{1,0:T(8,128)(2,1)S(1)}, bf16[176,384]{1,0:T(8,128)(2,1)S(1)}, u32[]{:S(2)}, u32[]{:S(2)}) collective-permute-start(bf16[176,384]{1,0:T(8,128)(2,1)S(1)} %copy-done.12), channel_id=1, source_target_pairs={{0,2},{1,3},{2,0},{3,1},{4,6},{5,7},{6,4},{7,5},{8,10},{9,11},{10,... | collective-permute-start | bytes 405512 | tf_op jit(solution)/shard_map/ppermute | solution.py:309
  19.8 6.3 %collective-permute-start.4 = (bf16[176,384]{1,0:T(8,128)(2,1)S(1)}, bf16[176,384]{1,0:T(8,128)(2,1)S(1)}, u32[]{:S(2)}, u32[]{:S(2)}) collective-permute-start(bf16[176,384]{1,0:T(8,128)(2,1)S(1)} %copy-done.11), channel_id=1, source_target_pairs={{0,3},{1,2},{2,1},{3,0},{4,7},{5,6},{6,5},{7,4},{8,11},{9,10},{10,... | collective-permute-start | bytes 405512 | tf_op jit(solution)/shard_map/ppermute | solution.py:309
  22.7 16.4 %collective-permute-start.1 = (f32[10,40,90]{2,1,0:T(8,128)S(1)}, f32[10,40,90]{2,1,0:T(8,128)S(1)}, u32[]{:S(2)}, u32[]{:S(2)}) collective-permute-start(f32[10,40,90]{2,1,0:T(8,128)S(1)} %get-tuple-element.49), channel_id=1, source_target_pairs={{0,4},{4,0},{8,12},{12,8},{16,20},{20,16},{24,28},{28,24},{1,5},{5... | collective-permute-start | bytes 432008 | tf_op jit(solution)/shard_map/ppermute | solution.py:309
  27.3 16.8 %copy-start.8 = (bf16[720,720]{1,0:T(8,128)(2,1)S(1)}, bf16[720,720]{1,0:T(8,128)(2,1)}, u32[]{:S(2)}) copy-start(bf16[720,720]{1,0:T(8,128)(2,1)} %root.3) | copy-start | bytes 3110404
  27.4 11.8 %collective-permute-start.9 = (bf16[80,384]{1,0:T(8,128)(2,1)S(1)}, bf16[80,384]{1,0:T(8,128)(2,1)S(1)}, u32[]{:S(2)}, u32[]{:S(2)}) collective-permute-start(bf16[80,384]{1,0:T(8,128)(2,1)S(1)} %get-tuple-element.63), channel_id=1, source_target_pairs={{0,8},{4,12},{8,0},{12,4},{16,24},{20,28},{24,16},{28,20},{1,9},{5... | collective-permute-start | bytes 184328 | tf_op jit(solution)/shard_map/ppermute | solution.py:309
  28.9 10.2 %collective-permute-start.10 = (bf16[80,384]{1,0:T(8,128)(2,1)S(1)}, bf16[80,384]{1,0:T(8,128)(2,1)S(1)}, u32[]{:S(2)}, u32[]{:S(2)}) collective-permute-start(bf16[80,384]{1,0:T(8,128)(2,1)S(1)} %get-tuple-element.64), channel_id=1, source_target_pairs={{0,16},{4,20},{8,24},{12,28},{16,0},{20,4},{24,8},{28,12},{1,17},{... | collective-permute-start | bytes 184328 | tf_op jit(solution)/shard_map/ppermute | solution.py:309
  31.5 7.6 %collective-permute-start.11 = (bf16[80,384]{1,0:T(8,128)(2,1)S(1)}, bf16[80,384]{1,0:T(8,128)(2,1)S(1)}, u32[]{:S(2)}, u32[]{:S(2)}) collective-permute-start(bf16[80,384]{1,0:T(8,128)(2,1)S(1)} %get-tuple-element.65), channel_id=1, source_target_pairs={{0,24},{4,28},{8,16},{12,20},{16,8},{20,12},{24,0},{28,4},{1,25},{... | collective-permute-start | bytes 184328 | tf_op jit(solution)/shard_map/ppermute | solution.py:309
  39.6 6.7 %collective-permute-start.14 = (bf16[80,384]{1,0:T(8,128)(2,1)S(1)}, bf16[80,384]{1,0:T(8,128)(2,1)S(1)}, u32[]{:S(2)}, u32[]{:S(2)}) collective-permute-start(bf16[80,384]{1,0:T(8,128)(2,1)S(1)} %shard_map.131.refs_0_), channel_id=1, source_target_pairs={{0,24},{4,28},{8,16},{12,20},{16,8},{20,12},{24,0},{28,4},{1,25},{... | collective-permute-start | bytes 184328 | tf_op jit(solution)/shard_map/ppermute | solution.py:309
  43.5 5.1 %collective-permute-start.13 = (bf16[80,384]{1,0:T(8,128)(2,1)S(1)}, bf16[80,384]{1,0:T(8,128)(2,1)S(1)}, u32[]{:S(2)}, u32[]{:S(2)}) collective-permute-start(bf16[80,384]{1,0:T(8,128)(2,1)S(1)} %shard_map.131.refs_0_), channel_id=1, source_target_pairs={{0,16},{4,20},{8,24},{12,28},{16,0},{20,4},{24,8},{28,12},{1,17},{... | collective-permute-start | bytes 184328 | tf_op jit(solution)/shard_map/ppermute | solution.py:309
  43.5 5.1 %collective-permute-start.12 = (bf16[80,384]{1,0:T(8,128)(2,1)S(1)}, bf16[80,384]{1,0:T(8,128)(2,1)S(1)}, u32[]{:S(2)}, u32[]{:S(2)}) collective-permute-start(bf16[80,384]{1,0:T(8,128)(2,1)S(1)} %shard_map.131.refs_0_), channel_id=1, source_target_pairs={{0,8},{4,12},{8,0},{12,4},{16,24},{20,28},{24,16},{28,20},{1,9},{5... | collective-permute-start | bytes 184328 | tf_op jit(solution)/shard_map/ppermute | solution.py:309
  48.6 23.7 %copy-start.2 = (bf16[2,4,80,720]{3,2,1,0:T(8,128)(2,1)S(1)}, bf16[2,4,80,720]{3,2,1,0:T(8,128)(2,1)}, u32[]{:S(2)}) copy-start(bf16[2,4,80,720]{3,2,1,0:T(8,128)(2,1)} %alpha.5) | copy-start | bytes 2764804
  48.6 23.7 %copy-start.9 = (bf16[4,80,720]{2,1,0:T(8,128)(2,1)S(1)}, bf16[4,80,720]{2,1,0:T(8,128)(2,1)}, u32[]{:S(2)}) copy-start(bf16[4,80,720]{2,1,0:T(8,128)(2,1)} %static.3) | copy-start | bytes 1382404
  49.9 7.8 %collective-permute-start.19 = (bf16[160,384]{1,0:T(8,128)(2,1)S(1)}, bf16[160,384]{1,0:T(8,128)(2,1)S(1)}, u32[]{:S(2)}, u32[]{:S(2)}) collective-permute-start(bf16[160,384]{1,0:T(8,128)(2,1)S(1)} %get-tuple-element.71), channel_id=1, source_target_pairs={{0,1},{1,0},{2,3},{3,2},{4,5},{5,4},{6,7},{7,6},{8,9},{9,8},{10,11... | collective-permute-start | bytes 368648 | tf_op jit(solution)/shard_map/ppermute | solution.py:394
  49.9 10.0 %collective-permute-start.20 = (bf16[160,384]{1,0:T(8,128)(2,1)S(1)}, bf16[160,384]{1,0:T(8,128)(2,1)S(1)}, u32[]{:S(2)}, u32[]{:S(2)}) collective-permute-start(bf16[160,384]{1,0:T(8,128)(2,1)S(1)} %get-tuple-element.72), channel_id=1, source_target_pairs={{0,2},{1,3},{2,0},{3,1},{4,6},{5,7},{6,4},{7,5},{8,10},{9,11},{10,... | collective-permute-start | bytes 368648 | tf_op jit(solution)/shard_map/ppermute | solution.py:394
  51.5 3.1 %collective-permute-start.26 = (bf16[80,384]{1,0:T(8,128)(2,1)S(1)}, bf16[80,384]{1,0:T(8,128)(2,1)S(1)}, u32[]{:S(2)}, u32[]{:S(2)}) collective-permute-start(bf16[80,384]{1,0:T(8,128)(2,1)S(1)} %get-tuple-element.80), channel_id=1, source_target_pairs={{0,1},{1,0},{2,3},{3,2},{4,5},{5,4},{6,7},{7,6},{8,9},{9,8},{10,11... | collective-permute-start | bytes 184328 | tf_op jit(solution)/shard_map/ppermute | solution.py:394
  51.7 5.9 %collective-permute-start.27 = (bf16[80,384]{1,0:T(8,128)(2,1)S(1)}, bf16[80,384]{1,0:T(8,128)(2,1)S(1)}, u32[]{:S(2)}, u32[]{:S(2)}) collective-permute-start(bf16[80,384]{1,0:T(8,128)(2,1)S(1)} %get-tuple-element.81), channel_id=1, source_target_pairs={{0,2},{1,3},{2,0},{3,1},{4,6},{5,7},{6,4},{7,5},{8,10},{9,11},{10,... | collective-permute-start | bytes 184328 | tf_op jit(solution)/shard_map/ppermute | solution.py:394
  52.2 9.2 %collective-permute-start.21 = (bf16[160,384]{1,0:T(8,128)(2,1)S(1)}, bf16[160,384]{1,0:T(8,128)(2,1)S(1)}, u32[]{:S(2)}, u32[]{:S(2)}) collective-permute-start(bf16[160,384]{1,0:T(8,128)(2,1)S(1)} %get-tuple-element.73), channel_id=1, source_target_pairs={{0,3},{1,2},{2,1},{3,0},{4,7},{5,6},{6,5},{7,4},{8,11},{9,10},{10,... | collective-permute-start | bytes 368648 | tf_op jit(solution)/shard_map/ppermute | solution.py:394
  54.6 7.2 %collective-permute-start.15 = (bf16[160,384]{1,0:T(8,128)(2,1)S(1)}, bf16[160,384]{1,0:T(8,128)(2,1)S(1)}, u32[]{:S(2)}, u32[]{:S(2)}) collective-permute-start(bf16[160,384]{1,0:T(8,128)(2,1)S(1)} %get-tuple-element.66), channel_id=1, source_target_pairs={{0,4},{1,5},{2,6},{3,7},{4,0},{5,1},{6,2},{7,3},{8,12},{9,13},{10,... | collective-permute-start | bytes 368648 | tf_op jit(solution)/shard_map/ppermute | solution.py:394
  57.5 10.8 %collective-permute-start.16 = (bf16[160,384]{1,0:T(8,128)(2,1)S(1)}, bf16[160,384]{1,0:T(8,128)(2,1)S(1)}, u32[]{:S(2)}, u32[]{:S(2)}) collective-permute-start(bf16[160,384]{1,0:T(8,128)(2,1)S(1)} %get-tuple-element.67), channel_id=1, source_target_pairs={{0,5},{1,4},{2,7},{3,6},{4,1},{5,0},{6,3},{7,2},{8,13},{9,12},{10,... | collective-permute-start | bytes 368648 | tf_op jit(solution)/shard_map/ppermute | solution.py:394
  57.7 11.6 %collective-permute-start.17 = (bf16[160,384]{1,0:T(8,128)(2,1)S(1)}, bf16[160,384]{1,0:T(8,128)(2,1)S(1)}, u32[]{:S(2)}, u32[]{:S(2)}) collective-permute-start(bf16[160,384]{1,0:T(8,128)(2,1)S(1)} %get-tuple-element.68), channel_id=1, source_target_pairs={{0,6},{1,7},{2,4},{3,5},{4,2},{5,3},{6,0},{7,1},{8,14},{9,15},{10,... | collective-permute-start | bytes 368648 | tf_op jit(solution)/shard_map/ppermute | solution.py:394
  60.0 11.0 %collective-permute-start.18 = (bf16[160,384]{1,0:T(8,128)(2,1)S(1)}, bf16[160,384]{1,0:T(8,128)(2,1)S(1)}, u32[]{:S(2)}, u32[]{:S(2)}) collective-permute-start(bf16[160,384]{1,0:T(8,128)(2,1)S(1)} %get-tuple-element.69), channel_id=1, source_target_pairs={{0,7},{1,6},{2,5},{3,4},{4,3},{5,2},{6,1},{7,0},{8,15},{9,14},{10,... | collective-permute-start | bytes 368648 | tf_op jit(solution)/shard_map/ppermute | solution.py:394
  61.4 13.3 %collective-permute-start.28 = (bf16[80,384]{1,0:T(8,128)(2,1)S(1)}, bf16[80,384]{1,0:T(8,128)(2,1)S(1)}, u32[]{:S(2)}, u32[]{:S(2)}) collective-permute-start(bf16[80,384]{1,0:T(8,128)(2,1)S(1)} %get-tuple-element.82), channel_id=1, source_target_pairs={{0,3},{1,2},{2,1},{3,0},{4,7},{5,6},{6,5},{7,4},{8,11},{9,10},{10,... | collective-permute-start | bytes 184328 | tf_op jit(solution)/shard_map/ppermute | solution.py:394
  61.8 12.9 %collective-permute-start.22 = (bf16[80,384]{1,0:T(8,128)(2,1)S(1)}, bf16[80,384]{1,0:T(8,128)(2,1)S(1)}, u32[]{:S(2)}, u32[]{:S(2)}) collective-permute-start(bf16[80,384]{1,0:T(8,128)(2,1)S(1)} %get-tuple-element.75), channel_id=1, source_target_pairs={{0,4},{1,5},{2,6},{3,7},{4,0},{5,1},{6,2},{7,3},{8,12},{9,13},{10,... | collective-permute-start | bytes 184328 | tf_op jit(solution)/shard_map/ppermute | solution.py:394
  68.3 6.4 %collective-permute-start.23 = (bf16[80,384]{1,0:T(8,128)(2,1)S(1)}, bf16[80,384]{1,0:T(8,128)(2,1)S(1)}, u32[]{:S(2)}, u32[]{:S(2)}) collective-permute-start(bf16[80,384]{1,0:T(8,128)(2,1)S(1)} %get-tuple-element.76), channel_id=1, source_target_pairs={{0,5},{1,4},{2,7},{3,6},{4,1},{5,0},{6,3},{7,2},{8,13},{9,12},{10,... | collective-permute-start | bytes 184328 | tf_op jit(solution)/shard_map/ppermute | solution.py:394
  69.3 5.6 %collective-permute-start.24 = (bf16[80,384]{1,0:T(8,128)(2,1)S(1)}, bf16[80,384]{1,0:T(8,128)(2,1)S(1)}, u32[]{:S(2)}, u32[]{:S(2)}) collective-permute-start(bf16[80,384]{1,0:T(8,128)(2,1)S(1)} %get-tuple-element.77), channel_id=1, source_target_pairs={{0,6},{1,7},{2,4},{3,5},{4,2},{5,3},{6,0},{7,1},{8,14},{9,15},{10,... | collective-permute-start | bytes 184328 | tf_op jit(solution)/shard_map/ppermute | solution.py:394
  71.0 4.9 %collective-permute-start.25 = (bf16[80,384]{1,0:T(8,128)(2,1)S(1)}, bf16[80,384]{1,0:T(8,128)(2,1)S(1)}, u32[]{:S(2)}, u32[]{:S(2)}) collective-permute-start(bf16[80,384]{1,0:T(8,128)(2,1)S(1)} %get-tuple-element.78), channel_id=1, source_target_pairs={{0,7},{1,6},{2,5},{3,4},{4,3},{5,2},{6,1},{7,0},{8,15},{9,14},{10,... | collective-permute-start | bytes 184328 | tf_op jit(solution)/shard_map/ppermute | solution.py:394
  (11 other events, 48.6 us)

commit v3 on v2

--- a/solution.py
+++ b/solution.py
@@ -94,35 +94,58 @@
     ]
 
 
+def order_matrix(plan):
+    row = iota((plan.lat, plan.lat), 0)
+    source = (row // plan.rows ^ lax.axis_index("band")) * plan.rows + row % plan.rows
+    return one_hot(iota((plan.lat, plan.lat), 1) == source)
+
+
 def lon_kernel(plan, alpha, static, root, lat, *refs):
     n = 2 * plan.bands
-    x_refs, (lat_out, a_buf, s_buf, r_buf, packed, sems) = refs[:n], refs[n:]
+    x_refs, (lat_k, lat_s, l_buf, a_buf, s_buf, r_buf, packed, sems) = refs[:n], refs[n:]
     species, rows, extra, members = plan.species, plan.rows, plan.extra, plan.members
-    moves = [(root, r_buf)] + [(alpha.at[m], a_buf.at[m]) for m in range(members)]
-    moves += [(static, s_buf), (lat, lat_out)]
+    moves = [(lat, l_buf), (root, r_buf)] + [(alpha.at[m], a_buf.at[m]) for m in range(members)]
+    moves.append((static, s_buf))
     copies = [pltpu.make_async_copy(src, dst, sems.at[i]) for i, (src, dst) in enumerate(moves)]
     for copy in copies:
         copy.start()
     rank, me = lax.axis_index("mem"), lax.axis_index("band")
+    first = (rank // plan.copies) * plan.count
     t = iota((extra, rows), 0)
-    mine = iota((extra, rows), 1) == (rank // plan.copies) * plan.count + t
-    select = one_hot(mine & (t < plan.count) & (rank % plan.copies == 0))
-    for copy in copies:
+    select = one_hot((iota((extra, rows), 1) == first + t) & (t < plan.count) & (rank % plan.copies == 0))
+    copies[0].wait()
+    order = order_matrix(plan)
+    lat_k[...] = dot_nt(l_buf[...], order).astype(BF16)
+    shape = (plan.bands * extra, plan.lat)
+    row = iota(shape, 0)
+    t = row % extra
+    source = (row // extra ^ me) * rows + first + t
+    pick = one_hot((iota(shape, 1) == source) & (t < plan.count) & (rank % plan.copies == 0))
+    lat_s[...] = dot_nt(l_buf[...], pick).astype(BF16)
+    ys = []
+    for copy in copies[1:-1]:
         copy.wait()
+    half = members // 2
+    left = [a_buf[m, s] for s in range(species) for m in range(half)]
+    ys.append(dot(jnp.concatenate(left, 0), r_buf[...]))
+    copies[-1].wait()
     left = []
     for s in range(species):
-        left += [a_buf[m, s] for m in range(members)] + [dot(select, s_buf[s]).astype(BF16)]
-    y = dot(jnp.concatenate(left, 0), r_buf[...])
-    size = members * rows + extra
-    fields = [y[s * size : (s + 1) * size] for s in range(species)]
-    for half in range(2):
-        for b in range(plan.bands):
-            at = (2 * b + half) * plan.width
-            packed[half, b] = pack(fields, at, plan.width, plan.slot).astype(BF16)
+        left += [a_buf[m, s] for m in range(half, members)] + [dot(select, s_buf[s]).astype(BF16)]
+    ys.append(dot(jnp.concatenate(left, 0), r_buf[...]))
+    tops = (half * rows, (members - half) * rows + extra)
+    at_row = 0
+    for y, size in zip(ys, tops):
+        fields = [y[s * size : (s + 1) * size] for s in range(species)]
+        for h in range(2):
+            for b in range(plan.bands):
+                at = (2 * b + h) * plan.width
+                packed[h, b, at_row : at_row + size, :] = pack(fields, at, plan.width, plan.slot).astype(BF16)
+        at_row += size
     for own in range(2):
-        half = (rank & 1) ^ 1 ^ own
+        h = (rank & 1) ^ 1 ^ own
         for k in range(plan.bands):
-            x_refs[own * plan.bands + k][...] = packed[half, me ^ k]
+            x_refs[own * plan.bands + k][...] = packed[h, me ^ k]
 
 
 def root_kernel(plan, root, lat, w_ref, lat_t):
@@ -148,24 +171,7 @@
             for m in range(plan.members):
                 pieces = [pert[m, s].astype(F32) for s in range(plan.species)]
                 p_ref[m] = pack(pieces, *at).astype(BF16)
-            s_ref[...] = 0.6 * pack([std[s] for s in range(plan.species)], *at)
-
-
-def order_matrix(plan):
-    row = iota((plan.lat, plan.lat), 0)
-    source = (row // plan.rows ^ lax.axis_index("band")) * plan.rows + row % plan.rows
-    return one_hot(iota((plan.lat, plan.lat), 1) == source)
-
-
-def forward_kernel(plan, lat, lat_k, lat_s):
-    rank, me = lax.axis_index("mem"), lax.axis_index("band")
-    lat_k[...] = dot_nt(lat[...], order_matrix(plan)).astype(BF16)
-    shape = (plan.bands * plan.extra, plan.lat)
-    row = iota(shape, 0)
-    t = row % plan.extra
-    source = (row // plan.extra ^ me) * plan.rows + (rank // plan.copies) * plan.count + t
-    pick = one_hot((iota(shape, 1) == source) & (t < plan.count) & (rank % plan.copies == 0))
-    lat_s[...] = dot_nt(lat[...], pick).astype(BF16)
+            s_ref[...] = 0.6 * pack([std[s].astype(F32) for s in range(plan.species)], *at)
 
 
 def normal_kernel(plan, error, jac, count, mask, h_p, h_o, inverse):
@@ -189,12 +195,12 @@
         side = jnp.broadcast_to(rank & 1, (n, plan.width)) == 0
         for i, pair in enumerate(pairs):
             low, high = sums[pair][:, : plan.width], sums[pair][:, plan.width :]
-            h_p[i, r : r + n, :] = jnp.where(side, high, low)
+            h_p[i, r : r + n, :] = jnp.where(side, high, low).astype(BF16)
             h_o[i, r : r + n, :] = jnp.where(side, low, high)
 
 
 def lat_kernel(plan, weights, lat_k, lat_s, pert, std, *refs):
-    x_refs, out = refs[: plan.bands], refs[plan.bands]
+    x_refs, outs = refs[: plan.bands], refs[plan.bands :]
     rows = plan.rows
     factor = factors(plan, weights, lax.axis_index("mem"))
     z = jnp.concatenate([x[plan.members * rows :, :] for x in x_refs], 0)
@@ -202,15 +208,25 @@
     for m in range(plan.members):
         z = jnp.concatenate([x[m * rows : (m + 1) * rows, :] for x in x_refs], 0)
         acc += factor[m] * pert[m].astype(F32) * dot(lat_k[...], z)
-    out[...] = acc.astype(out.dtype)
-
-
-def pair_kernel(plan, own, got, first, *refs):
-    others, total = refs[:-1], refs[-1]
+    if len(outs) == 1:
+        outs[0][...] = acc
+        return
+    far, near, total = outs
+    total[...] = acc
+    side = lax.axis_index("mem") // plan.blocks
+    n = plan.padded // 2
+    far[...] = total[pl.ds(pl.multiple_of((side ^ 1) * n, 16), n), :].astype(BF16)
+    near[...] = total[pl.ds(pl.multiple_of(side * n, 16), n), :].astype(BF16)
+
+
+def pair_kernel(plan, far, own, got, *refs):
+    outs, total = refs[:-1], refs[-1]
     block = lax.axis_index("mem") // 2
-    total[...] = own[...] + got[...].astype(F32)
-    for k, out in enumerate((first, *others)):
-        at = pl.multiple_of((block ^ k) * plan.height, 8)
+    n, half = plan.padded // 2, plan.blocks // 2
+    side = block // half ^ far
+    total[...] = own[pl.ds(pl.multiple_of(side * n, 16), n), :] + got[...].astype(F32)
+    for k, out in enumerate(outs):
+        at = pl.multiple_of((block % half ^ k) * plan.height, 8)
         out[...] = total[pl.ds(at, plan.height), :].astype(out.dtype)
 
 
@@ -231,7 +247,7 @@
                 part = [p[i * n : (i + 1) * n] for p in pieces]
                 sums = []
                 for s in range(species):
-                    terms = [h[pairs.index((min(s, t), max(s, t)))] * part[t] for t in range(species)]
+                    terms = [h[pairs.index((min(s, t), max(s, t)))].astype(F32) * part[t] for t in range(species)]
                     sums.append(functools.reduce(jnp.add, terms))
                 blocks.append(pack(sums, 0, plan.width, plan.slot))
             if plan.height > 2 * n:
@@ -320,11 +336,14 @@
 
     sent = struct((members * plan.rows + plan.extra, lanes), BF16)
     lat = pad_lat(lat_root, 0)
-    *got, lat = call(
-        functools.partial(lon_kernel, plan), [sent] * (2 * bands) + [struct(lat.shape, BF16)],
+    lat_shapes = [struct((plan.padded, plan.lat), BF16), struct((plan.padded, bands * plan.extra), BF16)]
+    sizes = [sent.shape] * (2 * bands) + [(plan.padded, up(plan.lat, 128)), (plan.padded, 128)]
+    *got, lat_k, lat_s = call(
+        functools.partial(lon_kernel, plan), [sent] * (2 * bands) + lat_shapes,
         alpha, static_ctl, lon_root, lat, flops=10**9, spaces=[pltpu.HBM] * 4,
-        vmem=VMEM_BYTES - 2 * (2 * bands * math.prod(sent.shape) + math.prod(lat.shape)) - (3 << 17),
+        vmem=VMEM_BYTES - 2 * sum(math.prod(size) for size in sizes) - (3 << 17),
         scratch=[
+            pltpu.VMEM(lat.shape, BF16),
             pltpu.VMEM(alpha.shape, BF16),
             pltpu.VMEM(static_ctl.shape, BF16),
             pltpu.VMEM(lon_root.shape, BF16),
@@ -340,34 +359,38 @@
     pert_shape = struct((members, plan.padded, lanes), BF16)
     std_shape = struct((plan.padded, lanes), F32)
     pert, std = pad_lat(perturbations, 2), pad_lat(static_std, 1)
-    lat_k, lat_s = call(
-        functools.partial(forward_kernel, plan),
-        [struct((plan.padded, plan.lat), BF16), struct((plan.padded, bands * plan.extra), BF16)], lat,
-    )
     perts_p, std_p = call(functools.partial(prep_kernel, plan, 0), [pert_shape, std_shape], pert, std)
     perts_o, std_o = call(functools.partial(prep_kernel, plan, 1), [pert_shape, std_shape], pert, std)
     h_shape = struct((species * (species + 1) // 2, plan.pixel, plan.width), F32)
     h_p, h_o = call(
-        functools.partial(normal_kernel, plan), [h_shape, h_shape],
+        functools.partial(normal_kernel, plan), [struct(h_shape.shape, BF16), h_shape],
         channel_error, jacobian, obs_count, channel_mask, smem=1,
         scratch=[pltpu.SMEM(channel_error.shape, F32)],
     )
     h_got = send(h_p, "mem", 1)
     perts_got = send(perts_p, "mem", 1)
 
-    sums = []
-    for own, pert, std, kind in ((0, perts_p, std_p, BF16), (1, perts_o, std_o, F32)):
-        sums += call(
-            functools.partial(lat_kernel, plan), [struct((plan.padded, lanes), kind)],
-            member_weight, lat_k, lat_s, pert, std, *fields[own], smem=1,
-        )
-    got = send(sums[0], "mem", 1)
-    scratch = [pltpu.VMEM((plan.padded, lanes), F32)]
+    n = plan.padded // 2
+    whole, part = pltpu.VMEM((plan.padded, lanes), F32), pltpu.VMEM((n, lanes), F32)
+    far, near = call(
+        functools.partial(lat_kernel, plan), [struct((n, lanes), BF16)] * 2,
+        member_weight, lat_k, lat_s, perts_p, std_p, *fields[0], smem=1, scratch=[whole],
+    )
+    (own,) = call(
+        functools.partial(lat_kernel, plan), [struct((plan.padded, lanes), F32)],
+        member_weight, lat_k, lat_s, perts_o, std_o, *fields[1], smem=1,
+    )
+    half = plan.blocks // 2
+    last = call(
+        functools.partial(pair_kernel, plan, 1), [block] * half,
+        own, send(far, "mem", 1), scratch=[part],
+    )
     parts = call(
-        functools.partial(pair_kernel, plan),
-        [struct((plan.height, lanes), F32)] + [block] * (plan.blocks - 1),
-        sums[1], got, scratch=scratch,
-    )
+        functools.partial(pair_kernel, plan, 0),
+        [struct((plan.height, lanes), F32)] + [block] * (half - 1),
+        own, send(near, "mem", 1), scratch=[part],
+    )
+    parts = list(parts) + list(last)
     parts = [parts[0]] + [send(parts[k], "mem", 2 * k) for k in range(1, plan.blocks)]
     (g,) = call(functools.partial(pixel_kernel, plan), [block], h_o, h_got, *parts)
     gs = [g] + [send(g, "mem", 2 * k) for k in range(1, plan.blocks)]
@@ -384,7 +407,7 @@
     for flip, pert in ((1, perts_got), (0, perts_o)):
         got = call(
             functools.partial(back_kernel, plan, flip), shapes,
-            member_weight, lat_t, pert, std_o, *gs, smem=1, scratch=scratch,
+            member_weight, lat_t, pert, std_o, *gs, smem=1, scratch=[whole],
         )
         for late in range(2):
             for k in range(bands):

time: 77.9 us -> 78.8 us (1.012)
  starting transfers between devices: 32.1 us -> 34 us
  waiting for transfers between devices: 20.9 us -> 19.5 us
    ppermute x15 -> x16, starting transfers between devices: 17.4 us -> 20.7 us  [send(): return lax.ppermute(x, axis, [(i, i ^ k) for i in range(n)])]
    ppermute x15 -> x16, waiting for transfers between devices: 13.1 us -> 11.4 us  [send(): return lax.ppermute(x, axis, [(i, i ^ k) for i in range(n)])]
    ppermute x14, starting transfers between devices: 14.7 us -> 13.3 us  [shards(): x = lax.ppermute(x, ('mem', 'band'), swap)]
    unnamed x30 -> x32, local copies, waits for them, and re-layouts: 4.62 us -> 4.87 us
  transfers between devices with their start and end apart: 29 -> 30, of which waited for: 10 -> 10; matrix products, arithmetic and copies ran while one was open for 6% -> 6% of each run, Pallas kernels for 15% -> 16%
where the time goes in v3:
time: 78.8 us; the launch traced here: 78.4 us
  starting transfers between devices  34 us (43%)
  waiting for transfers between devices  19.5 us (25%)
  Pallas kernels  18.8 us (24%)
  local copies, waits for them, and re-layouts  4.87 us (6%)
  between operations  1.12 us (1%)
    ppermute x16, starting transfers between devices, send(): return lax.ppermute(x, axis, [(i, i ^ k) for i in range(n)])  20.7 us
    pallas_call x12, Pallas kernels, call(): pl.pallas_call(kernel, out_shape=outs, in_specs=[SMEM] * smem + [VMEM] *...  14.8 us
    ppermute x14, starting transfers between devices, shards(): x = lax.ppermute(x, ('mem', 'band'), swap)  13.3 us
    ppermute x16, waiting for transfers between devices, send(): return lax.ppermute(x, axis, [(i, i ^ k) for i in range(n)])  11.4 us
    ppermute x14, waiting for transfers between devices, shards(): x = lax.ppermute(x, ('mem', 'band'), swap)  8.19 us
    unnamed x32, local copies, waits for them, and re-layouts  4.87 us
    pallas_call x1, Pallas kernels, shards(): pl.pallas_call(functools.partial(early_kernel, plan), out_shape=[struct(a...  2.38 us
    pallas_call x1, Pallas kernels, shards(): pl.pallas_call(functools.partial(late_kernel, plan), out_shape=struct(alp...  1.62 us
  transfers between devices with their start and end apart: 30, of which 10 were waited for; matrix products, arithmetic and copies ran while one was open for 6% of the time, Pallas kernels for 16%

profile of v3, /device:TPU:0, one launch (start us, length us, event | category | flops | bytes accessed | tf_op | source)
XLA Modules:
  0.0 78.4 jit_solution(5669143981403698361)
XLA Ops:
  0.6 4.4 %shard_map.126 = (bf16[176,384]{1,0:T(8,128)(2,1)}, bf16[176,384]{1,0:T(8,128)(2,1)}, bf16[176,384]{1,0:T(8,128)(2,1)}, bf16[176,384]{1,0:T(8,128)(2,1)}, bf16[1...) custom-call(bf16[2,4,80,720]{3,2,1,0:T(8,128)(2,1)} %alpha.5, ...), custom_call_target="tpu_custom_call" | custom-call | flops 1000000000 | bytes 3951104 | tf_op jit(solution)/shard_map/pallas_call | solution.py:30
  5.6 2.6 %collective-permute-start.6 = (bf16[176,384]{1,0:T(8,128)(2,1)}, bf16[176,384]{1,0:T(8,128)(2,1)S(1)}, u32[]{:S(2)}, u32[]{:S(2)}) collective-permute-start(bf16[176,384]{1,0:T(8,128)(2,1)} %get-tuple-element.60), channel_id=1, source_target_pairs={{0,2},{1,3},{2,0},{3,1},{4,6},{5,7},{6,4},{7,5},{8,10},{9,11},{10,... | collective-permute-start | bytes 405512 | tf_op jit(solution)/shard_map/ppermute | solution.py:325
  8.3 2.6 %copy.14.pert = bf16[2,4,320,180]{3,2,1,0:T(8,128)(2,1)S(1)} copy(bf16[2,4,320,180]{2,1,3,0:T(4,128)(2,1)} %param.13) | data formatting | bytes 1843200 | tf_op args[2]
  10.9 1.9 %copy.15.std = f32[4,320,180]{2,1,0:T(8,128)S(1)} copy(f32[4,320,180]{1,0,2:T(4,128)} %param.14) | data formatting | bytes 1843200 | tf_op args[3]
  13.7 1.6 %collective-permute-start = (bf16[2,320,384]{2,1,0:T(8,128)(2,1)S(1)}, bf16[2,320,384]{2,1,0:T(8,128)(2,1)S(1)}, u32[]{:S(2)}, u32[]{:S(2)}) collective-permute-start(bf16[2,320,384]{2,1,0:T(8,128)(2,1)S(1)} %get-tuple-element.46.pert), channel_id=1, source_target_pairs={{0,4},{4,0},{8,12},{12,8},{16,20},{20,16},{24,28},{28,24},{1,5},{5... | collective-permute-start | bytes 1474568 | tf_op jit(solution)/shard_map/ppermute | solution.py:325
  15.3 1.5 %collective-permute-start.3 = (bf16[176,384]{1,0:T(8,128)(2,1)S(1)}, bf16[176,384]{1,0:T(8,128)(2,1)S(1)}, u32[]{:S(2)}, u32[]{:S(2)}) collective-permute-start(bf16[176,384]{1,0:T(8,128)(2,1)S(1)} %copy-done.14), channel_id=1, source_target_pairs={{0,2},{1,3},{2,0},{3,1},{4,6},{5,7},{6,4},{7,5},{8,10},{9,11},{10,... | collective-permute-start | bytes 405512 | tf_op jit(solution)/shard_map/ppermute | solution.py:325
  16.9 1.1 %shard_map.128 = (bf16[160,384]{1,0:T(8,128)(2,1)S(1)}, bf16[160,384]{1,0:T(8,128)(2,1)S(1)}) custom-call(s32[16]{0:T(128)S(1)} %copy-done.8, bf16[320,320]{1,0:T(8,128)(2,1)S(1)} %copy-done.3, bf16[320,64]{1,0:T(8,128)(2,1)S(1)} %copy-done.4, bf16[2,320,384]{2,1,0:T(8,128)(2,1)S(1)} %get-tuple-element.46.pert, f32[320,384]{1,0:T(8,128)S(1)} %get-tuple-element.57.std, ...), custom_call_target="tpu_custom_call" | custom-call | flops 100000000 | bytes 2015296 | tf_op jit(solution)/shard_map/pallas_call | solution.py:30
  20.8 2.8 %shard_map.125 = (bf16[10,40,90]{2,1,0:T(8,128)(2,1)S(1)}, f32[10,40,90]{2,1,0:T(8,128)S(1)}) custom-call(f32[32]{0:T(128)S(1)} %copy-done.9, bf16[32,4,40,180]{3,2,1,0:T(8,128)(2,1)S(1)} %copy-done, s32[40,180]{1,0:T(8,128)S(1)} %copy-done.7, s32[32,40,180]{2,1,0:T(8,128)S(1)} %copy-done.1), custom_call_target="tpu_custom_call" | custom-call | flops 100000000 | bytes 3009728 | tf_op jit(solution)/shard_map/pallas_call | solution.py:30
  23.6 1.2 %collective-permute-start.1 = (bf16[10,40,90]{2,1,0:T(8,128)(2,1)S(1)}, bf16[10,40,90]{2,1,0:T(8,128)(2,1)S(1)}, u32[]{:S(2)}, u32[]{:S(2)}) collective-permute-start(bf16[10,40,90]{2,1,0:T(8,128)(2,1)S(1)} %get-tuple-element.49), channel_id=1, source_target_pairs={{0,4},{4,0},{8,12},{12,8},{16,20},{20,16},{24,28},{28,24},{1,5},{5... | collective-permute-start | bytes 216008 | tf_op jit(solution)/shard_map/ppermute | solution.py:325
  25.9 4.5 %collective-permute-done.8.got = bf16[160,384]{1,0:T(8,128)(2,1)S(1)} collective-permute-done((bf16[160,384]{1,0:T(8,128)(2,1)S(1)}, bf16[160,384]{1,0:T(8,128)(2,1)S(1)}, u32[]{:S(2)}, u32[]{:S(2)}) %collective-permute-start.8) | collective-permute-done | bytes 122912 | tf_op jit(solution)/shard_map/ppermute | solution.py:325
  30.5 2.1 %collective-permute-start.9 = (bf16[80,384]{1,0:T(8,128)(2,1)S(1)}, bf16[80,384]{1,0:T(8,128)(2,1)S(1)}, u32[]{:S(2)}, u32[]{:S(2)}) collective-permute-start(bf16[80,384]{1,0:T(8,128)(2,1)S(1)} %get-tuple-element.64), channel_id=1, source_target_pairs={{0,8},{4,12},{8,0},{12,4},{16,24},{20,28},{24,16},{28,20},{1,9},{5... | collective-permute-start | bytes 184328 | tf_op jit(solution)/shard_map/ppermute | solution.py:325
  33.1 3.1 %collective-permute-start.11 = (bf16[80,384]{1,0:T(8,128)(2,1)S(1)}, bf16[80,384]{1,0:T(8,128)(2,1)S(1)}, u32[]{:S(2)}, u32[]{:S(2)}) collective-permute-start(bf16[80,384]{1,0:T(8,128)(2,1)S(1)} %get-tuple-element.66), channel_id=1, source_target_pairs={{0,16},{4,20},{8,24},{12,28},{16,0},{20,4},{24,8},{28,12},{1,17},{... | collective-permute-start | bytes 184328 | tf_op jit(solution)/shard_map/ppermute | solution.py:325
  36.2 1.3 %collective-permute-start.12 = (bf16[80,384]{1,0:T(8,128)(2,1)S(1)}, bf16[80,384]{1,0:T(8,128)(2,1)S(1)}, u32[]{:S(2)}, u32[]{:S(2)}) collective-permute-start(bf16[80,384]{1,0:T(8,128)(2,1)S(1)} %get-tuple-element.67), channel_id=1, source_target_pairs={{0,24},{4,28},{8,16},{12,20},{16,8},{20,12},{24,0},{28,4},{1,25},{... | collective-permute-start | bytes 184328 | tf_op jit(solution)/shard_map/ppermute | solution.py:325
  37.6 2.7 %collective-permute-done.11.refs_1_ = bf16[80,384]{1,0:T(8,128)(2,1)S(1)} collective-permute-done((bf16[80,384]{1,0:T(8,128)(2,1)S(1)}, bf16[80,384]{1,0:T(8,128)(2,1)S(1)}, u32[]{:S(2)}, u32[]{:S(2)}) %collective-permute-start.11) | collective-permute-done | bytes 61472 | tf_op jit(solution)/shard_map/ppermute | solution.py:325
  40.3 1.9 %collective-permute-done.12.refs_2_ = bf16[80,384]{1,0:T(8,128)(2,1)S(1)} collective-permute-done((bf16[80,384]{1,0:T(8,128)(2,1)S(1)}, bf16[80,384]{1,0:T(8,128)(2,1)S(1)}, u32[]{:S(2)}, u32[]{:S(2)}) %collective-permute-start.12) | collective-permute-done | bytes 61472 | tf_op jit(solution)/shard_map/ppermute | solution.py:325
  42.7 1.5 %collective-permute-start.15 = (bf16[80,384]{1,0:T(8,128)(2,1)S(1)}, bf16[80,384]{1,0:T(8,128)(2,1)S(1)}, u32[]{:S(2)}, u32[]{:S(2)}) collective-permute-start(bf16[80,384]{1,0:T(8,128)(2,1)S(1)} %shard_map.131.refs_0_), channel_id=1, source_target_pairs={{0,24},{4,28},{8,16},{12,20},{16,8},{20,12},{24,0},{28,4},{1,25},{... | collective-permute-start | bytes 184328 | tf_op jit(solution)/shard_map/ppermute | solution.py:325
  44.2 2.9 %collective-permute-start.13 = (bf16[80,384]{1,0:T(8,128)(2,1)S(1)}, bf16[80,384]{1,0:T(8,128)(2,1)S(1)}, u32[]{:S(2)}, u32[]{:S(2)}) collective-permute-start(bf16[80,384]{1,0:T(8,128)(2,1)S(1)} %shard_map.131.refs_0_), channel_id=1, source_target_pairs={{0,8},{4,12},{8,0},{12,4},{16,24},{20,28},{24,16},{28,20},{1,9},{5... | collective-permute-start | bytes 184328 | tf_op jit(solution)/shard_map/ppermute | solution.py:325
  47.2 1.3 %shard_map.122 = (bf16[720,768]{1,0:T(8,128)(2,1)S(1)}, bf16[320,320]{1,0:T(8,128)(2,1)S(1)}) custom-call(bf16[720,720]{1,0:T(8,128)(2,1)S(1)} %copy-done.10, bf16[320,320]{1,0:T(8,128)(2,1)S(1)} %copy-done.12), custom_call_target="tpu_custom_call" | custom-call | flops 1000000000 | bytes 2552320 | tf_op jit(solution)/shard_map/pallas_call | solution.py:30
  48.8 1.3 %collective-permute-done.14.refs_2_ = bf16[80,384]{1,0:T(8,128)(2,1)S(1)} collective-permute-done((bf16[80,384]{1,0:T(8,128)(2,1)S(1)}, bf16[80,384]{1,0:T(8,128)(2,1)S(1)}, u32[]{:S(2)}, u32[]{:S(2)}) %collective-permute-start.14) | collective-permute-done | bytes 61472 | tf_op jit(solution)/shard_map/ppermute | solution.py:325
  50.1 1.3 %shard_map.133 = (bf16[160,384]{1,0:T(8,128)(2,1)S(1)}, bf16[160,384]{1,0:T(8,128)(2,1)S(1)}, bf16[160,384]{1,0:T(8,128)(2,1)S(1)}, bf16[160,384]{1,0:T(8,128)(2...) custom-call(s32[16]{0:T(128)S(1)} %copy-done.8, ...), custom_call_target="tpu_custom_call" | custom-call | flops 100000000 | bytes 2170944 | tf_op jit(solution)/shard_map/pallas_call | solution.py:30
  51.5 1.6 %collective-permute-start.21 = (bf16[160,384]{1,0:T(8,128)(2,1)S(1)}, bf16[160,384]{1,0:T(8,128)(2,1)S(1)}, u32[]{:S(2)}, u32[]{:S(2)}) collective-permute-start(bf16[160,384]{1,0:T(8,128)(2,1)S(1)} %get-tuple-element.74), channel_id=1, source_target_pairs={{0,2},{1,3},{2,0},{3,1},{4,6},{5,7},{6,4},{7,5},{8,10},{9,11},{10,... | collective-permute-start | bytes 368648 | tf_op jit(solution)/shard_map/ppermute | solution.py:417
  53.7 1.2 %collective-permute-start.22 = (bf16[160,384]{1,0:T(8,128)(2,1)S(1)}, bf16[160,384]{1,0:T(8,128)(2,1)S(1)}, u32[]{:S(2)}, u32[]{:S(2)}) collective-permute-start(bf16[160,384]{1,0:T(8,128)(2,1)S(1)} %get-tuple-element.75), channel_id=1, source_target_pairs={{0,3},{1,2},{2,1},{3,0},{4,7},{5,6},{6,5},{7,4},{8,11},{9,10},{10,... | collective-permute-start | bytes 368648 | tf_op jit(solution)/shard_map/ppermute | solution.py:417
  54.9 1.2 %shard_map.132 = (bf16[160,384]{1,0:T(8,128)(2,1)S(1)}, bf16[160,384]{1,0:T(8,128)(2,1)S(1)}, bf16[160,384]{1,0:T(8,128)(2,1)S(1)}, bf16[160,384]{1,0:T(8,128)(2...) custom-call(s32[16]{0:T(128)S(1)} %copy-done.8, ...), custom_call_target="tpu_custom_call" | custom-call | flops 100000000 | bytes 2170944 | tf_op jit(solution)/shard_map/pallas_call | solution.py:30
  56.1 1.2 %collective-permute-start.16 = (bf16[160,384]{1,0:T(8,128)(2,1)S(1)}, bf16[160,384]{1,0:T(8,128)(2,1)S(1)}, u32[]{:S(2)}, u32[]{:S(2)}) collective-permute-start(bf16[160,384]{1,0:T(8,128)(2,1)S(1)} %get-tuple-element.68), channel_id=1, source_target_pairs={{0,4},{1,5},{2,6},{3,7},{4,0},{5,1},{6,2},{7,3},{8,12},{9,13},{10,... | collective-permute-start | bytes 368648 | tf_op jit(solution)/shard_map/ppermute | solution.py:417
  57.3 1.7 %collective-permute-done.28.refs_6_ = bf16[80,384]{1,0:T(8,128)(2,1)S(1)} collective-permute-done((bf16[80,384]{1,0:T(8,128)(2,1)S(1)}, bf16[80,384]{1,0:T(8,128)(2,1)S(1)}, u32[]{:S(2)}, u32[]{:S(2)}) %collective-permute-start.28) | collective-permute-done | bytes 61472 | tf_op jit(solution)/shard_map/ppermute | solution.py:417
  59.0 2.0 %collective-permute-start.18 = (bf16[160,384]{1,0:T(8,128)(2,1)S(1)}, bf16[160,384]{1,0:T(8,128)(2,1)S(1)}, u32[]{:S(2)}, u32[]{:S(2)}) collective-permute-start(bf16[160,384]{1,0:T(8,128)(2,1)S(1)} %get-tuple-element.70), channel_id=1, source_target_pairs={{0,6},{1,7},{2,4},{3,5},{4,2},{5,3},{6,0},{7,1},{8,14},{9,15},{10,... | collective-permute-start | bytes 368648 | tf_op jit(solution)/shard_map/ppermute | solution.py:417
  61.1 1.4 %collective-permute-start.19 = (bf16[160,384]{1,0:T(8,128)(2,1)S(1)}, bf16[160,384]{1,0:T(8,128)(2,1)S(1)}, u32[]{:S(2)}, u32[]{:S(2)}) collective-permute-start(bf16[160,384]{1,0:T(8,128)(2,1)S(1)} %get-tuple-element.71), channel_id=1, source_target_pairs={{0,7},{1,6},{2,5},{3,4},{4,3},{5,2},{6,1},{7,0},{8,15},{9,14},{10,... | collective-permute-start | bytes 368648 | tf_op jit(solution)/shard_map/ppermute | solution.py:417
  64.3 5.6 %collective-permute-done.17.refs_1_ = bf16[160,384]{1,0:T(8,128)(2,1)S(1)} collective-permute-done((bf16[160,384]{1,0:T(8,128)(2,1)S(1)}, bf16[160,384]{1,0:T(8,128)(2,1)S(1)}, u32[]{:S(2)}, u32[]{:S(2)}) %collective-permute-start.17) | collective-permute-done | bytes 122912 | tf_op jit(solution)/shard_map/ppermute | solution.py:417
  70.4 1.5 %collective-permute-start.25 = (bf16[80,384]{1,0:T(8,128)(2,1)S(1)}, bf16[80,384]{1,0:T(8,128)(2,1)S(1)}, u32[]{:S(2)}, u32[]{:S(2)}) collective-permute-start(bf16[80,384]{1,0:T(8,128)(2,1)S(1)} %get-tuple-element.79), channel_id=1, source_target_pairs={{0,6},{1,7},{2,4},{3,5},{4,2},{5,3},{6,0},{7,1},{8,14},{9,15},{10,... | collective-permute-start | bytes 184328 | tf_op jit(solution)/shard_map/ppermute | solution.py:417
  71.9 1.4 %collective-permute-start.26 = (bf16[80,384]{1,0:T(8,128)(2,1)S(1)}, bf16[80,384]{1,0:T(8,128)(2,1)S(1)}, u32[]{:S(2)}, u32[]{:S(2)}) collective-permute-start(bf16[80,384]{1,0:T(8,128)(2,1)S(1)} %get-tuple-element.80), channel_id=1, source_target_pairs={{0,7},{1,6},{2,5},{3,4},{4,3},{5,2},{6,1},{7,0},{8,15},{9,14},{10,... | collective-permute-start | bytes 184328 | tf_op jit(solution)/shard_map/ppermute | solution.py:417
  73.4 2.4 %early.1 = (f32[2,4,80,720]{3,2,1,0:T(8,128)}, f32[4,80,720]{2,1,0:T(8,128)}) custom-call(bf16[2,4,80,720]{3,2,1,0:T(8,128)(2,1)S(1)} %copy-done.2, bf16[4,80,720]{2,1,0:T(8,128)(2,1)S(1)} %copy-done.11, bf16[720,768]{1,0:T(8,128)(2,1)S(1)} %get-tuple-element.44.w, bf16[160,384]{1,0:T(8,128)(2,1)S(1)} %collective-permute-done.16.refs_0_, ...), custom_call_target="tpu_custom_call" | custom-call | flops 1000000000 | bytes 10000000 | tf_op jit(solution)/shard_map/early/pallas_call | solution.py:426
  76.6 1.6 %late.1 = f32[2,4,80,720]{3,2,1,0:T(8,128)} custom-call(f32[2,4,80,720]{3,2,1,0:T(8,128)} %get-tuple-element.76._, bf16[2,4,80,720]{3,2,1,0:T(8,128)(2,1)S(1)} %copy-done.2, bf16[720,768]{1,0:T(8,128)(2,1)S(1)} %get-tuple-element.44.w, bf16[80,384]{1,0:T(8,128)(2,1)S(1)} %collective-permute-done.23.refs_0_, ...), custom_call_target="tpu_custom_call", output_to_operand_aliasing={{}: (0, {})} | custom-call | flops 1000000000 | bytes 10000000 | tf_op jit(solution)/shard_map/late/pallas_call | solution.py:438
  (74 shorter events, 10.7 us)
Async XLA Ops:
  5.0 10.3 %collective-permute-start.5 = (bf16[176,384]{1,0:T(8,128)(2,1)}, bf16[176,384]{1,0:T(8,128)(2,1)S(1)}, u32[]{:S(2)}, u32[]{:S(2)}) collective-permute-start(bf16[176,384]{1,0:T(8,128)(2,1)} %get-tuple-element.59), channel_id=1, source_target_pairs={{0,1},{1,0},{2,3},{3,2},{4,5},{5,4},{6,7},{7,6},{8,9},{9,8},{10,11... | collective-permute-start | bytes 405512 | tf_op jit(solution)/shard_map/ppermute | solution.py:325
  5.6 11.2 %collective-permute-start.6 = (bf16[176,384]{1,0:T(8,128)(2,1)}, bf16[176,384]{1,0:T(8,128)(2,1)S(1)}, u32[]{:S(2)}, u32[]{:S(2)}) collective-permute-start(bf16[176,384]{1,0:T(8,128)(2,1)} %get-tuple-element.60), channel_id=1, source_target_pairs={{0,2},{1,3},{2,0},{3,1},{4,6},{5,7},{6,4},{7,5},{8,10},{9,11},{10,... | collective-permute-start | bytes 405512 | tf_op jit(solution)/shard_map/ppermute | solution.py:325
  8.1 8.7 %collective-permute-start.7 = (bf16[176,384]{1,0:T(8,128)(2,1)}, bf16[176,384]{1,0:T(8,128)(2,1)S(1)}, u32[]{:S(2)}, u32[]{:S(2)}) collective-permute-start(bf16[176,384]{1,0:T(8,128)(2,1)} %get-tuple-element.61), channel_id=1, source_target_pairs={{0,3},{1,2},{2,1},{3,0},{4,7},{5,6},{6,5},{7,4},{8,11},{9,10},{10,... | collective-permute-start | bytes 405512 | tf_op jit(solution)/shard_map/ppermute | solution.py:325
  8.2 10.9 %collective-permute-start.2 = (bf16[176,384]{1,0:T(8,128)(2,1)}, bf16[176,384]{1,0:T(8,128)(2,1)S(1)}, u32[]{:S(2)}, u32[]{:S(2)}) collective-permute-start(bf16[176,384]{1,0:T(8,128)(2,1)} %get-tuple-element.54), channel_id=1, source_target_pairs={{0,1},{1,0},{2,3},{3,2},{4,5},{5,4},{6,7},{7,6},{8,9},{9,8},{10,11... | collective-permute-start | bytes 405512 | tf_op jit(solution)/shard_map/ppermute | solution.py:325
  13.7 40.0 %collective-permute-start = (bf16[2,320,384]{2,1,0:T(8,128)(2,1)S(1)}, bf16[2,320,384]{2,1,0:T(8,128)(2,1)S(1)}, u32[]{:S(2)}, u32[]{:S(2)}) collective-permute-start(bf16[2,320,384]{2,1,0:T(8,128)(2,1)S(1)} %get-tuple-element.46.pert), channel_id=1, source_target_pairs={{0,4},{4,0},{8,12},{12,8},{16,20},{20,16},{24,28},{28,24},{1,5},{5... | collective-permute-start | bytes 1474568 | tf_op jit(solution)/shard_map/ppermute | solution.py:325
  15.3 8.3 %collective-permute-start.3 = (bf16[176,384]{1,0:T(8,128)(2,1)S(1)}, bf16[176,384]{1,0:T(8,128)(2,1)S(1)}, u32[]{:S(2)}, u32[]{:S(2)}) collective-permute-start(bf16[176,384]{1,0:T(8,128)(2,1)S(1)} %copy-done.14), channel_id=1, source_target_pairs={{0,2},{1,3},{2,0},{3,1},{4,6},{5,7},{6,4},{7,5},{8,10},{9,11},{10,... | collective-permute-start | bytes 405512 | tf_op jit(solution)/shard_map/ppermute | solution.py:325
  16.8 8.0 %collective-permute-start.4 = (bf16[176,384]{1,0:T(8,128)(2,1)S(1)}, bf16[176,384]{1,0:T(8,128)(2,1)S(1)}, u32[]{:S(2)}, u32[]{:S(2)}) collective-permute-start(bf16[176,384]{1,0:T(8,128)(2,1)S(1)} %copy-done.13), channel_id=1, source_target_pairs={{0,3},{1,2},{2,1},{3,0},{4,7},{5,6},{6,5},{7,4},{8,11},{9,10},{10,... | collective-permute-start | bytes 405512 | tf_op jit(solution)/shard_map/ppermute | solution.py:325
  18.0 12.4 %collective-permute-start.8 = (bf16[160,384]{1,0:T(8,128)(2,1)S(1)}, bf16[160,384]{1,0:T(8,128)(2,1)S(1)}, u32[]{:S(2)}, u32[]{:S(2)}) collective-permute-start(bf16[160,384]{1,0:T(8,128)(2,1)S(1)} %get-tuple-element.62), channel_id=1, source_target_pairs={{0,4},{4,0},{8,12},{12,8},{16,20},{20,16},{24,28},{28,24},{1,5},{5... | collective-permute-start | bytes 368648 | tf_op jit(solution)/shard_map/ppermute | solution.py:325
  19.0 14.1 %collective-permute-start.10 = (bf16[160,384]{1,0:T(8,128)(2,1)S(1)}, bf16[160,384]{1,0:T(8,128)(2,1)S(1)}, u32[]{:S(2)}, u32[]{:S(2)}) collective-permute-start(bf16[160,384]{1,0:T(8,128)(2,1)S(1)} %get-tuple-element.65), channel_id=1, source_target_pairs={{0,4},{4,0},{8,12},{12,8},{16,20},{20,16},{24,28},{28,24},{1,5},{5... | collective-permute-start | bytes 368648 | tf_op jit(solution)/shard_map/ppermute | solution.py:325
  23.6 14.0 %collective-permute-start.1 = (bf16[10,40,90]{2,1,0:T(8,128)(2,1)S(1)}, bf16[10,40,90]{2,1,0:T(8,128)(2,1)S(1)}, u32[]{:S(2)}, u32[]{:S(2)}) collective-permute-start(bf16[10,40,90]{2,1,0:T(8,128)(2,1)S(1)} %get-tuple-element.49), channel_id=1, source_target_pairs={{0,4},{4,0},{8,12},{12,8},{16,20},{20,16},{24,28},{28,24},{1,5},{5... | collective-permute-start | bytes 216008 | tf_op jit(solution)/shard_map/ppermute | solution.py:325
  30.5 7.1 %collective-permute-start.9 = (bf16[80,384]{1,0:T(8,128)(2,1)S(1)}, bf16[80,384]{1,0:T(8,128)(2,1)S(1)}, u32[]{:S(2)}, u32[]{:S(2)}) collective-permute-start(bf16[80,384]{1,0:T(8,128)(2,1)S(1)} %get-tuple-element.64), channel_id=1, source_target_pairs={{0,8},{4,12},{8,0},{12,4},{16,24},{20,28},{24,16},{28,20},{1,9},{5... | collective-permute-start | bytes 184328 | tf_op jit(solution)/shard_map/ppermute | solution.py:325
  33.1 7.2 %collective-permute-start.11 = (bf16[80,384]{1,0:T(8,128)(2,1)S(1)}, bf16[80,384]{1,0:T(8,128)(2,1)S(1)}, u32[]{:S(2)}, u32[]{:S(2)}) collective-permute-start(bf16[80,384]{1,0:T(8,128)(2,1)S(1)} %get-tuple-element.66), channel_id=1, source_target_pairs={{0,16},{4,20},{8,24},{12,28},{16,0},{20,4},{24,8},{28,12},{1,17},{... | collective-permute-start | bytes 184328 | tf_op jit(solution)/shard_map/ppermute | solution.py:325
  36.2 6.0 %collective-permute-start.12 = (bf16[80,384]{1,0:T(8,128)(2,1)S(1)}, bf16[80,384]{1,0:T(8,128)(2,1)S(1)}, u32[]{:S(2)}, u32[]{:S(2)}) collective-permute-start(bf16[80,384]{1,0:T(8,128)(2,1)S(1)} %get-tuple-element.67), channel_id=1, source_target_pairs={{0,24},{4,28},{8,16},{12,20},{16,8},{20,12},{24,0},{28,4},{1,25},{... | collective-permute-start | bytes 184328 | tf_op jit(solution)/shard_map/ppermute | solution.py:325
  42.7 6.1 %collective-permute-start.15 = (bf16[80,384]{1,0:T(8,128)(2,1)S(1)}, bf16[80,384]{1,0:T(8,128)(2,1)S(1)}, u32[]{:S(2)}, u32[]{:S(2)}) collective-permute-start(bf16[80,384]{1,0:T(8,128)(2,1)S(1)} %shard_map.131.refs_0_), channel_id=1, source_target_pairs={{0,24},{4,28},{8,16},{12,20},{16,8},{20,12},{24,0},{28,4},{1,25},{... | collective-permute-start | bytes 184328 | tf_op jit(solution)/shard_map/ppermute | solution.py:325
  44.2 5.9 %collective-permute-start.14 = (bf16[80,384]{1,0:T(8,128)(2,1)S(1)}, bf16[80,384]{1,0:T(8,128)(2,1)S(1)}, u32[]{:S(2)}, u32[]{:S(2)}) collective-permute-start(bf16[80,384]{1,0:T(8,128)(2,1)S(1)} %shard_map.131.refs_0_), channel_id=1, source_target_pairs={{0,16},{4,20},{8,24},{12,28},{16,0},{20,4},{24,8},{28,12},{1,17},{... | collective-permute-start | bytes 184328 | tf_op jit(solution)/shard_map/ppermute | solution.py:325
  44.2 5.9 %collective-permute-start.13 = (bf16[80,384]{1,0:T(8,128)(2,1)S(1)}, bf16[80,384]{1,0:T(8,128)(2,1)S(1)}, u32[]{:S(2)}, u32[]{:S(2)}) collective-permute-start(bf16[80,384]{1,0:T(8,128)(2,1)S(1)} %shard_map.131.refs_0_), channel_id=1, source_target_pairs={{0,8},{4,12},{8,0},{12,4},{16,24},{20,28},{24,16},{28,20},{1,9},{5... | collective-permute-start | bytes 184328 | tf_op jit(solution)/shard_map/ppermute | solution.py:325
  50.1 23.3 %copy-start.2 = (bf16[2,4,80,720]{3,2,1,0:T(8,128)(2,1)S(1)}, bf16[2,4,80,720]{3,2,1,0:T(8,128)(2,1)}, u32[]{:S(2)}) copy-start(bf16[2,4,80,720]{3,2,1,0:T(8,128)(2,1)} %alpha.5) | copy-start | bytes 2764804
  50.1 23.3 %copy-start.11 = (bf16[4,80,720]{2,1,0:T(8,128)(2,1)S(1)}, bf16[4,80,720]{2,1,0:T(8,128)(2,1)}, u32[]{:S(2)}) copy-start(bf16[4,80,720]{2,1,0:T(8,128)(2,1)} %static.3) | copy-start | bytes 1382404
  51.4 7.7 %collective-permute-start.20 = (bf16[160,384]{1,0:T(8,128)(2,1)S(1)}, bf16[160,384]{1,0:T(8,128)(2,1)S(1)}, u32[]{:S(2)}, u32[]{:S(2)}) collective-permute-start(bf16[160,384]{1,0:T(8,128)(2,1)S(1)} %get-tuple-element.73), channel_id=1, source_target_pairs={{0,1},{1,0},{2,3},{3,2},{4,5},{5,4},{6,7},{7,6},{8,9},{9,8},{10,11... | collective-permute-start | bytes 368648 | tf_op jit(solution)/shard_map/ppermute | solution.py:417
  51.5 9.6 %collective-permute-start.21 = (bf16[160,384]{1,0:T(8,128)(2,1)S(1)}, bf16[160,384]{1,0:T(8,128)(2,1)S(1)}, u32[]{:S(2)}, u32[]{:S(2)}) collective-permute-start(bf16[160,384]{1,0:T(8,128)(2,1)S(1)} %get-tuple-element.74), channel_id=1, source_target_pairs={{0,2},{1,3},{2,0},{3,1},{4,6},{5,7},{6,4},{7,5},{8,10},{9,11},{10,... | collective-permute-start | bytes 368648 | tf_op jit(solution)/shard_map/ppermute | solution.py:417
  53.0 3.1 %collective-permute-start.27 = (bf16[80,384]{1,0:T(8,128)(2,1)S(1)}, bf16[80,384]{1,0:T(8,128)(2,1)S(1)}, u32[]{:S(2)}, u32[]{:S(2)}) collective-permute-start(bf16[80,384]{1,0:T(8,128)(2,1)S(1)} %get-tuple-element.82), channel_id=1, source_target_pairs={{0,1},{1,0},{2,3},{3,2},{4,5},{5,4},{6,7},{7,6},{8,9},{9,8},{10,11... | collective-permute-start | bytes 184328 | tf_op jit(solution)/shard_map/ppermute | solution.py:417
  53.2 5.9 %collective-permute-start.28 = (bf16[80,384]{1,0:T(8,128)(2,1)S(1)}, bf16[80,384]{1,0:T(8,128)(2,1)S(1)}, u32[]{:S(2)}, u32[]{:S(2)}) collective-permute-start(bf16[80,384]{1,0:T(8,128)(2,1)S(1)} %get-tuple-element.83), channel_id=1, source_target_pairs={{0,2},{1,3},{2,0},{3,1},{4,6},{5,7},{6,4},{7,5},{8,10},{9,11},{10,... | collective-permute-start | bytes 184328 | tf_op jit(solution)/shard_map/ppermute | solution.py:417
  53.7 8.8 %collective-permute-start.22 = (bf16[160,384]{1,0:T(8,128)(2,1)S(1)}, bf16[160,384]{1,0:T(8,128)(2,1)S(1)}, u32[]{:S(2)}, u32[]{:S(2)}) collective-permute-start(bf16[160,384]{1,0:T(8,128)(2,1)S(1)} %get-tuple-element.75), channel_id=1, source_target_pairs={{0,3},{1,2},{2,1},{3,0},{4,7},{5,6},{6,5},{7,4},{8,11},{9,10},{10,... | collective-permute-start | bytes 368648 | tf_op jit(solution)/shard_map/ppermute | solution.py:417
  56.1 7.0 %collective-permute-start.16 = (bf16[160,384]{1,0:T(8,128)(2,1)S(1)}, bf16[160,384]{1,0:T(8,128)(2,1)S(1)}, u32[]{:S(2)}, u32[]{:S(2)}) collective-permute-start(bf16[160,384]{1,0:T(8,128)(2,1)S(1)} %get-tuple-element.68), channel_id=1, source_target_pairs={{0,4},{1,5},{2,6},{3,7},{4,0},{5,1},{6,2},{7,3},{8,12},{9,13},{10,... | collective-permute-start | bytes 368648 | tf_op jit(solution)/shard_map/ppermute | solution.py:417
  59.0 10.9 %collective-permute-start.17 = (bf16[160,384]{1,0:T(8,128)(2,1)S(1)}, bf16[160,384]{1,0:T(8,128)(2,1)S(1)}, u32[]{:S(2)}, u32[]{:S(2)}) collective-permute-start(bf16[160,384]{1,0:T(8,128)(2,1)S(1)} %get-tuple-element.69), channel_id=1, source_target_pairs={{0,5},{1,4},{2,7},{3,6},{4,1},{5,0},{6,3},{7,2},{8,13},{9,12},{10,... | collective-permute-start | bytes 368648 | tf_op jit(solution)/shard_map/ppermute | solution.py:417
  59.0 11.4 %collective-permute-start.18 = (bf16[160,384]{1,0:T(8,128)(2,1)S(1)}, bf16[160,384]{1,0:T(8,128)(2,1)S(1)}, u32[]{:S(2)}, u32[]{:S(2)}) collective-permute-start(bf16[160,384]{1,0:T(8,128)(2,1)S(1)} %get-tuple-element.70), channel_id=1, source_target_pairs={{0,6},{1,7},{2,4},{3,5},{4,2},{5,3},{6,0},{7,1},{8,14},{9,15},{10,... | collective-permute-start | bytes 368648 | tf_op jit(solution)/shard_map/ppermute | solution.py:417
  61.1 10.9 %collective-permute-start.19 = (bf16[160,384]{1,0:T(8,128)(2,1)S(1)}, bf16[160,384]{1,0:T(8,128)(2,1)S(1)}, u32[]{:S(2)}, u32[]{:S(2)}) collective-permute-start(bf16[160,384]{1,0:T(8,128)(2,1)S(1)} %get-tuple-element.71), channel_id=1, source_target_pairs={{0,7},{1,6},{2,5},{3,4},{4,3},{5,2},{6,1},{7,0},{8,15},{9,14},{10,... | collective-permute-start | bytes 368648 | tf_op jit(solution)/shard_map/ppermute | solution.py:417
  62.5 13.3 %collective-permute-start.29 = (bf16[80,384]{1,0:T(8,128)(2,1)S(1)}, bf16[80,384]{1,0:T(8,128)(2,1)S(1)}, u32[]{:S(2)}, u32[]{:S(2)}) collective-permute-start(bf16[80,384]{1,0:T(8,128)(2,1)S(1)} %get-tuple-element.84), channel_id=1, source_target_pairs={{0,3},{1,2},{2,1},{3,0},{4,7},{5,6},{6,5},{7,4},{8,11},{9,10},{10,... | collective-permute-start | bytes 184328 | tf_op jit(solution)/shard_map/ppermute | solution.py:417
  63.2 12.6 %collective-permute-start.23 = (bf16[80,384]{1,0:T(8,128)(2,1)S(1)}, bf16[80,384]{1,0:T(8,128)(2,1)S(1)}, u32[]{:S(2)}, u32[]{:S(2)}) collective-permute-start(bf16[80,384]{1,0:T(8,128)(2,1)S(1)} %get-tuple-element.77), channel_id=1, source_target_pairs={{0,4},{1,5},{2,6},{3,7},{4,0},{5,1},{6,2},{7,3},{8,12},{9,13},{10,... | collective-permute-start | bytes 184328 | tf_op jit(solution)/shard_map/ppermute | solution.py:417
  69.9 5.9 %collective-permute-start.24 = (bf16[80,384]{1,0:T(8,128)(2,1)S(1)}, bf16[80,384]{1,0:T(8,128)(2,1)S(1)}, u32[]{:S(2)}, u32[]{:S(2)}) collective-permute-start(bf16[80,384]{1,0:T(8,128)(2,1)S(1)} %get-tuple-element.78), channel_id=1, source_target_pairs={{0,5},{1,4},{2,7},{3,6},{4,1},{5,0},{6,3},{7,2},{8,13},{9,12},{10,... | collective-permute-start | bytes 184328 | tf_op jit(solution)/shard_map/ppermute | solution.py:417
  70.4 5.6 %collective-permute-start.25 = (bf16[80,384]{1,0:T(8,128)(2,1)S(1)}, bf16[80,384]{1,0:T(8,128)(2,1)S(1)}, u32[]{:S(2)}, u32[]{:S(2)}) collective-permute-start(bf16[80,384]{1,0:T(8,128)(2,1)S(1)} %get-tuple-element.79), channel_id=1, source_target_pairs={{0,6},{1,7},{2,4},{3,5},{4,2},{5,3},{6,0},{7,1},{8,14},{9,15},{10,... | collective-permute-start | bytes 184328 | tf_op jit(solution)/shard_map/ppermute | solution.py:417
  71.9 4.6 %collective-permute-start.26 = (bf16[80,384]{1,0:T(8,128)(2,1)S(1)}, bf16[80,384]{1,0:T(8,128)(2,1)S(1)}, u32[]{:S(2)}, u32[]{:S(2)}) collective-permute-start(bf16[80,384]{1,0:T(8,128)(2,1)S(1)} %get-tuple-element.80), channel_id=1, source_target_pairs={{0,7},{1,6},{2,5},{3,4},{4,3},{5,2},{6,1},{7,0},{8,15},{9,14},{10,... | collective-permute-start | bytes 184328 | tf_op jit(solution)/shard_map/ppermute | solution.py:417
  (13 other events, 79.1 us)

commit v4 on v3

--- a/solution.py
+++ b/solution.py
@@ -10,7 +10,6 @@
 
 
 F32 = jnp.float32
-VMEM_BYTES = 67043328
 BF16 = jnp.bfloat16
 VMEM = pl.BlockSpec(memory_space=pltpu.VMEM)
 SMEM = pl.BlockSpec(memory_space=pltpu.SMEM)
@@ -25,7 +24,7 @@
     return jax.ShapeDtypeStruct(tuple(shape), dtype)
 
 
-def call(kernel, outs, *args, smem=0, scratch=(), flops=10**8, vmem=24 << 20, spaces=None):
+def call(kernel, outs, *args, smem=0, scratch=(), flops=10**8, vmem=14 << 20, spaces=None):
     size = sum(math.prod(a.shape) * a.dtype.itemsize for a in (*args, *outs))
     return pl.pallas_call(
         kernel,
@@ -123,12 +122,13 @@
     pick = one_hot((iota(shape, 1) == source) & (t < plan.count) & (rank % plan.copies == 0))
     lat_s[...] = dot_nt(l_buf[...], pick).astype(BF16)
     ys = []
-    for copy in copies[1:-1]:
+    half = members // 2
+    for copy in copies[1 : 2 + half]:
         copy.wait()
-    half = members // 2
     left = [a_buf[m, s] for s in range(species) for m in range(half)]
     ys.append(dot(jnp.concatenate(left, 0), r_buf[...]))
-    copies[-1].wait()
+    for copy in copies[2 + half :]:
+        copy.wait()
     left = []
     for s in range(species):
         left += [a_buf[m, s] for m in range(half, members)] + [dot(select, s_buf[s]).astype(BF16)]
@@ -191,7 +191,7 @@
             return tuple(total + scaled[s] * j[t] for total, (s, t) in zip(totals, pairs))
 
         zero = tuple(jnp.zeros((n, lon), F32) for _ in pairs)
-        sums = dict(zip(pairs, lax.fori_loop(0, channels, step, zero, unroll=8)))
+        sums = dict(zip(pairs, lax.fori_loop(0, channels, step, zero, unroll=16)))
         side = jnp.broadcast_to(rank & 1, (n, plan.width)) == 0
         for i, pair in enumerate(pairs):
             low, high = sums[pair][:, : plan.width], sums[pair][:, plan.width :]
@@ -337,11 +337,10 @@
     sent = struct((members * plan.rows + plan.extra, lanes), BF16)
     lat = pad_lat(lat_root, 0)
     lat_shapes = [struct((plan.padded, plan.lat), BF16), struct((plan.padded, bands * plan.extra), BF16)]
-    sizes = [sent.shape] * (2 * bands) + [(plan.padded, up(plan.lat, 128)), (plan.padded, 128)]
     *got, lat_k, lat_s = call(
         functools.partial(lon_kernel, plan), [sent] * (2 * bands) + lat_shapes,
         alpha, static_ctl, lon_root, lat, flops=10**9, spaces=[pltpu.HBM] * 4,
-        vmem=VMEM_BYTES - 2 * sum(math.prod(size) for size in sizes) - (3 << 17),
+        vmem=53 << 20,
         scratch=[
             pltpu.VMEM(lat.shape, BF16),
             pltpu.VMEM(alpha.shape, BF16),
@@ -418,7 +417,7 @@
                 backs[late, flip, k] = x
     early, last = [[backs[late, 1 - own, k] for own in range(2) for k in range(bands)] for late in range(2)]
 
-    params = pltpu.CompilerParams(vmem_limit_bytes=24 << 20)
+    params = pltpu.CompilerParams(vmem_limit_bytes=20 << 20)
     cost = pl.CostEstimate(flops=10**9, bytes_accessed=10**7, transcendentals=0)
     n_early = members - n_late
     hbm = pl.BlockSpec(memory_space=pltpu.HBM)

time: 78.8 us -> 77.3 us (0.981)
  local copies, waits for them, and re-layouts: 4.87 us -> 3.74 us
    unnamed x32 -> x28, local copies, waits for them, and re-layouts: 4.87 us -> 3.74 us
  transfers between devices with their start and end apart: 30 -> 30, of which waited for: 10 -> 10; matrix products, arithmetic and copies ran while one was open for 6% -> 4% of each run, Pallas kernels for 16% -> 17%
where the time goes in v4:
time: 77.3 us; the launch traced here: 77 us
  starting transfers between devices  34 us (44%)
  waiting for transfers between devices  19.5 us (25%)
  Pallas kernels  18.6 us (24%)
  local copies, waits for them, and re-layouts  3.74 us (5%)
  between operations  1.1 us (1%)
    ppermute x16, starting transfers between devices, send(): return lax.ppermute(x, axis, [(i, i ^ k) for i in range(n)])  20.7 us
    pallas_call x12, Pallas kernels, call(): pl.pallas_call(kernel, out_shape=outs, in_specs=[SMEM] * smem + [VMEM] *...  14.6 us
    ppermute x14, starting transfers between devices, shards(): x = lax.ppermute(x, ('mem', 'band'), swap)  13.3 us
    ppermute x16, waiting for transfers between devices, send(): return lax.ppermute(x, axis, [(i, i ^ k) for i in range(n)])  11.3 us
    ppermute x14, waiting for transfers between devices, shards(): x = lax.ppermute(x, ('mem', 'band'), swap)  8.18 us
    unnamed x28, local copies, waits for them, and re-layouts  3.74 us
    pallas_call x1, Pallas kernels, shards(): pl.pallas_call(functools.partial(early_kernel, plan), out_shape=[struct(a...  2.37 us
    pallas_call x1, Pallas kernels, shards(): pl.pallas_call(functools.partial(late_kernel, plan), out_shape=struct(alp...  1.62 us
  transfers between devices with their start and end apart: 30, of which 10 were waited for; matrix products, arithmetic and copies ran while one was open for 4% of the time, Pallas kernels for 17%

profile of v4, /device:TPU:0, one launch (start us, length us, event | category | flops | bytes accessed | tf_op | source)
XLA Modules:
  0.0 77.0 jit_solution(14367431919370592649)
XLA Ops:
  0.6 4.2 %shard_map.126 = (bf16[176,384]{1,0:T(8,128)(2,1)S(1)}, bf16[176,384]{1,0:T(8,128)(2,1)}, bf16[176,384]{1,0:T(8,128)(2,1)}, bf16[176,384]{1,0:T(8,128)(2,1)}, bf...) custom-call(bf16[2,4,80,720]{3,2,1,0:T(8,128)(2,1)} %alpha.5, ...), custom_call_target="tpu_custom_call" | custom-call | flops 1000000000 | bytes 3951104 | tf_op jit(solution)/shard_map/pallas_call | solution.py:29
  5.4 2.6 %collective-permute-start.6 = (bf16[176,384]{1,0:T(8,128)(2,1)}, bf16[176,384]{1,0:T(8,128)(2,1)S(1)}, u32[]{:S(2)}, u32[]{:S(2)}) collective-permute-start(bf16[176,384]{1,0:T(8,128)(2,1)} %get-tuple-element.60), channel_id=1, source_target_pairs={{0,2},{1,3},{2,0},{3,1},{4,6},{5,7},{6,4},{7,5},{8,10},{9,11},{10,... | collective-permute-start | bytes 405512 | tf_op jit(solution)/shard_map/ppermute | solution.py:325
  8.2 1.3 %copy.14.pert = bf16[2,4,320,180]{3,2,1,0:T(8,128)(2,1)S(1)} copy(bf16[2,4,320,180]{2,1,3,0:T(4,128)(2,1)S(1)} %copy-done.10) | data formatting | bytes 1843200 | tf_op args[2]
  9.5 1.9 %copy.15.std = f32[4,320,180]{2,1,0:T(8,128)S(1)} copy(f32[4,320,180]{1,0,2:T(4,128)} %param.14) | data formatting | bytes 1843200 | tf_op args[3]
  12.2 1.6 %collective-permute-start = (bf16[2,320,384]{2,1,0:T(8,128)(2,1)S(1)}, bf16[2,320,384]{2,1,0:T(8,128)(2,1)S(1)}, u32[]{:S(2)}, u32[]{:S(2)}) collective-permute-start(bf16[2,320,384]{2,1,0:T(8,128)(2,1)S(1)} %get-tuple-element.46.pert), channel_id=1, source_target_pairs={{0,4},{4,0},{8,12},{12,8},{16,20},{20,16},{24,28},{28,24},{1,5},{5... | collective-permute-start | bytes 1474568 | tf_op jit(solution)/shard_map/ppermute | solution.py:325
  13.9 1.5 %collective-permute-start.3 = (bf16[176,384]{1,0:T(8,128)(2,1)S(1)}, bf16[176,384]{1,0:T(8,128)(2,1)S(1)}, u32[]{:S(2)}, u32[]{:S(2)}) collective-permute-start(bf16[176,384]{1,0:T(8,128)(2,1)S(1)} %copy-done.12), channel_id=1, source_target_pairs={{0,2},{1,3},{2,0},{3,1},{4,6},{5,7},{6,4},{7,5},{8,10},{9,11},{10,... | collective-permute-start | bytes 405512 | tf_op jit(solution)/shard_map/ppermute | solution.py:325
  15.4 1.2 %shard_map.128 = (bf16[160,384]{1,0:T(8,128)(2,1)S(1)}, bf16[160,384]{1,0:T(8,128)(2,1)S(1)}) custom-call(s32[16]{0:T(128)S(1)} %copy-done.5, bf16[320,320]{1,0:T(8,128)(2,1)S(1)} %copy-done.3, bf16[320,64]{1,0:T(8,128)(2,1)S(1)} %get-tuple-element.51.lat_s, bf16[2,320,384]{2,1,0:T(8,128)(2,1)S(1)} %get-tuple-element.46.pert, ...), custom_call_target="tpu_custom_call" | custom-call | flops 100000000 | bytes 2015296 | tf_op jit(solution)/shard_map/pallas_call | solution.py:29
  16.6 1.1 %collective-permute-start.8 = (bf16[160,384]{1,0:T(8,128)(2,1)S(1)}, bf16[160,384]{1,0:T(8,128)(2,1)S(1)}, u32[]{:S(2)}, u32[]{:S(2)}) collective-permute-start(bf16[160,384]{1,0:T(8,128)(2,1)S(1)} %get-tuple-element.62), channel_id=1, source_target_pairs={{0,4},{4,0},{8,12},{12,8},{16,20},{20,16},{24,28},{28,24},{1,5},{5... | collective-permute-start | bytes 368648 | tf_op jit(solution)/shard_map/ppermute | solution.py:325
  19.5 2.8 %shard_map.125 = (bf16[10,40,90]{2,1,0:T(8,128)(2,1)S(1)}, f32[10,40,90]{2,1,0:T(8,128)S(1)}) custom-call(f32[32]{0:T(128)S(1)} %copy-done.6, bf16[32,4,40,180]{3,2,1,0:T(8,128)(2,1)S(1)} %copy-done, s32[40,180]{1,0:T(8,128)S(1)} %copy-done.4, s32[32,40,180]{2,1,0:T(8,128)S(1)} %copy-done.1), custom_call_target="tpu_custom_call" | custom-call | flops 100000000 | bytes 3009728 | tf_op jit(solution)/shard_map/pallas_call | solution.py:29
  24.5 4.5 %collective-permute-done.8.got = bf16[160,384]{1,0:T(8,128)(2,1)S(1)} collective-permute-done((bf16[160,384]{1,0:T(8,128)(2,1)S(1)}, bf16[160,384]{1,0:T(8,128)(2,1)S(1)}, u32[]{:S(2)}, u32[]{:S(2)}) %collective-permute-start.8) | collective-permute-done | bytes 122912 | tf_op jit(solution)/shard_map/ppermute | solution.py:325
  29.1 2.1 %collective-permute-start.9 = (bf16[80,384]{1,0:T(8,128)(2,1)S(1)}, bf16[80,384]{1,0:T(8,128)(2,1)S(1)}, u32[]{:S(2)}, u32[]{:S(2)}) collective-permute-start(bf16[80,384]{1,0:T(8,128)(2,1)S(1)} %get-tuple-element.64), channel_id=1, source_target_pairs={{0,8},{4,12},{8,0},{12,4},{16,24},{20,28},{24,16},{28,20},{1,9},{5... | collective-permute-start | bytes 184328 | tf_op jit(solution)/shard_map/ppermute | solution.py:325
  31.7 3.1 %collective-permute-start.11 = (bf16[80,384]{1,0:T(8,128)(2,1)S(1)}, bf16[80,384]{1,0:T(8,128)(2,1)S(1)}, u32[]{:S(2)}, u32[]{:S(2)}) collective-permute-start(bf16[80,384]{1,0:T(8,128)(2,1)S(1)} %get-tuple-element.66), channel_id=1, source_target_pairs={{0,16},{4,20},{8,24},{12,28},{16,0},{20,4},{24,8},{28,12},{1,17},{... | collective-permute-start | bytes 184328 | tf_op jit(solution)/shard_map/ppermute | solution.py:325
  34.8 1.3 %collective-permute-start.12 = (bf16[80,384]{1,0:T(8,128)(2,1)S(1)}, bf16[80,384]{1,0:T(8,128)(2,1)S(1)}, u32[]{:S(2)}, u32[]{:S(2)}) collective-permute-start(bf16[80,384]{1,0:T(8,128)(2,1)S(1)} %get-tuple-element.67), channel_id=1, source_target_pairs={{0,24},{4,28},{8,16},{12,20},{16,8},{20,12},{24,0},{28,4},{1,25},{... | collective-permute-start | bytes 184328 | tf_op jit(solution)/shard_map/ppermute | solution.py:325
  36.2 2.7 %collective-permute-done.11.refs_1_ = bf16[80,384]{1,0:T(8,128)(2,1)S(1)} collective-permute-done((bf16[80,384]{1,0:T(8,128)(2,1)S(1)}, bf16[80,384]{1,0:T(8,128)(2,1)S(1)}, u32[]{:S(2)}, u32[]{:S(2)}) %collective-permute-start.11) | collective-permute-done | bytes 61472 | tf_op jit(solution)/shard_map/ppermute | solution.py:325
  38.9 1.9 %collective-permute-done.12.refs_2_ = bf16[80,384]{1,0:T(8,128)(2,1)S(1)} collective-permute-done((bf16[80,384]{1,0:T(8,128)(2,1)S(1)}, bf16[80,384]{1,0:T(8,128)(2,1)S(1)}, u32[]{:S(2)}, u32[]{:S(2)}) %collective-permute-start.12) | collective-permute-done | bytes 61472 | tf_op jit(solution)/shard_map/ppermute | solution.py:325
  41.3 1.5 %collective-permute-start.15 = (bf16[80,384]{1,0:T(8,128)(2,1)S(1)}, bf16[80,384]{1,0:T(8,128)(2,1)S(1)}, u32[]{:S(2)}, u32[]{:S(2)}) collective-permute-start(bf16[80,384]{1,0:T(8,128)(2,1)S(1)} %shard_map.131.refs_0_), channel_id=1, source_target_pairs={{0,24},{4,28},{8,16},{12,20},{16,8},{20,12},{24,0},{28,4},{1,25},{... | collective-permute-start | bytes 184328 | tf_op jit(solution)/shard_map/ppermute | solution.py:325
  42.8 2.9 %collective-permute-start.13 = (bf16[80,384]{1,0:T(8,128)(2,1)S(1)}, bf16[80,384]{1,0:T(8,128)(2,1)S(1)}, u32[]{:S(2)}, u32[]{:S(2)}) collective-permute-start(bf16[80,384]{1,0:T(8,128)(2,1)S(1)} %shard_map.131.refs_0_), channel_id=1, source_target_pairs={{0,8},{4,12},{8,0},{12,4},{16,24},{20,28},{24,16},{28,20},{1,9},{5... | collective-permute-start | bytes 184328 | tf_op jit(solution)/shard_map/ppermute | solution.py:325
  45.7 1.3 %shard_map.122 = (bf16[720,768]{1,0:T(8,128)(2,1)S(1)}, bf16[320,320]{1,0:T(8,128)(2,1)S(1)}) custom-call(bf16[720,720]{1,0:T(8,128)(2,1)S(1)} %copy-done.7, bf16[320,320]{1,0:T(8,128)(2,1)S(1)} %copy-done.9), custom_call_target="tpu_custom_call" | custom-call | flops 1000000000 | bytes 2552320 | tf_op jit(solution)/shard_map/pallas_call | solution.py:29
  47.4 1.3 %collective-permute-done.14.refs_2_ = bf16[80,384]{1,0:T(8,128)(2,1)S(1)} collective-permute-done((bf16[80,384]{1,0:T(8,128)(2,1)S(1)}, bf16[80,384]{1,0:T(8,128)(2,1)S(1)}, u32[]{:S(2)}, u32[]{:S(2)}) %collective-permute-start.14) | collective-permute-done | bytes 61472 | tf_op jit(solution)/shard_map/ppermute | solution.py:325
  48.7 1.3 %shard_map.133 = (bf16[160,384]{1,0:T(8,128)(2,1)S(1)}, bf16[160,384]{1,0:T(8,128)(2,1)S(1)}, bf16[160,384]{1,0:T(8,128)(2,1)S(1)}, bf16[160,384]{1,0:T(8,128)(2...) custom-call(s32[16]{0:T(128)S(1)} %copy-done.5, ...), custom_call_target="tpu_custom_call" | custom-call | flops 100000000 | bytes 2170944 | tf_op jit(solution)/shard_map/pallas_call | solution.py:29
  50.0 1.6 %collective-permute-start.21 = (bf16[160,384]{1,0:T(8,128)(2,1)S(1)}, bf16[160,384]{1,0:T(8,128)(2,1)S(1)}, u32[]{:S(2)}, u32[]{:S(2)}) collective-permute-start(bf16[160,384]{1,0:T(8,128)(2,1)S(1)} %get-tuple-element.74), channel_id=1, source_target_pairs={{0,2},{1,3},{2,0},{3,1},{4,6},{5,7},{6,4},{7,5},{8,10},{9,11},{10,... | collective-permute-start | bytes 368648 | tf_op jit(solution)/shard_map/ppermute | solution.py:416
  52.3 1.2 %collective-permute-start.22 = (bf16[160,384]{1,0:T(8,128)(2,1)S(1)}, bf16[160,384]{1,0:T(8,128)(2,1)S(1)}, u32[]{:S(2)}, u32[]{:S(2)}) collective-permute-start(bf16[160,384]{1,0:T(8,128)(2,1)S(1)} %get-tuple-element.75), channel_id=1, source_target_pairs={{0,3},{1,2},{2,1},{3,0},{4,7},{5,6},{6,5},{7,4},{8,11},{9,10},{10,... | collective-permute-start | bytes 368648 | tf_op jit(solution)/shard_map/ppermute | solution.py:416
  53.5 1.3 %shard_map.132 = (bf16[160,384]{1,0:T(8,128)(2,1)S(1)}, bf16[160,384]{1,0:T(8,128)(2,1)S(1)}, bf16[160,384]{1,0:T(8,128)(2,1)S(1)}, bf16[160,384]{1,0:T(8,128)(2...) custom-call(s32[16]{0:T(128)S(1)} %copy-done.5, ...), custom_call_target="tpu_custom_call" | custom-call | flops 100000000 | bytes 2170944 | tf_op jit(solution)/shard_map/pallas_call | solution.py:29
  54.7 1.2 %collective-permute-start.16 = (bf16[160,384]{1,0:T(8,128)(2,1)S(1)}, bf16[160,384]{1,0:T(8,128)(2,1)S(1)}, u32[]{:S(2)}, u32[]{:S(2)}) collective-permute-start(bf16[160,384]{1,0:T(8,128)(2,1)S(1)} %get-tuple-element.68), channel_id=1, source_target_pairs={{0,4},{1,5},{2,6},{3,7},{4,0},{5,1},{6,2},{7,3},{8,12},{9,13},{10,... | collective-permute-start | bytes 368648 | tf_op jit(solution)/shard_map/ppermute | solution.py:416
  55.9 1.7 %collective-permute-done.28.refs_6_ = bf16[80,384]{1,0:T(8,128)(2,1)S(1)} collective-permute-done((bf16[80,384]{1,0:T(8,128)(2,1)S(1)}, bf16[80,384]{1,0:T(8,128)(2,1)S(1)}, u32[]{:S(2)}, u32[]{:S(2)}) %collective-permute-start.28) | collective-permute-done | bytes 61472 | tf_op jit(solution)/shard_map/ppermute | solution.py:416
  57.6 2.0 %collective-permute-start.18 = (bf16[160,384]{1,0:T(8,128)(2,1)S(1)}, bf16[160,384]{1,0:T(8,128)(2,1)S(1)}, u32[]{:S(2)}, u32[]{:S(2)}) collective-permute-start(bf16[160,384]{1,0:T(8,128)(2,1)S(1)} %get-tuple-element.70), channel_id=1, source_target_pairs={{0,6},{1,7},{2,4},{3,5},{4,2},{5,3},{6,0},{7,1},{8,14},{9,15},{10,... | collective-permute-start | bytes 368648 | tf_op jit(solution)/shard_map/ppermute | solution.py:416
  59.6 1.4 %collective-permute-start.19 = (bf16[160,384]{1,0:T(8,128)(2,1)S(1)}, bf16[160,384]{1,0:T(8,128)(2,1)S(1)}, u32[]{:S(2)}, u32[]{:S(2)}) collective-permute-start(bf16[160,384]{1,0:T(8,128)(2,1)S(1)} %get-tuple-element.71), channel_id=1, source_target_pairs={{0,7},{1,6},{2,5},{3,4},{4,3},{5,2},{6,1},{7,0},{8,15},{9,14},{10,... | collective-permute-start | bytes 368648 | tf_op jit(solution)/shard_map/ppermute | solution.py:416
  62.9 5.6 %collective-permute-done.17.refs_1_ = bf16[160,384]{1,0:T(8,128)(2,1)S(1)} collective-permute-done((bf16[160,384]{1,0:T(8,128)(2,1)S(1)}, bf16[160,384]{1,0:T(8,128)(2,1)S(1)}, u32[]{:S(2)}, u32[]{:S(2)}) %collective-permute-start.17) | collective-permute-done | bytes 122912 | tf_op jit(solution)/shard_map/ppermute | solution.py:416
  69.0 1.5 %collective-permute-start.25 = (bf16[80,384]{1,0:T(8,128)(2,1)S(1)}, bf16[80,384]{1,0:T(8,128)(2,1)S(1)}, u32[]{:S(2)}, u32[]{:S(2)}) collective-permute-start(bf16[80,384]{1,0:T(8,128)(2,1)S(1)} %get-tuple-element.79), channel_id=1, source_target_pairs={{0,6},{1,7},{2,4},{3,5},{4,2},{5,3},{6,0},{7,1},{8,14},{9,15},{10,... | collective-permute-start | bytes 184328 | tf_op jit(solution)/shard_map/ppermute | solution.py:416
  70.5 1.4 %collective-permute-start.26 = (bf16[80,384]{1,0:T(8,128)(2,1)S(1)}, bf16[80,384]{1,0:T(8,128)(2,1)S(1)}, u32[]{:S(2)}, u32[]{:S(2)}) collective-permute-start(bf16[80,384]{1,0:T(8,128)(2,1)S(1)} %get-tuple-element.80), channel_id=1, source_target_pairs={{0,7},{1,6},{2,5},{3,4},{4,3},{5,2},{6,1},{7,0},{8,15},{9,14},{10,... | collective-permute-start | bytes 184328 | tf_op jit(solution)/shard_map/ppermute | solution.py:416
  72.0 2.4 %early.1 = (f32[2,4,80,720]{3,2,1,0:T(8,128)}, f32[4,80,720]{2,1,0:T(8,128)}) custom-call(bf16[2,4,80,720]{3,2,1,0:T(8,128)(2,1)S(1)} %copy-done.2, bf16[4,80,720]{2,1,0:T(8,128)(2,1)S(1)} %copy-done.8, bf16[720,768]{1,0:T(8,128)(2,1)S(1)} %get-tuple-element.44.w, bf16[160,384]{1,0:T(8,128)(2,1)S(1)} %collective-permute-done.16.refs_0_, ...), custom_call_target="tpu_custom_call" | custom-call | flops 1000000000 | bytes 10000000 | tf_op jit(solution)/shard_map/early/pallas_call | solution.py:425
  75.2 1.6 %late.1 = f32[2,4,80,720]{3,2,1,0:T(8,128)} custom-call(f32[2,4,80,720]{3,2,1,0:T(8,128)} %get-tuple-element.76._, bf16[2,4,80,720]{3,2,1,0:T(8,128)(2,1)S(1)} %copy-done.2, bf16[720,768]{1,0:T(8,128)(2,1)S(1)} %get-tuple-element.44.w, bf16[80,384]{1,0:T(8,128)(2,1)S(1)} %collective-permute-done.23.refs_0_, ...), custom_call_target="tpu_custom_call", output_to_operand_aliasing={{}: (0, {})} | custom-call | flops 1000000000 | bytes 10000000 | tf_op jit(solution)/shard_map/late/pallas_call | solution.py:437
  (70 shorter events, 10.8 us)
Async XLA Ops:
  4.9 9.0 %collective-permute-start.5 = (bf16[176,384]{1,0:T(8,128)(2,1)}, bf16[176,384]{1,0:T(8,128)(2,1)S(1)}, u32[]{:S(2)}, u32[]{:S(2)}) collective-permute-start(bf16[176,384]{1,0:T(8,128)(2,1)} %get-tuple-element.59), channel_id=1, source_target_pairs={{0,1},{1,0},{2,3},{3,2},{4,5},{5,4},{6,7},{7,6},{8,9},{9,8},{10,11... | collective-permute-start | bytes 405512 | tf_op jit(solution)/shard_map/ppermute | solution.py:325
  5.4 9.9 %collective-permute-start.6 = (bf16[176,384]{1,0:T(8,128)(2,1)}, bf16[176,384]{1,0:T(8,128)(2,1)S(1)}, u32[]{:S(2)}, u32[]{:S(2)}) collective-permute-start(bf16[176,384]{1,0:T(8,128)(2,1)} %get-tuple-element.60), channel_id=1, source_target_pairs={{0,2},{1,3},{2,0},{3,1},{4,6},{5,7},{6,4},{7,5},{8,10},{9,11},{10,... | collective-permute-start | bytes 405512 | tf_op jit(solution)/shard_map/ppermute | solution.py:325
  8.0 7.4 %collective-permute-start.7 = (bf16[176,384]{1,0:T(8,128)(2,1)}, bf16[176,384]{1,0:T(8,128)(2,1)S(1)}, u32[]{:S(2)}, u32[]{:S(2)}) collective-permute-start(bf16[176,384]{1,0:T(8,128)(2,1)} %get-tuple-element.61), channel_id=1, source_target_pairs={{0,3},{1,2},{2,1},{3,0},{4,7},{5,6},{6,5},{7,4},{8,11},{9,10},{10,... | collective-permute-start | bytes 405512 | tf_op jit(solution)/shard_map/ppermute | solution.py:325
  8.0 9.7 %collective-permute-start.2 = (bf16[176,384]{1,0:T(8,128)(2,1)}, bf16[176,384]{1,0:T(8,128)(2,1)S(1)}, u32[]{:S(2)}, u32[]{:S(2)}) collective-permute-start(bf16[176,384]{1,0:T(8,128)(2,1)} %get-tuple-element.54), channel_id=1, source_target_pairs={{0,1},{1,0},{2,3},{3,2},{4,5},{5,4},{6,7},{7,6},{8,9},{9,8},{10,11... | collective-permute-start | bytes 405512 | tf_op jit(solution)/shard_map/ppermute | solution.py:325
  12.2 40.0 %collective-permute-start = (bf16[2,320,384]{2,1,0:T(8,128)(2,1)S(1)}, bf16[2,320,384]{2,1,0:T(8,128)(2,1)S(1)}, u32[]{:S(2)}, u32[]{:S(2)}) collective-permute-start(bf16[2,320,384]{2,1,0:T(8,128)(2,1)S(1)} %get-tuple-element.46.pert), channel_id=1, source_target_pairs={{0,4},{4,0},{8,12},{12,8},{16,20},{20,16},{24,28},{28,24},{1,5},{5... | collective-permute-start | bytes 1474568 | tf_op jit(solution)/shard_map/ppermute | solution.py:325
  13.9 8.4 %collective-permute-start.3 = (bf16[176,384]{1,0:T(8,128)(2,1)S(1)}, bf16[176,384]{1,0:T(8,128)(2,1)S(1)}, u32[]{:S(2)}, u32[]{:S(2)}) collective-permute-start(bf16[176,384]{1,0:T(8,128)(2,1)S(1)} %copy-done.12), channel_id=1, source_target_pairs={{0,2},{1,3},{2,0},{3,1},{4,6},{5,7},{6,4},{7,5},{8,10},{9,11},{10,... | collective-permute-start | bytes 405512 | tf_op jit(solution)/shard_map/ppermute | solution.py:325
  15.4 8.0 %collective-permute-start.4 = (bf16[176,384]{1,0:T(8,128)(2,1)S(1)}, bf16[176,384]{1,0:T(8,128)(2,1)S(1)}, u32[]{:S(2)}, u32[]{:S(2)}) collective-permute-start(bf16[176,384]{1,0:T(8,128)(2,1)S(1)} %copy-done.11), channel_id=1, source_target_pairs={{0,3},{1,2},{2,1},{3,0},{4,7},{5,6},{6,5},{7,4},{8,11},{9,10},{10,... | collective-permute-start | bytes 405512 | tf_op jit(solution)/shard_map/ppermute | solution.py:325
  16.6 12.4 %collective-permute-start.8 = (bf16[160,384]{1,0:T(8,128)(2,1)S(1)}, bf16[160,384]{1,0:T(8,128)(2,1)S(1)}, u32[]{:S(2)}, u32[]{:S(2)}) collective-permute-start(bf16[160,384]{1,0:T(8,128)(2,1)S(1)} %get-tuple-element.62), channel_id=1, source_target_pairs={{0,4},{4,0},{8,12},{12,8},{16,20},{20,16},{24,28},{28,24},{1,5},{5... | collective-permute-start | bytes 368648 | tf_op jit(solution)/shard_map/ppermute | solution.py:325
  17.7 13.9 %collective-permute-start.10 = (bf16[160,384]{1,0:T(8,128)(2,1)S(1)}, bf16[160,384]{1,0:T(8,128)(2,1)S(1)}, u32[]{:S(2)}, u32[]{:S(2)}) collective-permute-start(bf16[160,384]{1,0:T(8,128)(2,1)S(1)} %get-tuple-element.65), channel_id=1, source_target_pairs={{0,4},{4,0},{8,12},{12,8},{16,20},{20,16},{24,28},{28,24},{1,5},{5... | collective-permute-start | bytes 368648 | tf_op jit(solution)/shard_map/ppermute | solution.py:325
  22.3 13.9 %collective-permute-start.1 = (bf16[10,40,90]{2,1,0:T(8,128)(2,1)S(1)}, bf16[10,40,90]{2,1,0:T(8,128)(2,1)S(1)}, u32[]{:S(2)}, u32[]{:S(2)}) collective-permute-start(bf16[10,40,90]{2,1,0:T(8,128)(2,1)S(1)} %get-tuple-element.49), channel_id=1, source_target_pairs={{0,4},{4,0},{8,12},{12,8},{16,20},{20,16},{24,28},{28,24},{1,5},{5... | collective-permute-start | bytes 216008 | tf_op jit(solution)/shard_map/ppermute | solution.py:325
  29.1 7.1 %collective-permute-start.9 = (bf16[80,384]{1,0:T(8,128)(2,1)S(1)}, bf16[80,384]{1,0:T(8,128)(2,1)S(1)}, u32[]{:S(2)}, u32[]{:S(2)}) collective-permute-start(bf16[80,384]{1,0:T(8,128)(2,1)S(1)} %get-tuple-element.64), channel_id=1, source_target_pairs={{0,8},{4,12},{8,0},{12,4},{16,24},{20,28},{24,16},{28,20},{1,9},{5... | collective-permute-start | bytes 184328 | tf_op jit(solution)/shard_map/ppermute | solution.py:325
  31.7 7.2 %collective-permute-start.11 = (bf16[80,384]{1,0:T(8,128)(2,1)S(1)}, bf16[80,384]{1,0:T(8,128)(2,1)S(1)}, u32[]{:S(2)}, u32[]{:S(2)}) collective-permute-start(bf16[80,384]{1,0:T(8,128)(2,1)S(1)} %get-tuple-element.66), channel_id=1, source_target_pairs={{0,16},{4,20},{8,24},{12,28},{16,0},{20,4},{24,8},{28,12},{1,17},{... | collective-permute-start | bytes 184328 | tf_op jit(solution)/shard_map/ppermute | solution.py:325
  34.8 6.0 %collective-permute-start.12 = (bf16[80,384]{1,0:T(8,128)(2,1)S(1)}, bf16[80,384]{1,0:T(8,128)(2,1)S(1)}, u32[]{:S(2)}, u32[]{:S(2)}) collective-permute-start(bf16[80,384]{1,0:T(8,128)(2,1)S(1)} %get-tuple-element.67), channel_id=1, source_target_pairs={{0,24},{4,28},{8,16},{12,20},{16,8},{20,12},{24,0},{28,4},{1,25},{... | collective-permute-start | bytes 184328 | tf_op jit(solution)/shard_map/ppermute | solution.py:325
  41.3 6.1 %collective-permute-start.15 = (bf16[80,384]{1,0:T(8,128)(2,1)S(1)}, bf16[80,384]{1,0:T(8,128)(2,1)S(1)}, u32[]{:S(2)}, u32[]{:S(2)}) collective-permute-start(bf16[80,384]{1,0:T(8,128)(2,1)S(1)} %shard_map.131.refs_0_), channel_id=1, source_target_pairs={{0,24},{4,28},{8,16},{12,20},{16,8},{20,12},{24,0},{28,4},{1,25},{... | collective-permute-start | bytes 184328 | tf_op jit(solution)/shard_map/ppermute | solution.py:325
  42.8 5.9 %collective-permute-start.14 = (bf16[80,384]{1,0:T(8,128)(2,1)S(1)}, bf16[80,384]{1,0:T(8,128)(2,1)S(1)}, u32[]{:S(2)}, u32[]{:S(2)}) collective-permute-start(bf16[80,384]{1,0:T(8,128)(2,1)S(1)} %shard_map.131.refs_0_), channel_id=1, source_target_pairs={{0,16},{4,20},{8,24},{12,28},{16,0},{20,4},{24,8},{28,12},{1,17},{... | collective-permute-start | bytes 184328 | tf_op jit(solution)/shard_map/ppermute | solution.py:325
  42.8 5.9 %collective-permute-start.13 = (bf16[80,384]{1,0:T(8,128)(2,1)S(1)}, bf16[80,384]{1,0:T(8,128)(2,1)S(1)}, u32[]{:S(2)}, u32[]{:S(2)}) collective-permute-start(bf16[80,384]{1,0:T(8,128)(2,1)S(1)} %shard_map.131.refs_0_), channel_id=1, source_target_pairs={{0,8},{4,12},{8,0},{12,4},{16,24},{20,28},{24,16},{28,20},{1,9},{5... | collective-permute-start | bytes 184328 | tf_op jit(solution)/shard_map/ppermute | solution.py:325
  48.7 23.3 %copy-start.2 = (bf16[2,4,80,720]{3,2,1,0:T(8,128)(2,1)S(1)}, bf16[2,4,80,720]{3,2,1,0:T(8,128)(2,1)}, u32[]{:S(2)}) copy-start(bf16[2,4,80,720]{3,2,1,0:T(8,128)(2,1)} %alpha.5) | copy-start | bytes 2764804
  48.7 23.3 %copy-start.8 = (bf16[4,80,720]{2,1,0:T(8,128)(2,1)S(1)}, bf16[4,80,720]{2,1,0:T(8,128)(2,1)}, u32[]{:S(2)}) copy-start(bf16[4,80,720]{2,1,0:T(8,128)(2,1)} %static.3) | copy-start | bytes 1382404
  50.0 7.7 %collective-permute-start.20 = (bf16[160,384]{1,0:T(8,128)(2,1)S(1)}, bf16[160,384]{1,0:T(8,128)(2,1)S(1)}, u32[]{:S(2)}, u32[]{:S(2)}) collective-permute-start(bf16[160,384]{1,0:T(8,128)(2,1)S(1)} %get-tuple-element.73), channel_id=1, source_target_pairs={{0,1},{1,0},{2,3},{3,2},{4,5},{5,4},{6,7},{7,6},{8,9},{9,8},{10,11... | collective-permute-start | bytes 368648 | tf_op jit(solution)/shard_map/ppermute | solution.py:416
  50.0 9.6 %collective-permute-start.21 = (bf16[160,384]{1,0:T(8,128)(2,1)S(1)}, bf16[160,384]{1,0:T(8,128)(2,1)S(1)}, u32[]{:S(2)}, u32[]{:S(2)}) collective-permute-start(bf16[160,384]{1,0:T(8,128)(2,1)S(1)} %get-tuple-element.74), channel_id=1, source_target_pairs={{0,2},{1,3},{2,0},{3,1},{4,6},{5,7},{6,4},{7,5},{8,10},{9,11},{10,... | collective-permute-start | bytes 368648 | tf_op jit(solution)/shard_map/ppermute | solution.py:416
  51.6 3.1 %collective-permute-start.27 = (bf16[80,384]{1,0:T(8,128)(2,1)S(1)}, bf16[80,384]{1,0:T(8,128)(2,1)S(1)}, u32[]{:S(2)}, u32[]{:S(2)}) collective-permute-start(bf16[80,384]{1,0:T(8,128)(2,1)S(1)} %get-tuple-element.82), channel_id=1, source_target_pairs={{0,1},{1,0},{2,3},{3,2},{4,5},{5,4},{6,7},{7,6},{8,9},{9,8},{10,11... | collective-permute-start | bytes 184328 | tf_op jit(solution)/shard_map/ppermute | solution.py:416
  51.7 5.9 %collective-permute-start.28 = (bf16[80,384]{1,0:T(8,128)(2,1)S(1)}, bf16[80,384]{1,0:T(8,128)(2,1)S(1)}, u32[]{:S(2)}, u32[]{:S(2)}) collective-permute-start(bf16[80,384]{1,0:T(8,128)(2,1)S(1)} %get-tuple-element.83), channel_id=1, source_target_pairs={{0,2},{1,3},{2,0},{3,1},{4,6},{5,7},{6,4},{7,5},{8,10},{9,11},{10,... | collective-permute-start | bytes 184328 | tf_op jit(solution)/shard_map/ppermute | solution.py:416
  52.3 8.8 %collective-permute-start.22 = (bf16[160,384]{1,0:T(8,128)(2,1)S(1)}, bf16[160,384]{1,0:T(8,128)(2,1)S(1)}, u32[]{:S(2)}, u32[]{:S(2)}) collective-permute-start(bf16[160,384]{1,0:T(8,128)(2,1)S(1)} %get-tuple-element.75), channel_id=1, source_target_pairs={{0,3},{1,2},{2,1},{3,0},{4,7},{5,6},{6,5},{7,4},{8,11},{9,10},{10,... | collective-permute-start | bytes 368648 | tf_op jit(solution)/shard_map/ppermute | solution.py:416
  54.7 7.0 %collective-permute-start.16 = (bf16[160,384]{1,0:T(8,128)(2,1)S(1)}, bf16[160,384]{1,0:T(8,128)(2,1)S(1)}, u32[]{:S(2)}, u32[]{:S(2)}) collective-permute-start(bf16[160,384]{1,0:T(8,128)(2,1)S(1)} %get-tuple-element.68), channel_id=1, source_target_pairs={{0,4},{1,5},{2,6},{3,7},{4,0},{5,1},{6,2},{7,3},{8,12},{9,13},{10,... | collective-permute-start | bytes 368648 | tf_op jit(solution)/shard_map/ppermute | solution.py:416
  57.6 10.9 %collective-permute-start.17 = (bf16[160,384]{1,0:T(8,128)(2,1)S(1)}, bf16[160,384]{1,0:T(8,128)(2,1)S(1)}, u32[]{:S(2)}, u32[]{:S(2)}) collective-permute-start(bf16[160,384]{1,0:T(8,128)(2,1)S(1)} %get-tuple-element.69), channel_id=1, source_target_pairs={{0,5},{1,4},{2,7},{3,6},{4,1},{5,0},{6,3},{7,2},{8,13},{9,12},{10,... | collective-permute-start | bytes 368648 | tf_op jit(solution)/shard_map/ppermute | solution.py:416
  57.6 11.4 %collective-permute-start.18 = (bf16[160,384]{1,0:T(8,128)(2,1)S(1)}, bf16[160,384]{1,0:T(8,128)(2,1)S(1)}, u32[]{:S(2)}, u32[]{:S(2)}) collective-permute-start(bf16[160,384]{1,0:T(8,128)(2,1)S(1)} %get-tuple-element.70), channel_id=1, source_target_pairs={{0,6},{1,7},{2,4},{3,5},{4,2},{5,3},{6,0},{7,1},{8,14},{9,15},{10,... | collective-permute-start | bytes 368648 | tf_op jit(solution)/shard_map/ppermute | solution.py:416
  59.6 10.9 %collective-permute-start.19 = (bf16[160,384]{1,0:T(8,128)(2,1)S(1)}, bf16[160,384]{1,0:T(8,128)(2,1)S(1)}, u32[]{:S(2)}, u32[]{:S(2)}) collective-permute-start(bf16[160,384]{1,0:T(8,128)(2,1)S(1)} %get-tuple-element.71), channel_id=1, source_target_pairs={{0,7},{1,6},{2,5},{3,4},{4,3},{5,2},{6,1},{7,0},{8,15},{9,14},{10,... | collective-permute-start | bytes 368648 | tf_op jit(solution)/shard_map/ppermute | solution.py:416
  61.1 13.3 %collective-permute-start.29 = (bf16[80,384]{1,0:T(8,128)(2,1)S(1)}, bf16[80,384]{1,0:T(8,128)(2,1)S(1)}, u32[]{:S(2)}, u32[]{:S(2)}) collective-permute-start(bf16[80,384]{1,0:T(8,128)(2,1)S(1)} %get-tuple-element.84), channel_id=1, source_target_pairs={{0,3},{1,2},{2,1},{3,0},{4,7},{5,6},{6,5},{7,4},{8,11},{9,10},{10,... | collective-permute-start | bytes 184328 | tf_op jit(solution)/shard_map/ppermute | solution.py:416
  61.8 12.6 %collective-permute-start.23 = (bf16[80,384]{1,0:T(8,128)(2,1)S(1)}, bf16[80,384]{1,0:T(8,128)(2,1)S(1)}, u32[]{:S(2)}, u32[]{:S(2)}) collective-permute-start(bf16[80,384]{1,0:T(8,128)(2,1)S(1)} %get-tuple-element.77), channel_id=1, source_target_pairs={{0,4},{1,5},{2,6},{3,7},{4,0},{5,1},{6,2},{7,3},{8,12},{9,13},{10,... | collective-permute-start | bytes 184328 | tf_op jit(solution)/shard_map/ppermute | solution.py:416
  68.5 5.9 %collective-permute-start.24 = (bf16[80,384]{1,0:T(8,128)(2,1)S(1)}, bf16[80,384]{1,0:T(8,128)(2,1)S(1)}, u32[]{:S(2)}, u32[]{:S(2)}) collective-permute-start(bf16[80,384]{1,0:T(8,128)(2,1)S(1)} %get-tuple-element.78), channel_id=1, source_target_pairs={{0,5},{1,4},{2,7},{3,6},{4,1},{5,0},{6,3},{7,2},{8,13},{9,12},{10,... | collective-permute-start | bytes 184328 | tf_op jit(solution)/shard_map/ppermute | solution.py:416
  69.0 5.6 %collective-permute-start.25 = (bf16[80,384]{1,0:T(8,128)(2,1)S(1)}, bf16[80,384]{1,0:T(8,128)(2,1)S(1)}, u32[]{:S(2)}, u32[]{:S(2)}) collective-permute-start(bf16[80,384]{1,0:T(8,128)(2,1)S(1)} %get-tuple-element.79), channel_id=1, source_target_pairs={{0,6},{1,7},{2,4},{3,5},{4,2},{5,3},{6,0},{7,1},{8,14},{9,15},{10,... | collective-permute-start | bytes 184328 | tf_op jit(solution)/shard_map/ppermute | solution.py:416
  70.5 4.6 %collective-permute-start.26 = (bf16[80,384]{1,0:T(8,128)(2,1)S(1)}, bf16[80,384]{1,0:T(8,128)(2,1)S(1)}, u32[]{:S(2)}, u32[]{:S(2)}) collective-permute-start(bf16[80,384]{1,0:T(8,128)(2,1)S(1)} %get-tuple-element.80), channel_id=1, source_target_pairs={{0,7},{1,6},{2,5},{3,4},{4,3},{5,2},{6,1},{7,0},{8,15},{9,14},{10,... | collective-permute-start | bytes 184328 | tf_op jit(solution)/shard_map/ppermute | solution.py:416
  (11 other events, 74.5 us)
